TPU v7x, 32 devices: a whole 2x2x4 slice. The times are simulated.
32 devices in a mesh: stream: 2 (over x), batch: 16 (over z, y, core).
Axes of the slice: x: 2, y: 2, z: 4, core: 2. Of those that a mesh axis runs over, the one named last changes fastest.
Arguments:
- tokens: bfloat16 [2, 32, 1024, 768], P('stream', 'batch'), may hold values from -6 to 6
- cotangent: bfloat16 [2, 32, 1024, 768], P('stream', 'batch'), may hold values from -6 to 6
- lengths: int32 [32], P('batch'), may hold values from 128 to 1024, as said below
- ln1_gain: bfloat16 [768], P('batch'), may hold values from 0.099609375 to 1.8984375
- w_qkv: bfloat16 [768, 2304], P('batch'), may hold values from -0.21875 to 0.21875
- w_out: bfloat16 [768, 768], P('batch'), may hold values from -0.875 to 0.875
- ln2_gain: bfloat16 [768], P('batch'), may hold values from 0.099609375 to 1.8984375
- w_up: bfloat16 [768, 3072], P('batch'), may hold values from -0.21875 to 0.21875
- w_down: bfloat16 [3072, 768], P('batch'), may hold values from -0.109375 to 0.109375
Outputs:
- out: bfloat16 [2, 32, 1024, 768], P('stream', 'batch')
- tokens_grad: float32 [2, 32, 1024, 768], P('stream', 'batch')
- ln1_gain_grad: float32 [768], P(('stream', 'batch'))
- w_qkv_grad: float32 [768, 2304], P(('stream', 'batch'))
- w_out_grad: float32 [768, 768], P(('stream', 'batch'))
- ln2_gain_grad: float32 [768], P(('stream', 'batch'))
- w_up_grad: float32 [768, 3072], P(('stream', 'batch'))
- w_down_grad: float32 [3072, 768], P(('stream', 'batch'))
Inputs may be any that keep to these rules, and one draw needn't show every extreme that they name: `lengths`: each length is a multiple of 16; in every draw some row is 1024 long.
All inputs are finite; a program needn't handle non-finite values.
Results may differ from a plain program's by a relative error of at most 0.014.
Values may be sent and summed in bfloat16 or wider, within the bound.
A program may use at most 512 MiB of HBM per device.

v0:
```python
import math

import jax
import jax.numpy as jnp
from jax import lax
from jax.sharding import PartitionSpec as P

HD = 64
BLOCK = 16
MICRO = 2


def from_behind(x, axis, by):
    peers = lax.axis_size(axis)
    pairs = [(i, i + by) for i in range(peers) if 0 <= i + by < peers]
    return lax.ppermute(x, axis, pairs)


def rotary_tables(length, width):
    half_width = width // 2
    places = jnp.arange(length).astype(jnp.float32)
    rates = jnp.exp(jnp.arange(half_width).astype(jnp.float32) * (-2.0 * math.log(10000.0) / width))
    angles = places[:, None] * rates[None, :]
    return (jnp.cos(angles)[:, None, :], jnp.sin(angles)[:, None, :])


def rotate(field, cosine, sine):
    half_width = field.shape[-1] // 2
    first_half = field[..., :half_width]
    second_half = field[..., half_width:]
    return jnp.concatenate(
        [first_half * cosine - second_half * sine, second_half * cosine + first_half * sine],
        axis=-1,
    )


def layer_norm(values, gain_vec):
    center = values - jnp.mean(values, axis=-1, keepdims=True)
    spread = jnp.mean(center * center, axis=-1, keepdims=True)
    return center * lax.rsqrt(spread + 1e-05) * gain_vec


def gelu_tanh(values):
    return jax.nn.gelu(values, approximate=True)


def turned(flat_rows, cosine, sine, row_count):
    shaped = flat_rows.reshape(row_count, cosine.shape[0], -1, HD)
    return rotate(shaped, cosine, sine).reshape(flat_rows.shape)


def main_mask(side_index, length_row, start_row, count_rows, span_keys):
    query_pos = start_row + jnp.arange(count_rows)
    key_pos = jnp.arange(span_keys)
    query_blk = (query_pos // BLOCK)[:, None]
    key_blk = (key_pos // BLOCK)[None, :]
    live_key = (key_pos < length_row)[None, :]
    clean_side = side_index == 0
    return live_key & ((key_blk < query_blk) | clean_side & (key_blk == query_blk))


def diag_mask(side_index, length_row, start_row, count_rows):
    key_pos = start_row + jnp.arange(count_rows)
    live_key = (key_pos < length_row).reshape(count_rows // BLOCK, 1, BLOCK)
    seen = live_key & (side_index == 1)
    return jnp.broadcast_to(seen, (count_rows // BLOCK, BLOCK, BLOCK)).reshape(count_rows, BLOCK)


def pair_scores(query3, key3, diag_key3, allowed, diag_allowed):
    rows_q = query3.shape[0]
    raw_main = jnp.einsum("qhd,khd->hqk", query3, key3, preferred_element_type=jnp.float32)
    main_scores = jnp.where(allowed[None], raw_main * 0.125, -1e30)
    query_diag = query3.reshape(rows_q // BLOCK, BLOCK, -1, HD)
    key_diag = diag_key3.reshape(rows_q // BLOCK, BLOCK, -1, HD)
    raw_diag = jnp.einsum(
        "nqhd,nkhd->hnqk", query_diag, key_diag, preferred_element_type=jnp.float32
    )
    raw_diag = raw_diag.reshape(raw_diag.shape[0], rows_q, BLOCK)
    diag_scores = jnp.where(diag_allowed[None], raw_diag * 0.125, -1e30)
    return (main_scores, diag_scores)


def group_forward(
    query_grp, key_grp, value_grp, diag_key_grp, diag_value_grp, allowed, diag_allowed
):
    rows_q = query_grp.shape[0]
    query3 = query_grp.reshape(rows_q, -1, HD)
    key3 = key_grp.reshape(key_grp.shape[0], -1, HD)
    value3 = value_grp.reshape(value_grp.shape[0], -1, HD)
    diag_key3 = diag_key_grp.reshape(rows_q, -1, HD)
    diag_value3 = diag_value_grp.reshape(rows_q // BLOCK, BLOCK, -1, HD)
    main_scores, diag_scores = pair_scores(query3, key3, diag_key3, allowed, diag_allowed)
    top_score = jnp.maximum(
        jnp.max(main_scores, axis=2, keepdims=True), jnp.max(diag_scores, axis=2, keepdims=True)
    )
    main_exp = jnp.exp(main_scores - top_score)
    diag_exp = jnp.exp(diag_scores - top_score)
    totals = jnp.sum(main_exp, axis=2, keepdims=True) + jnp.sum(diag_exp, axis=2, keepdims=True)
    main_low = (main_exp / totals).astype(jnp.bfloat16)
    diag_low = (diag_exp / totals).astype(jnp.bfloat16)
    heads_grp = diag_low.shape[0]
    diag_low = diag_low.reshape(heads_grp, rows_q // BLOCK, BLOCK, BLOCK)
    mixed3 = jnp.einsum("hqk,khd->qhd", main_low, value3, preferred_element_type=jnp.float32)
    mixed_diag = jnp.einsum(
        "hnqk,nkhd->nqhd", diag_low, diag_value3, preferred_element_type=jnp.float32
    )
    mixed3 = mixed3 + mixed_diag.reshape(rows_q, heads_grp, HD)
    return (mixed3.reshape(rows_q, -1), (top_score + jnp.log(totals))[:, :, 0])


def group_backward(
    query_grp,
    key_grp,
    value_grp,
    diag_key_grp,
    diag_value_grp,
    allowed,
    diag_allowed,
    log_grp,
    grad_grp,
):
    rows_q = query_grp.shape[0]
    count_keys = key_grp.shape[0]
    blocks_q = rows_q // BLOCK
    query3 = query_grp.reshape(rows_q, -1, HD)
    key3 = key_grp.reshape(count_keys, -1, HD)
    value3 = value_grp.reshape(count_keys, -1, HD)
    diag_key3 = diag_key_grp.reshape(rows_q, -1, HD)
    grad3 = grad_grp.reshape(rows_q, -1, HD)
    heads_grp = grad3.shape[1]
    main_scores, diag_scores = pair_scores(query3, key3, diag_key3, allowed, diag_allowed)
    main_probs = jnp.exp(main_scores - log_grp[:, :, None])
    diag_probs = jnp.exp(diag_scores - log_grp[:, :, None])
    main_low = main_probs.astype(jnp.bfloat16)
    diag_low = diag_probs.astype(jnp.bfloat16).reshape(heads_grp, blocks_q, BLOCK, BLOCK)
    grad_blocks = grad3.reshape(blocks_q, BLOCK, heads_grp, HD)
    query_blocks = query3.reshape(blocks_q, BLOCK, heads_grp, HD)
    key_blocks = diag_key3.reshape(blocks_q, BLOCK, heads_grp, HD)
    value_blocks = diag_value_grp.reshape(blocks_q, BLOCK, heads_grp, HD)
    main_gp = jnp.einsum("qhd,khd->hqk", grad3, value3, preferred_element_type=jnp.float32)
    diag_gp = jnp.einsum(
        "nqhd,nkhd->hnqk", grad_blocks, value_blocks, preferred_element_type=jnp.float32
    )
    diag_gp = diag_gp.reshape(heads_grp, rows_q, BLOCK)
    row_sum = jnp.sum(main_probs * main_gp, axis=2, keepdims=True) + jnp.sum(
        diag_probs * diag_gp, axis=2, keepdims=True
    )
    main_raw = (main_probs * (main_gp - row_sum) * 0.125).astype(jnp.bfloat16)
    diag_raw = (diag_probs * (diag_gp - row_sum) * 0.125).astype(jnp.bfloat16)
    diag_raw = diag_raw.reshape(heads_grp, blocks_q, BLOCK, BLOCK)
    grad_query = jnp.einsum("hqk,khd->qhd", main_raw, key3, preferred_element_type=jnp.float32)
    grad_query = grad_query + jnp.einsum(
        "hnqk,nkhd->nqhd", diag_raw, key_blocks, preferred_element_type=jnp.float32
    ).reshape(rows_q, heads_grp, HD)
    grad_key = jnp.einsum("hqk,qhd->khd", main_raw, query3, preferred_element_type=jnp.float32)
    grad_value = jnp.einsum("hqk,qhd->khd", main_low, grad3, preferred_element_type=jnp.float32)
    diag_key_grad = jnp.einsum(
        "hnqk,nqhd->nkhd", diag_raw, query_blocks, preferred_element_type=jnp.float32
    )
    diag_value_grad = jnp.einsum(
        "hnqk,nqhd->nkhd", diag_low, grad_blocks, preferred_element_type=jnp.float32
    )
    return (
        grad_query.reshape(rows_q, -1),
        grad_key.reshape(count_keys, -1),
        grad_value.reshape(count_keys, -1),
        diag_key_grad.reshape(rows_q, -1),
        diag_value_grad.reshape(rows_q, -1),
    )


def attend_row(query_row, keys_row, values_row, far_keys, far_values, side_index, length_row):
    length, width = query_row.shape
    block_rows = min(512, length)
    noisy_side = side_index == 1
    main_keys = jnp.where(noisy_side, far_keys, keys_row)
    main_values = jnp.where(noisy_side, far_values, values_row)
    mixed_parts = []
    log_parts = []
    for block_number in range(length // block_rows):
        start_row = block_number * block_rows
        span_keys = start_row + block_rows
        allowed = main_mask(side_index, length_row, start_row, block_rows, span_keys)
        diag_allowed = diag_mask(side_index, length_row, start_row, block_rows)
        mixed_blk, log_blk = group_forward(
            query_row[start_row:span_keys],
            main_keys[:span_keys],
            main_values[:span_keys],
            keys_row[start_row:span_keys],
            values_row[start_row:span_keys],
            allowed,
            diag_allowed,
        )
        mixed_parts.append(mixed_blk)
        log_parts.append(log_blk)
    return (jnp.concatenate(mixed_parts, axis=0), jnp.concatenate(log_parts, axis=1))


def attend_back(
    query_row,
    keys_row,
    values_row,
    far_keys,
    far_values,
    side_index,
    length_row,
    log_sums,
    grad_row,
):
    length, width = query_row.shape
    block_rows = min(512, length)
    noisy_side = side_index == 1
    main_keys = jnp.where(noisy_side, far_keys, keys_row)
    main_values = jnp.where(noisy_side, far_values, values_row)
    query_parts = []
    main_keys_grad = jnp.zeros((length, width), jnp.float32)
    main_values_grad = jnp.zeros((length, width), jnp.float32)
    diag_key_parts = []
    diag_value_parts = []
    for block_number in range(length // block_rows):
        start_row = block_number * block_rows
        span_keys = start_row + block_rows
        allowed = main_mask(side_index, length_row, start_row, block_rows, span_keys)
        diag_allowed = diag_mask(side_index, length_row, start_row, block_rows)
        query_blk, key_blk, value_blk, diag_key_blk, diag_value_blk = group_backward(
            query_row[start_row:span_keys],
            main_keys[:span_keys],
            main_values[:span_keys],
            keys_row[start_row:span_keys],
            values_row[start_row:span_keys],
            allowed,
            diag_allowed,
            log_sums[:, start_row:span_keys],
            grad_row[start_row:span_keys],
        )
        query_parts.append(query_blk)
        main_keys_grad = main_keys_grad.at[:span_keys].add(key_blk)
        main_values_grad = main_values_grad.at[:span_keys].add(value_blk)
        diag_key_parts.append(diag_key_blk)
        diag_value_parts.append(diag_value_blk)
    diag_keys_grad = jnp.concatenate(diag_key_parts, axis=0)
    diag_values_grad = jnp.concatenate(diag_value_parts, axis=0)
    own_keys_grad = jnp.where(noisy_side, 0.0, main_keys_grad) + diag_keys_grad
    own_values_grad = jnp.where(noisy_side, 0.0, main_values_grad) + diag_values_grad
    far_keys_grad = jnp.where(noisy_side, main_keys_grad, 0.0)
    far_values_grad = jnp.where(noisy_side, main_values_grad, 0.0)
    return (
        jnp.concatenate(query_parts, axis=0),
        own_keys_grad,
        own_values_grad,
        far_keys_grad,
        far_values_grad,
    )


def shards(tokens, cotangent, lengths, ln1_gain, w_qkv, w_out, ln2_gain, w_up, w_down):
    side_index = lax.axis_index("stream")
    rows_dev = tokens.shape[1]
    per_micro = rows_dev // MICRO
    length = tokens.shape[2]
    width = tokens.shape[3]
    cosine, sine = rotary_tables(length, HD)
    outputs = []
    input_grads = []
    grad_total = None
    for micro_step in range(MICRO):
        gathered = (
            lax.all_gather(ln1_gain, "batch", axis=0, tiled=True),
            lax.all_gather(w_qkv, "batch", axis=0, tiled=True),
            lax.all_gather(w_out, "batch", axis=0, tiled=True),
            lax.all_gather(ln2_gain, "batch", axis=0, tiled=True),
            lax.all_gather(w_up, "batch", axis=0, tiled=True),
            lax.all_gather(w_down, "batch", axis=0, tiled=True),
        )
        gain_one = gathered[0].astype(jnp.float32)
        query_key_value_weight = gathered[1]
        output_weight = gathered[2]
        gain_two = gathered[3].astype(jnp.float32)
        up_weight = gathered[4]
        down_weight = gathered[5]
        first_row = micro_step * per_micro
        inputs = tokens[0, first_row : first_row + per_micro].astype(jnp.float32).reshape(-1, width)
        row_lengths = lengths[first_row : first_row + per_micro]
        first_hidden = layer_norm(inputs, gain_one).astype(jnp.bfloat16)
        query_key_value_rows = jnp.dot(
            first_hidden, query_key_value_weight, preferred_element_type=jnp.float32
        )
        query_all = turned(query_key_value_rows[:, :width], cosine, sine, per_micro).astype(
            jnp.bfloat16
        )
        key_value = jnp.concatenate(
            [
                turned(query_key_value_rows[:, width : 2 * width], cosine, sine, per_micro),
                query_key_value_rows[:, 2 * width :],
            ],
            axis=1,
        ).astype(jnp.bfloat16)
        own_pair = key_value.reshape(per_micro, length, 2 * width)
        far_pair = from_behind(own_pair, "stream", 1)
        query_all = query_all.reshape(per_micro, length, width)
        row_number = 0
        mixed_row, log_row = attend_row(
            query_all[row_number],
            own_pair[row_number, :, :width],
            own_pair[row_number, :, width:],
            far_pair[row_number, :, :width],
            far_pair[row_number, :, width:],
            side_index,
            row_lengths[row_number],
        )
        log_rows = [log_row]
        mixed_low = mixed_row.astype(jnp.bfloat16)
        residual_middle = inputs + jnp.dot(
            mixed_low, output_weight, preferred_element_type=jnp.float32
        )
        second_hidden = layer_norm(residual_middle, gain_two).astype(jnp.bfloat16)
        upper_projection = jnp.dot(second_hidden, up_weight, preferred_element_type=jnp.float32)
        active_low = gelu_tanh(upper_projection).astype(jnp.bfloat16)
        result_rows = residual_middle + jnp.dot(
            active_low, down_weight, preferred_element_type=jnp.float32
        )
        outputs.append(result_rows.astype(jnp.bfloat16).reshape(per_micro, length, width))
        grad_rows = (
            cotangent[0, first_row : first_row + per_micro].astype(jnp.float32).reshape(-1, width)
        )
        grad_low = grad_rows.astype(jnp.bfloat16)
        down_grad = jnp.einsum(
            "tf,td->fd", active_low, grad_low, preferred_element_type=jnp.float32
        )
        active_grad = jnp.einsum(
            "td,fd->tf", grad_low, down_weight, preferred_element_type=jnp.float32
        ).astype(jnp.bfloat16)
        unused_gelu, gelu_back = jax.vjp(gelu_tanh, upper_projection)
        upper_grad = gelu_back(active_grad.astype(jnp.float32))[0].astype(jnp.bfloat16)
        up_grad = jnp.einsum(
            "td,tf->df", second_hidden, upper_grad, preferred_element_type=jnp.float32
        )
        hidden_two_grad = jnp.einsum(
            "tf,df->td", upper_grad, up_weight, preferred_element_type=jnp.float32
        )
        unused_norm, norm_two_back = jax.vjp(layer_norm, residual_middle, gain_two)
        middle_norm_grad, gain_two_grad = norm_two_back(hidden_two_grad)
        middle_grad = grad_rows + middle_norm_grad
        branch_low = middle_grad.astype(jnp.bfloat16)
        out_grad = jnp.einsum(
            "te,td->ed", mixed_low, branch_low, preferred_element_type=jnp.float32
        )
        mixed_grad = jnp.einsum(
            "td,ed->te", branch_low, output_weight, preferred_element_type=jnp.float32
        )
        mixed_grad = mixed_grad.astype(jnp.bfloat16).reshape(per_micro, length, width)
        row_number = 0
        query_grad, own_key_grad, own_value_grad, far_key_grad, far_value_grad = attend_back(
            query_all[row_number],
            own_pair[row_number, :, :width],
            own_pair[row_number, :, width:],
            far_pair[row_number, :, :width],
            far_pair[row_number, :, width:],
            side_index,
            row_lengths[row_number],
            log_rows[row_number],
            mixed_grad[row_number],
        )
        own_grads = [jnp.concatenate([own_key_grad, own_value_grad], axis=1)]
        far_grads = [jnp.concatenate([far_key_grad, far_value_grad], axis=1)]
        back_pair = from_behind(jnp.stack(far_grads).astype(jnp.bfloat16), "stream", -1).astype(
            jnp.float32
        )
        pair_grad = (jnp.stack(own_grads) + back_pair).reshape(-1, 2 * width)
        qkv_grad = jnp.concatenate(
            [
                turned(query_grad, cosine, -sine, per_micro),
                turned(pair_grad[:, :width], cosine, -sine, per_micro),
                pair_grad[:, width:],
            ],
            axis=1,
        ).astype(jnp.bfloat16)
        qkv_weight_grad = jnp.einsum(
            "td,te->de", first_hidden, qkv_grad, preferred_element_type=jnp.float32
        )
        hidden_one_grad = jnp.einsum(
            "te,de->td", qkv_grad, query_key_value_weight, preferred_element_type=jnp.float32
        )
        unused_first, norm_one_back = jax.vjp(layer_norm, inputs, gain_one)
        input_norm_grad, gain_one_grad = norm_one_back(hidden_one_grad)
        input_grads.append((middle_grad + input_norm_grad).reshape(per_micro, length, width))
        grads = (gain_one_grad, qkv_weight_grad, out_grad, gain_two_grad, up_grad, down_grad)
        grads = (
            lax.psum_scatter(grads[0], ("stream", "batch"), scatter_dimension=0, tiled=True),
            lax.psum_scatter(grads[1], ("stream", "batch"), scatter_dimension=0, tiled=True),
            lax.psum_scatter(grads[2], ("stream", "batch"), scatter_dimension=0, tiled=True),
            lax.psum_scatter(grads[3], ("stream", "batch"), scatter_dimension=0, tiled=True),
            lax.psum_scatter(grads[4], ("stream", "batch"), scatter_dimension=0, tiled=True),
            lax.psum_scatter(grads[5], ("stream", "batch"), scatter_dimension=0, tiled=True),
        )
        grad_total = grads if grad_total is None else jax.tree.map(jnp.add, grad_total, grads)
    return (
        jnp.concatenate(outputs, axis=0)[None],
        jnp.concatenate(input_grads, axis=0)[None],
        grad_total[0],
        grad_total[1],
        grad_total[2],
        grad_total[3],
        grad_total[4],
        grad_total[5],
    )


def solution(mesh):
    placed = (
        P("stream", "batch", None, None),
        P("stream", "batch", None, None),
        P("batch"),
        P("batch"),
        P("batch", None),
        P("batch", None),
        P("batch"),
        P("batch", None),
        P("batch", None),
    )
    return jax.shard_map(
        shards,
        mesh=mesh,
        in_specs=placed,
        out_specs=(
            P("stream", "batch", None, None),
            P("stream", "batch", None, None),
            P(("stream", "batch")),
            P(("stream", "batch"), None),
            P(("stream", "batch"), None),
            P(("stream", "batch")),
            P(("stream", "batch"), None),
            P(("stream", "batch"), None),
        ),
        check_vma=False,
    )
```

profile of v0, /device:TPU:0, one launch (start us, length us, event | category | flops | bytes accessed | tf_op | source)
XLA Modules:
  0.0 1288.6 jit_solution(1125776141426684215)
XLA Ops:
  22.9 35.6 %all-reduce.9 = (bf16[768]{0:T(1024)(128)(2,1)S(1)}, bf16[768]{0:T(1024)(128)(2,1)S(1)}) all-reduce(bf16[768]{0:T(1024)(128)(2,1)S(1)} %dynamic-update-slice.20, bf16[768]{0:T(1024)(128)(2,1)S(1)} %dynamic-update-slice.21), channel_id=1, replica_groups=mesh['stream'=2,'batch'=16] {'batch'}, use_global_device_ids=true, to_apply=%add.4 | all-reduce | flops 1536 | bytes 6144
  220.8 47.8 %collective-permute-done = bf16[1,1024,1536]{2,1,0:T(8,128)(2,1)} collective-permute-done((bf16[1,1024,1536]{2,1,0:T(8,128)(2,1)}, bf16[1,1024,1536]{2,1,0:T(8,128)(2,1)}, u32[]{:S(2)}, u32[]{:S(2)}) %collective-permute-start) | collective-permute-done | bytes 3145760 | tf_op jit(solution)/shard_map/ppermute | solution.py:16
  361.8 14.4 %fusion.36 = (f32[12,512]{1,0:T(8,128)S(1)}, f32[12,512,1024]{2,1,0:T(8,128)}) fusion(pred[512,1024]{1,0:T(8,128)(4,1)} %get-tuple-element.263, bf16[1024,12,64]{0,2,1:T(8,128)(2,1)} %bitcast.375, bf16[1,512,12,64]{1,3,2,0:T(8,128)(2,1)} %copy-done.29), kind=kOutput, calls=%fused_computation.68 | convolution fusion | flops 824174592 | bytes 28073984 | tf_op jit(solution)/shard_map/qhd,khd->hqk/dot_general | solution.py:71
  382.9 11.9 fusion
  414.1 12.9 %fusion.111 = bf16[512,12,64]{0,2,1:T(8,128)(2,1)} fusion(f32[512,12,64]{0,2,1:T(8,128)S(1)} %copy-done.132, bf16[1024,12,64]{0,2,1:T(8,128)(2,1)S(1)} %bitcast.408, f32[12,512]{1,0:T(8,128)S(1)} %copy-done.175, f32[12,512]{1,0:T(8,128)S(1)} %max.62, f32[12,512,1024]{2,1,0:T(8,128)} %get-tuple-element.289, pred[512,1024]{1,0:T(8,128)(4,1)S(1)} %copy-done.54), kind=kOutput, calls=%fused_computation.264 | convolution fusion | flops 837550080 | bytes 29671424 | tf_op jit(solution)/shard_map/hqk,khd->qhd/dot_general | solution.py:103
  433.3 10.7 fusion.37
  449.4 12.1 fusion.1
  478.7 12.4 fusion.107
  517.2 17.2 %fusion.6 = bf16[1024,3072]{1,0:T(8,128)(2,1)} fusion(f32[1024,3072]{1,0:T(8,128)} %copy-done.69, bf16[3072,768]{1,0:T(8,128)(2,1)} %all-gather.11.cloned.1.call-done, bf16[1,2,1024,768]{3,2,1,0:T(8,128)(2,1)} %param.34), kind=kOutput, calls=%fused_computation.26 | convolution fusion | flops 4901044224 | bytes 25165824 | tf_op jit(solution)/shard_map/td,fd->tf/dot_general | solution.py:330
  534.4 11.3 fusion.244
  545.7 15.2 %fusion.11 = bf16[1024,3072]{1,0:T(8,128)(2,1)} fusion(f32[1024,3072]{1,0:T(8,128)} %fusion.244, bf16[3072,768]{1,0:T(8,128)(2,1)S(1)} %copy-done.185, bf16[1,2,1024,768]{3,2,1,0:T(8,128)(2,1)S(1)} %copy-done.111), kind=kOutput, calls=%fused_computation.31 | convolution fusion | flops 4901044224 | bytes 25165824 | tf_op jit(solution)/shard_map/td,fd->tf/dot_general | solution.py:330
  626.2 13.1 %fusion.26 = f32[12,64,1024]{2,1,0:T(8,128)} fusion(bf16[512,12,64]{0,2,1:T(8,128)(2,1)S(1)} %bitcast.403, f32[12,512]{1,0:T(8,128)S(1)} %copy-done.148, f32[12,512,1024]{2,1,0:T(8,128)} %get-tuple-element.289, pred[512,1024]{1,0:T(8,128)(4,1)S(1)} %copy-done.55), kind=kOutput, calls=%fused_computation.45 | convolution fusion | flops 830472192 | bytes 29646848 | tf_op jit(solution)/shard_map/hqk,qhd->khd/dot_general | solution.py:156
  639.3 20.9 %multiply_reduce_fusion.1 = (f32[12,512]{1,0:T(8,128)}, f32[12,512,1024]{2,1,0:T(8,128)}) fusion(f32[12,512]{1,0:T(8,128)S(1)} %copy-done.148, f32[12,512,1024]{2,1,0:T(8,128)} %get-tuple-element.289, pred[512,1024]{1,0:T(8,128)(4,1)S(1)} %copy-done.55, bf16[512,12,64]{0,2,1:T(8,128)(2,1)S(1)} %bitcast.404, bf16[1024,12,64]{0,2,1:T(8,128)(2,1)} %bitcast.407), kind=kOutput, calls=%fused_computation.4 | convolution fusion | flops 836757504 | bytes 53264384 | tf_op jit(solution)/shard_map/qhd,khd->hqk/dot_general | solution.py:140
  737.1 14.0 %convolution_add_fusion.1 = f32[3072,768]{1,0:T(8,128)} fusion(f32[3072,768]{1,0:T(8,128)} %fusion.99, bf16[1,2,1024,768]{3,2,1,0:T(8,128)(2,1)S(1)} %copy-done.112, f32[1024,3072]{1,0:T(8,128)} %fusion.244), kind=kOutput, calls=%fused_computation.84 | convolution fusion | flops 4862509056 | bytes 33030144 | tf_op jit(solution)/shard_map/tf,td->fd/dot_general | solution.py:327
  762.8 13.8 %fusion.24 = f32[12,64,1024]{2,1,0:T(8,128)} fusion(bf16[512,12,64]{0,2,1:T(8,128)(2,1)S(1)} %bitcast.402, f32[12,512]{1,0:T(8,128)S(1)} %copy-done.146, f32[12,512,1024]{2,1,0:T(8,128)} %get-tuple-element.279, pred[512,1024]{1,0:T(8,128)(4,1)S(1)} %copy-done.52), kind=kOutput, calls=%fused_computation.44 | convolution fusion | flops 830472192 | bytes 29646848 | tf_op jit(solution)/shard_map/hqk,qhd->khd/dot_general | solution.py:156
  860.5 18.0 %multiply_convert_fusion.1 = bf16[12,512,1024]{2,1,0:T(8,128)(2,1)S(1)} fusion(f32[12,512,1024]{2,1,0:T(8,128)} %get-tuple-element.300, f32[12,512]{1,0:T(8,128)S(1)} %copy-done.153, f32[12,512]{1,0:T(8,128)S(1)} %copy-done.149, f32[12,512,1024]{2,1,0:T(8,128)} %get-tuple-element.289, pred[512,1024]{1,0:T(8,128)(4,1)} %get-tuple-element.263), kind=kLoop, calls=%fused_computation.3 | loop fusion | flops 44040192 | bytes 63488000 | tf_op jit(solution)/shard_map/convert_element_type | solution.py:148
  910.6 19.3 %multiply_reduce_fusion = (f32[12,512]{1,0:T(8,128)}, f32[12,512,1024]{2,1,0:T(8,128)}) fusion(f32[12,512]{1,0:T(8,128)} %get-tuple-element.185, f32[12,512,1024]{2,1,0:T(8,128)} %get-tuple-element.279, pred[512,1024]{1,0:T(8,128)(4,1)} %get-tuple-element.264, bf16[512,12,64]{0,2,1:T(8,128)(2,1)} %bitcast.401, bf16[1024,12,64]{0,2,1:T(8,128)(2,1)} %bitcast.405), kind=kOutput, calls=%fused_computation.1 | convolution fusion | flops 836757504 | bytes 53264384 | tf_op jit(solution)/shard_map/qhd,khd->hqk/dot_general | solution.py:140
  962.0 10.6 convolution_add_fusion.2
  973.6 18.7 %multiply_convert_fusion = bf16[12,512,1024]{2,1,0:T(8,128)(2,1)S(1)} fusion(f32[12,512,1024]{2,1,0:T(8,128)} %get-tuple-element.308, f32[12,512]{1,0:T(8,128)S(1)} %copy-done.152, f32[12,512]{1,0:T(8,128)S(1)} %copy-done.147, f32[12,512,1024]{2,1,0:T(8,128)} %get-tuple-element.279, pred[512,1024]{1,0:T(8,128)(4,1)S(1)} %copy-done.53), kind=kLoop, calls=%fused_computation | loop fusion | flops 44040192 | bytes 63488000 | tf_op jit(solution)/shard_map/convert_element_type | solution.py:148
  1090.7 29.0 %collective-permute-done.3 = bf16[1,1024,1536]{2,1,0:T(8,128)(2,1)} collective-permute-done((bf16[1,1024,1536]{2,1,0:T(8,128)(2,1)}, bf16[1,1024,1536]{2,1,0:T(8,128)(2,1)}, u32[]{:S(2)}, u32[]{:S(2)}) %collective-permute-start.3) | collective-permute-done | bytes 3145760 | tf_op jit(solution)/shard_map/ppermute | solution.py:16
  1159.0 10.9 fusion.150
  1169.9 10.9 fusion.151
  1203.1 43.4 %all-reduce.8 = (f32[768]{0:T(1024)S(1)}, f32[768]{0:T(1024)S(1)}) all-reduce(f32[768]{0:T(1024)S(1)} %add.557, f32[768]{0:T(1024)S(1)} %add.560), channel_id=8, replica_groups=mesh['stream'=2,'batch'=16] {'stream','batch'}, use_global_device_ids=true, to_apply=%region_41.42.clone | all-reduce | flops 1536 | bytes 12288
  1264.7 16.8 %reduce-scatter.5.cloned.1.call-done = f32[24,2304]{1,0:T(8,128)} async-done(((f32[768,2304]{1,0:T(8,128)}), f32[24,2304]{1,0:T(8,128)}) %reduce-scatter.5.cloned.1.call-update) | async-done | bytes 221200 | tf_op jit(solution)/shard_map/reduce_scatter | solution.py:390
  (737 shorter events, 830.8 us)
Async XLA Ops:
  7.2 74.8 %all-gather.5.cloned.1.call-start = ((), (), s32[]{:S(2)}) async-start(), calls=%async_computation.4 | async-start | bytes 3760128 | tf_op jit(solution)/shard_map/all_gather | solution.py:269
  7.9 419.2 %all-gather.7.cloned.1.call-start = ((), (), s32[]{:S(2)}) async-start(), calls=%async_computation.5 | async-start | bytes 1253376 | tf_op jit(solution)/shard_map/all_gather | solution.py:270
  8.6 486.1 %all-gather.9.cloned.1.call-start = ((), (), s32[]{:S(2)}) async-start(), calls=%async_computation.6 | async-start | bytes 5013504 | tf_op jit(solution)/shard_map/all_gather | solution.py:272
  9.4 507.8 %all-gather.11.cloned.1.call-start = ((), (), s32[]{:S(2)}) async-start(), calls=%async_computation.7 | async-start | bytes 5013504 | tf_op jit(solution)/shard_map/all_gather | solution.py:273
  10.0 1254.7 %reduce-scatter.7.cloned.1.call-start = ((), (), s32[]{:S(2)}) async-start(), calls=%async_computation.9 | async-start | bytes 2433024 | tf_op jit(solution)/shard_map/reduce_scatter | solution.py:391
  58.5 36.9 %copy-start.157 = (f32[768]{0:T(1024)}, f32[768]{0:T(1024)S(1)}, u32[]{:S(2)}) copy-start(f32[768]{0:T(1024)S(1)} %convert_element_type.366) | copy-start | bytes 9220
  63.1 32.3 %copy-start.22 = (bf16[1,1,1024,768]{2,3,1,0:T(8,128)(2,1)}, bf16[1,1,1024,768]{2,3,1,0:T(8,128)(2,1)S(1)}, u32[]{:S(2)}) copy-start(bf16[1,1,1024,768]{2,3,1,0:T(8,128)(2,1)S(1)} %copy.391) | copy-start | bytes 4718596
  77.5 41.8 %copy-start.113 = (f32[1024,32]{0,1:T(8,128)}, f32[1024,32]{0,1:T(8,128)S(1)}, u32[]{:S(2)}) copy-start(f32[1024,32]{0,1:T(8,128)S(1)} %get-tuple-element.267) | copy-start | bytes 393220
  79.4 390.3 %copy-start.87 = (pred[512,512]{0,1:T(8,128)(4,1)}, pred[512,512]{0,1:T(8,128)(4,1)S(1)}, u32[]{:S(2)}) copy-start(pred[512,512]{0,1:T(8,128)(4,1)S(1)} %get-tuple-element.275) | copy-start | bytes 786436
  134.1 72.3 %collective-permute-start.1 = (bf16[1,1024,1536]{2,1,0:T(8,128)(2,1)}, bf16[1,1024,1536]{2,1,0:T(8,128)(2,1)}, u32[]{:S(2)}, u32[]{:S(2)}) collective-permute-start(bf16[1,1024,1536]{2,1,0:T(8,128)(2,1)} %pad_maximum_fusion.3), channel_id=1, source_target_pairs={{0,16},{1,17},{2,18},{3,19},{4,20},{5,21},{6,22},{7,23},{8,24},{9,... | collective-permute-start | bytes 9437192 | tf_op jit(solution)/shard_map/ppermute | solution.py:16
  141.1 127.5 %collective-permute-start = (bf16[1,1024,1536]{2,1,0:T(8,128)(2,1)}, bf16[1,1024,1536]{2,1,0:T(8,128)(2,1)}, u32[]{:S(2)}, u32[]{:S(2)}) collective-permute-start(bf16[1,1024,1536]{2,1,0:T(8,128)(2,1)} %pad_maximum_fusion.2), channel_id=1, source_target_pairs={{0,16},{1,17},{2,18},{3,19},{4,20},{5,21},{6,22},{7,23},{8,24},{9,... | collective-permute-start | bytes 9437192 | tf_op jit(solution)/shard_map/ppermute | solution.py:16
  186.7 212.1 %copy-start.6 = (f32[12,32,16,16]{2,3,1,0:T(8,128)}, f32[12,32,16,16]{2,3,1,0:T(8,128)S(1)}, u32[]{:S(2)}) copy-start(f32[12,32,16,16]{2,3,1,0:T(8,128)S(1)} %get-tuple-element.291) | copy-start | bytes 1179652
  430.4 144.9 %copy-start.138 = (f32[1024]{0:T(1024)}, f32[1024]{0:T(1024)S(1)}, u32[]{:S(2)}) copy-start(f32[1024]{0:T(1024)S(1)} %broadcast_multiply_fusion.2) | copy-start | bytes 12292
  430.8 144.5 %copy-start.142 = (f32[1024]{0:T(1024)}, f32[1024]{0:T(1024)S(1)}, u32[]{:S(2)}) copy-start(f32[1024]{0:T(1024)S(1)} %fusion.205) | copy-start | bytes 12292
  492.7 82.7 %copy-start.140 = (f32[1024]{0:T(1024)}, f32[1024]{0:T(1024)S(1)}, u32[]{:S(2)}) copy-start(f32[1024]{0:T(1024)S(1)} %broadcast_multiply_fusion) | copy-start | bytes 12292
  494.8 80.6 %copy-start.144 = (f32[1024]{0:T(1024)}, f32[1024]{0:T(1024)S(1)}, u32[]{:S(2)}) copy-start(f32[1024]{0:T(1024)S(1)} %fusion.207) | copy-start | bytes 12292
  607.0 58.6 %copy-start.85 = (bf16[512,768]{0,1:T(8,128)(2,1)}, bf16[512,768]{0,1:T(8,128)(2,1)S(1)}, u32[]{:S(2)}) copy-start(bf16[512,768]{0,1:T(8,128)(2,1)S(1)} %get-tuple-element.240) | copy-start | bytes 2359300
  665.5 599.2 %reduce-scatter.11.cloned.1.call-start = ((), (), s32[]{:S(2)}) async-start(), calls=%async_computation.11 | async-start | bytes 9732096 | tf_op jit(solution)/shard_map/reduce_scatter | solution.py:394
  751.1 513.6 %reduce-scatter.9.cloned.1.call-start = ((), (), s32[]{:S(2)}) async-start(), calls=%async_computation.10 | async-start | bytes 9732096 | tf_op jit(solution)/shard_map/reduce_scatter | solution.py:393
  909.2 175.4 %collective-permute-start.2 = (bf16[1,1024,1536]{2,1,0:T(8,128)(2,1)}, bf16[1,1024,1536]{2,1,0:T(8,128)(2,1)}, u32[]{:S(2)}, u32[]{:S(2)}) collective-permute-start(bf16[1,1024,1536]{2,1,0:T(8,128)(2,1)} %pad_maximum_fusion.4), channel_id=1, source_target_pairs={{16,0},{17,1},{18,2},{19,3},{20,4},{21,5},{22,6},{23,7},{24,8},{25... | collective-permute-start | bytes 9437192 | tf_op jit(solution)/shard_map/ppermute | solution.py:16
  972.6 308.9 %reduce-scatter.5.cloned.1.call-start = ((), (), s32[]{:S(2)}) async-start(), calls=%async_computation.8 | async-start | bytes 7299072 | tf_op jit(solution)/shard_map/reduce_scatter | solution.py:390
  1036.8 82.9 %collective-permute-start.3 = (bf16[1,1024,1536]{2,1,0:T(8,128)(2,1)}, bf16[1,1024,1536]{2,1,0:T(8,128)(2,1)}, u32[]{:S(2)}, u32[]{:S(2)}) collective-permute-start(bf16[1,1024,1536]{2,1,0:T(8,128)(2,1)} %pad_maximum_fusion.5), channel_id=1, source_target_pairs={{16,0},{17,1},{18,2},{19,3},{20,4},{21,5},{22,6},{23,7},{24,8},{25... | collective-permute-start | bytes 9437192 | tf_op jit(solution)/shard_map/ppermute | solution.py:16
  1200.0 47.6 %copy-start.170 = (f32[1024]{0:T(1024)S(1)}, f32[1024]{0:T(1024)}, u32[]{:S(2)}) copy-start(f32[1024]{0:T(1024)} %copy-done.169) | copy-start | bytes 12292
  1200.0 47.6 %copy-start.172 = (f32[1024]{0:T(1024)S(1)}, f32[1024]{0:T(1024)}, u32[]{:S(2)}) copy-start(f32[1024]{0:T(1024)} %copy-done.171) | copy-start | bytes 12292
  (191 other events, 1279.9 us)
Sparse Core Ops, SparseCore 0:
  10.3 49.8 all-gather.4
  62.5 37.3 all-gather.6
  102.2 52.3 all-gather.8
  156.7 51.9 all-gather.10
  665.6 98.3 reduce-scatter.6
  771.3 134.6 reduce-scatter.10
  972.7 147.0 reduce-scatter.8
  1159.1 122.3 reduce-scatter.4
where the time goes:
time: 1300 us; the launch traced here: 1290 us
  matrix products  492 us (38%)
  local copies, waits for them, and re-layouts  344 us (26%)
  other arithmetic  245 us (19%)
  waiting for transfers between devices  99.8 us (8%)
  blocking collectives  79 us (6%)
  between operations  17.3 us (1%)
    ppermute x4, waiting for transfers between devices, from_behind(): return lax.ppermute(x, axis, pairs)  80.3 us
    unnamed x2, blocking collectives  79 us
    dot_general x4, matrix products, group_backward(): jnp.einsum('qhd,khd->hqk', grad3, value3, preferred_element_type=jnp.floa...  59.6 us
    unnamed x417, local copies, waits for them, and re-layouts  59 us
    convert_element_type x4, other arithmetic, group_backward(): main_raw = (main_probs * (main_gp - row_sum) * 0.125).astype(jnp.bfloat16)  57.2 us
    dot_general x4, matrix products, group_forward(): jnp.einsum('hqk,khd->qhd', main_low, value3, preferred_element_type=jnp.f...  44.1 us
    dot_general x4, matrix products, group_backward(): jnp.einsum('hqk,qhd->khd', main_low, grad3, preferred_element_type=jnp.fl...  41.8 us
    dot_general x4, matrix products, pair_scores(): jnp.einsum('qhd,khd->hqk', query3, key3, preferred_element_type=jnp.float32)  41.2 us
  transfers between devices with their start and end apart: 12, of which 4 were waited for; matrix products, arithmetic and copies ran while one was open for 70% of the time, Pallas kernels for 0%

commit v1 on v0

v1 whole, which is shorter than its diff:
```python
import functools
import math

import jax
import jax.numpy as jnp
from jax import lax
from jax.experimental import pallas as pl
from jax.experimental.pallas import tpu as pltpu
from jax.sharding import PartitionSpec as P

HD = 64
BLOCK = 16
LANES = 128
TILE = 256
BIG = -1e30
f32, bf16 = jnp.float32, jnp.bfloat16


def mm(a, b):
    return lax.dot_general(a, b, (((1,), (0,)), ((), ())), preferred_element_type=f32)


def mm_t(a, b):
    return lax.dot_general(a, b, (((1,), (1,)), ((), ())), preferred_element_type=f32)


def t_mm(a, b):
    return lax.dot_general(a, b, (((0,), (0,)), ((), ())), preferred_element_type=f32)


def rotary_tables(length):
    half = HD // 2
    places = jnp.arange(length).astype(f32)
    rates = jnp.exp(jnp.arange(half).astype(f32) * (-2.0 * math.log(10000.0) / HD))
    angles = places[:, None] * rates[None, :]
    cosine, sine = jnp.cos(angles), jnp.sin(angles)
    return (
        jnp.concatenate([cosine] * 4, axis=1),
        jnp.concatenate([-sine, sine, -sine, sine], axis=1),
    )


def half_partner(x):
    lane = lax.broadcasted_iota(jnp.int32, x.shape, 1)
    low = lax.rem(lane, HD) < HD // 2
    return jnp.where(low, pltpu.roll(x, LANES - HD // 2, 1), pltpu.roll(x, HD // 2, 1))


def project_kernel(x_ref, gain_ref, w_ref, cos_ref, sin_ref, out_ref):
    x = x_ref[...].astype(f32)
    width = x.shape[1]
    center = x - jnp.mean(x, axis=1, keepdims=True)
    spread = jnp.mean(center * center, axis=1, keepdims=True)
    hidden = (center * lax.rsqrt(spread + 1e-5) * gain_ref[...].astype(f32)).astype(bf16)
    cosine, sine = cos_ref[...], sin_ref[...]
    for part in range(3):
        rows = mm(hidden, w_ref[:, part * width : (part + 1) * width])
        for pair in range(width // LANES):
            cols = slice(pair * LANES, (pair + 1) * LANES)
            field = rows[:, cols]
            if part < 2:
                field = field * cosine + half_partner(field) * sine
            if part == 0:
                field = field * 0.125
            out_ref[part, :, cols] = field.astype(bf16)


def project(x, gain, w, cosine, sine, tile=256):
    tokens, width = x.shape
    length = cosine.shape[0]
    per = length // tile
    return pl.pallas_call(
        project_kernel,
        name="project",
        grid=(tokens // tile,),
        in_specs=[
            pl.BlockSpec((tile, width), lambda i: (i, 0)),
            pl.BlockSpec((1, width), lambda i: (0, 0)),
            pl.BlockSpec((width, 3 * width), lambda i: (0, 0), pipeline_mode=pl.Buffered(1)),
            pl.BlockSpec((tile, LANES), lambda i: (lax.rem(i, per), 0)),
            pl.BlockSpec((tile, LANES), lambda i: (lax.rem(i, per), 0)),
        ],
        out_specs=pl.BlockSpec((3, tile, width), lambda i: (0, i, 0)),
        out_shape=jax.ShapeDtypeStruct((3, tokens, width), bf16),
        compiler_params=pltpu.CompilerParams(vmem_limit_bytes=48 << 20),
        cost_estimate=pl.CostEstimate(
            flops=6 * tokens * width * width, bytes_accessed=tokens * width * 8 + 6 * width * width, transcendentals=0
        ),
    )(x, gain, w, cosine, sine)


def mask_tables(length, row_length):
    pos = jnp.arange(length)
    blk = (pos // BLOCK)[:, None]
    lane = (jnp.arange(LANES) % HD)[None, :]
    dead = (pos >= row_length)[:, None]
    clean_query = (lane == blk).astype(bf16)
    noisy_query = (lane == blk - 1).astype(bf16)
    main_key = jnp.where((blk > lane) | dead, BIG, 0.0).astype(bf16)
    diag_key = jnp.where((blk != lane) | dead, BIG, 0.0).astype(bf16)
    return clean_query, noisy_query, main_key, diag_key


def low_lanes(shape):
    return lax.broadcasted_iota(jnp.int32, shape, 1) < HD


def attend_kernel(side_ref, qkv_ref, cq_ref, nq_ref, mk_ref, dk_ref, out_ref, log_ref,
                  qa, ka, kd, va, s_scr):
    length = out_ref.shape[1]
    clean = side_ref[0]
    noisy = 1 - clean
    tiles = length // TILE
    low = low_lanes((length, LANES))
    ones = jnp.ones((16, length), bf16)
    vc_t = qkv_ref[2, clean].T
    vn_t = qkv_ref[2, noisy].T
    for head in range(2):
        pick = low if head == 0 else jnp.logical_not(low)
        qa[0, head] = jnp.where(pick, qkv_ref[0, clean], cq_ref[...])
        qa[1, head] = jnp.where(pick, qkv_ref[0, noisy], nq_ref[...])
        qa[2, head] = jnp.where(pick, qkv_ref[0, noisy], cq_ref[...])
        ka[head] = jnp.where(pick, qkv_ref[1, clean], mk_ref[...])
        kd[head] = jnp.where(pick, qkv_ref[1, noisy], dk_ref[...])
        va[0, head, :HD] = vc_t[head * HD : (head + 1) * HD]
        va[1, head, :HD] = vn_t[head * HD : (head + 1) * HD]
        va[0, head, HD:] = ones
        va[1, head, HD:] = ones
    for copy in range(2):
        where_to = clean if copy == 0 else noisy
        for tile in range(tiles):
            rows = slice(tile * TILE, (tile + 1) * TILE)
            parts = []
            for head in range(2):
                pieces = [(qa[copy, head, rows, :], ka, 0, t) for t in range(tile + 1)]
                if copy == 1:
                    pieces.append((qa[2, head, rows, :], kd, 1, tile))
                top = None
                for n, (query, keys, vi, t) in enumerate(pieces):
                    s = mm_t(keys[head, t * TILE : (t + 1) * TILE, :], query)
                    if copy == 1 and tile == 0 and n == 0:
                        first = lax.broadcasted_iota(jnp.int32, s.shape, 1) < BLOCK
                        s = jnp.where(first, BIG, s)
                    s_scr[head, n * TILE : (n + 1) * TILE, :] = s
                    m = jnp.max(s, axis=0, keepdims=True)
                    top = m if top is None else jnp.maximum(top, m)
                acc = None
                for n, (query, keys, vi, t) in enumerate(pieces):
                    p = jnp.exp(s_scr[head, n * TILE : (n + 1) * TILE, :] - top).astype(bf16)
                    o = mm(va[vi, head, :, t * TILE : (t + 1) * TILE], p)
                    acc = o if acc is None else acc + o
                total = acc[HD : HD + 1, :]
                parts.append(acc[:HD] / total)
                log_ref[where_to, 0, head : head + 1, rows] = top + jnp.log(total)
            out_ref[where_to, rows, :] = jnp.concatenate(parts, axis=0).T.astype(bf16)


def attend(side, qkv, tables):
    _, copies, length, width = qkv.shape
    pairs = width // LANES
    table_spec = pl.BlockSpec((length, LANES), lambda i, s: (0, 0))
    return pl.pallas_call(
        attend_kernel,
        name="attend",
        grid_spec=pltpu.PrefetchScalarGridSpec(
            num_scalar_prefetch=1,
            grid=(pairs,),
            in_specs=[pl.BlockSpec((3, copies, length, LANES), lambda i, s: (0, 0, 0, i))] + [table_spec] * 4,
            out_specs=[
                pl.BlockSpec((copies, length, LANES), lambda i, s: (0, 0, i)),
                pl.BlockSpec((copies, 1, 2, length), lambda i, s: (0, i, 0, 0)),
            ],
            scratch_shapes=[
                pltpu.VMEM((3, 2, length, LANES), bf16),
                pltpu.VMEM((2, length, LANES), bf16),
                pltpu.VMEM((2, length, LANES), bf16),
                pltpu.VMEM((2, 2, HD + 16, length), bf16),
                pltpu.VMEM((2, length + TILE, TILE), f32),
            ],
        ),
        out_shape=[
            jax.ShapeDtypeStruct((copies, length, width), bf16),
            jax.ShapeDtypeStruct((copies, pairs, 2, length), f32),
        ],
        compiler_params=pltpu.CompilerParams(vmem_limit_bytes=48 << 20),
        cost_estimate=pl.CostEstimate(
            flops=8 * length * length * width, bytes_accessed=16 * length * width, transcendentals=length * length * 12
        ),
    )(side, qkv, *tables)


def split3(x):
    hi = x.astype(bf16)
    rest = x - hi.astype(f32)
    mid = rest.astype(bf16)
    lo = (rest - mid.astype(f32)).astype(bf16)
    return hi, mid, lo


def attend_back_kernel(side_ref, qkv_ref, o_ref, do_ref, log_ref, cq_ref, nq_ref, mk_ref, dk_ref, cos_ref, sin_ref,
                       dqkv_ref, qa, qz, ka, kd, kt, doz, dsum, dq, dkc, dvc):
    length = o_ref.shape[1]
    clean = side_ref[0]
    noisy = 1 - clean
    tiles = length // TILE
    low = low_lanes((length, LANES))
    zero = jnp.zeros((length, LANES), bf16)
    for copy in range(2):
        at = clean if copy == 0 else noisy
        kt[copy] = qkv_ref[1, at].T
        prod = (o_ref[at].astype(f32) * do_ref[at].astype(f32)).T
        dsum[copy, 0:1] = jnp.sum(prod[:HD], axis=0, keepdims=True)
        dsum[copy, 1:2] = jnp.sum(prod[HD:], axis=0, keepdims=True)
        for head in range(2):
            pick = low if head == 0 else jnp.logical_not(low)
            qa[copy, head] = jnp.where(pick, qkv_ref[0, at], (cq_ref, nq_ref)[copy][...])
            qz[copy, head] = jnp.where(pick, qkv_ref[0, at], zero)
            doz[copy, head] = jnp.where(pick, do_ref[at], zero)
            if copy == 0:
                ka[head] = jnp.where(pick, qkv_ref[1, at], mk_ref[...])
            else:
                qa[2, head] = jnp.where(pick, qkv_ref[0, at], cq_ref[...])
                kd[head] = jnp.where(pick, qkv_ref[1, at], dk_ref[...])
    cosine, sine = cos_ref[...], sin_ref[...]

    def piece(copy, tile, query, keys, kv_copy, t, mask_first):
        rows = slice(tile * TILE, (tile + 1) * TILE)
        krows = slice(t * TILE, (t + 1) * TILE)
        kv_at = clean if kv_copy == 0 else noisy
        at = clean if copy == 0 else noisy
        probs, raws = [], []
        for head in range(2):
            s = mm_t(keys[head, krows, :], qa[query, head, rows, :])
            p = jnp.exp(s - log_ref[at, 0, head : head + 1, rows])
            if mask_first:
                first = lax.broadcasted_iota(jnp.int32, s.shape, 1) < BLOCK
                p = jnp.where(first, 0.0, p)
            dp = mm_t(qkv_ref[2, kv_at, krows, :], doz[copy, head, rows, :])
            raw = (p * (dp - dsum[copy, head : head + 1, rows])).astype(bf16)
            p = p.astype(bf16)
            dq[copy, head * HD : (head + 1) * HD, rows] += mm(kt[kv_copy, head * HD : (head + 1) * HD, krows], raw)
            probs.append(p)
            raws.append(raw)
        p2 = jnp.concatenate(probs, axis=1)
        r2 = jnp.concatenate(raws, axis=1)
        do2 = jnp.concatenate([doz[copy, 0, rows, :], doz[copy, 1, rows, :]], axis=0)
        q2 = jnp.concatenate([qz[copy, 0, rows, :], qz[copy, 1, rows, :]], axis=0)
        return mm(p2, do2), mm(r2, q2)

    def finish(field, rotate, scale):
        if rotate:
            c, s = cosine, sine
            field = field * c - half_partner(field) * s
        return (field * scale if scale != 1.0 else field).astype(bf16)

    dq[...] = jnp.zeros_like(dq)
    for t in range(tiles):
        krows = slice(t * TILE, (t + 1) * TILE)
        dv_t, dk_t = piece(1, t, 2, kd, 1, t, False)
        dqkv_ref[2, noisy, krows, :] = dv_t.astype(bf16)
        dkc[krows, :] = dk_t
    dqkv_ref[1, noisy] = finish(dkc[...], True, 1.0)
    for t in range(tiles):
        krows = slice(t * TILE, (t + 1) * TILE)
        dv_acc = dk_acc = None
        for tile in range(t, tiles):
            for copy in range(2):
                dv_t, dk_t = piece(copy, tile, copy, ka, 0, t, copy == 1 and tile == 0)
                dv_acc = dv_t if dv_acc is None else dv_acc + dv_t
                dk_acc = dk_t if dk_acc is None else dk_acc + dk_t
        dqkv_ref[2, clean, krows, :] = dv_acc.astype(bf16)
        dkc[krows, :] = dk_acc
    dqkv_ref[1, clean] = finish(dkc[...], True, 1.0)
    dqkv_ref[0, clean] = finish(dq[0].T, True, 0.125)
    dqkv_ref[0, noisy] = finish(dq[1].T, True, 0.125)


def attend_back(side, qkv, mixed, grad, logs, tables, cosine, sine):
    _, copies, length, width = qkv.shape
    pairs = width // LANES
    table_spec = pl.BlockSpec((length, LANES), lambda i, s: (0, 0), pipeline_mode=pl.Buffered(1))
    row_spec = pl.BlockSpec((copies, length, LANES), lambda i, s: (0, 0, i))
    three = pl.BlockSpec((3, copies, length, LANES), lambda i, s: (0, 0, 0, i))
    return pl.pallas_call(
        attend_back_kernel,
        name="attend_back",
        grid_spec=pltpu.PrefetchScalarGridSpec(
            num_scalar_prefetch=1,
            grid=(pairs,),
            in_specs=[three, row_spec, row_spec, pl.BlockSpec((copies, 1, 2, length), lambda i, s: (0, i, 0, 0))]
            + [table_spec] * 6,
            out_specs=three,
            scratch_shapes=[
                pltpu.VMEM((3, 2, length, LANES), bf16),
                pltpu.VMEM((2, 2, length, LANES), bf16),
                pltpu.VMEM((2, length, LANES), bf16),
                pltpu.VMEM((2, length, LANES), bf16),
                pltpu.VMEM((2, LANES, length), bf16),
                pltpu.VMEM((2, 2, length, LANES), bf16),
                pltpu.VMEM((2, 2, length), f32),
                pltpu.VMEM((2, LANES, length), f32),
                pltpu.VMEM((length, LANES), f32),
                pltpu.VMEM((length, LANES), f32),
            ],
        ),
        out_shape=jax.ShapeDtypeStruct((3, copies, length, width), bf16),
        compiler_params=pltpu.CompilerParams(vmem_limit_bytes=48 << 20),
        cost_estimate=pl.CostEstimate(
            flops=20 * length * length * width, bytes_accessed=30 * length * width, transcendentals=length * length * 12
        ),
    )(side, qkv, mixed, grad, logs, *tables, cosine, sine)


ROOT = math.sqrt(2.0 / math.pi)


def feed_kernel(x_ref, mixed_ref, grad_ref, gain_ref, wo_ref, wu_ref, wd_ref,
                out_ref, act_ref, du_ref, h2_ref, dmid_ref, dbr_ref, dmix_ref, dgain_ref, *, chunk):
    width, ff = wu_ref.shape
    gain = gain_ref[...].astype(f32)
    middle = x_ref[...].astype(f32) + mm(mixed_ref[...], wo_ref[...])
    center = middle - jnp.mean(middle, axis=1, keepdims=True)
    spread = jnp.mean(center * center, axis=1, keepdims=True)
    inv = lax.rsqrt(spread + 1e-5)
    norm = center * inv
    hidden = (norm * gain).astype(bf16)
    h2_ref[...] = hidden
    grad = grad_ref[...]
    out = middle
    dh = jnp.zeros_like(middle)
    for c in range(ff // chunk):
        cols = slice(c * chunk, (c + 1) * chunk)
        u = mm(hidden, wu_ref[:, cols])
        da = mm_t(grad, wd_ref[cols, :]).astype(bf16).astype(f32)
        sq = u * u
        t = jnp.tanh(u * (ROOT + (ROOT * 0.044715) * sq))
        half = 0.5 + 0.5 * t
        act = (u * half).astype(bf16)
        slope = half + (u * (half * (1.0 - t))) * (ROOT + (3 * ROOT * 0.044715) * sq)
        du = (da * slope).astype(bf16)
        act_ref[:, cols] = act
        du_ref[:, cols] = du
        out = out + mm(act, wd_ref[cols, :])
        dh = dh + mm_t(du, wu_ref[:, cols])
    out_ref[...] = out.astype(bf16)

    @pl.when(pl.program_id(0) == 0)
    def _():
        dgain_ref[...] = jnp.zeros_like(dgain_ref)

    dgain_ref[...] += jnp.sum((dh * norm).reshape(-1, 8, width), axis=0)
    e = dh * gain
    dmid = grad.astype(f32) + inv * (
        e - jnp.mean(e, axis=1, keepdims=True) - norm * jnp.mean(e * norm, axis=1, keepdims=True)
    )
    dmid_ref[...] = dmid
    dbr = dmid.astype(bf16)
    dbr_ref[...] = dbr
    dmix_ref[...] = mm_t(dbr, wo_ref[...]).astype(bf16)


def feed(x, mixed, grad, gain, wo, wu, wd, tile=256, chunk=768):
    tokens, width = x.shape
    ff = wu.shape[1]
    row = pl.BlockSpec((tile, width), lambda i: (i, 0))
    wide = pl.BlockSpec((tile, ff), lambda i: (i, 0))
    def keep(shape):
        return pl.BlockSpec(shape, lambda i: (0, 0), pipeline_mode=pl.Buffered(1))
    return pl.pallas_call(
        functools.partial(feed_kernel, chunk=chunk),
        name="feed",
        grid=(tokens // tile,),
        in_specs=[row, row, row, keep((1, width)), keep((width, width)), keep((width, ff)), keep((ff, width))],
        out_specs=[row, wide, wide, row, row, row, row, pl.BlockSpec((8, width), lambda i: (0, 0))],
        out_shape=[
            jax.ShapeDtypeStruct((tokens, width), bf16),
            jax.ShapeDtypeStruct((tokens, ff), bf16),
            jax.ShapeDtypeStruct((tokens, ff), bf16),
            jax.ShapeDtypeStruct((tokens, width), bf16),
            jax.ShapeDtypeStruct((tokens, width), f32),
            jax.ShapeDtypeStruct((tokens, width), bf16),
            jax.ShapeDtypeStruct((tokens, width), bf16),
            jax.ShapeDtypeStruct((8, width), f32),
        ],
        compiler_params=pltpu.CompilerParams(vmem_limit_bytes=60 << 20),
        cost_estimate=pl.CostEstimate(
            flops=tokens * width * (4 * width + 8 * ff), bytes_accessed=tokens * (width * 18 + ff * 4),
            transcendentals=tokens * ff
        ),
    )(x, mixed, grad, gain, wo, wu, wd)


def weight_kernel(left_ref, right_ref, out_ref):
    out_ref[...] = t_mm(left_ref[...], right_ref[...]).astype(bf16)


def weight_grad(left, right, block_l, block_r, name):
    tokens, dl = left.shape
    dr = right.shape[1]
    return pl.pallas_call(
        weight_kernel,
        name=name,
        grid=(dl // block_l, dr // block_r),
        in_specs=[
            pl.BlockSpec((tokens, block_l), lambda i, j: (0, i)),
            pl.BlockSpec((tokens, block_r), lambda i, j: (0, j)),
        ],
        out_specs=pl.BlockSpec((block_l, block_r), lambda i, j: (i, j)),
        out_shape=jax.ShapeDtypeStruct((dl, dr), bf16),
        compiler_params=pltpu.CompilerParams(vmem_limit_bytes=48 << 20),
        cost_estimate=pl.CostEstimate(
            flops=2 * tokens * dl * dr, bytes_accessed=2 * tokens * (dl + dr) + 2 * dl * dr, transcendentals=0
        ),
    )(left, right)


def project_back_kernel(x_ref, gain_ref, w_ref, dqkv_ref, dmid_ref, dx_ref, dgain_ref):
    x = x_ref[...].astype(f32)
    width = x.shape[1]
    center = x - jnp.mean(x, axis=1, keepdims=True)
    spread = jnp.mean(center * center, axis=1, keepdims=True)
    inv = lax.rsqrt(spread + 1e-5)
    norm = center * inv
    dh = mm_t(dqkv_ref[0], w_ref[:, :width])
    dh = dh + mm_t(dqkv_ref[1], w_ref[:, width : 2 * width])
    dh = dh + mm_t(dqkv_ref[2], w_ref[:, 2 * width :])

    @pl.when(pl.program_id(0) == 0)
    def _():
        dgain_ref[...] = jnp.zeros_like(dgain_ref)

    dgain_ref[...] += jnp.sum((dh * norm).reshape(-1, 8, width), axis=0)
    e = dh * gain_ref[...].astype(f32)
    dx_ref[...] = dmid_ref[...] + inv * (
        e - jnp.mean(e, axis=1, keepdims=True) - norm * jnp.mean(e * norm, axis=1, keepdims=True)
    )


def project_back(x, gain, w, dqkv, dmid, tile=256):
    tokens, width = x.shape
    row = pl.BlockSpec((tile, width), lambda i: (i, 0))
    return pl.pallas_call(
        project_back_kernel,
        name="project_back",
        grid=(tokens // tile,),
        in_specs=[
            row,
            pl.BlockSpec((1, width), lambda i: (0, 0)),
            pl.BlockSpec((width, 3 * width), lambda i: (0, 0), pipeline_mode=pl.Buffered(1)),
            pl.BlockSpec((3, tile, width), lambda i: (0, i, 0)),
            row,
        ],
        out_specs=[row, pl.BlockSpec((8, width), lambda i: (0, 0))],
        out_shape=[jax.ShapeDtypeStruct((tokens, width), f32), jax.ShapeDtypeStruct((8, width), f32)],
        compiler_params=pltpu.CompilerParams(vmem_limit_bytes=48 << 20),
        cost_estimate=pl.CostEstimate(
            flops=6 * tokens * width * width, bytes_accessed=tokens * width * 16, transcendentals=0
        ),
    )(x, gain, w, dqkv, dmid)


def norm_kernel(x_ref, gain_ref, out_ref):
    x = x_ref[...].astype(f32)
    center = x - jnp.mean(x, axis=1, keepdims=True)
    spread = jnp.mean(center * center, axis=1, keepdims=True)
    out_ref[...] = (center * lax.rsqrt(spread + 1e-5) * gain_ref[...].astype(f32)).astype(bf16)


def norm_rows(x, gain, tile=512):
    tokens, width = x.shape
    row = pl.BlockSpec((tile, width), lambda i: (i, 0))
    return pl.pallas_call(
        norm_kernel,
        name="norm_rows",
        grid=(tokens // tile,),
        in_specs=[row, pl.BlockSpec((1, width), lambda i: (0, 0))],
        out_specs=row,
        out_shape=jax.ShapeDtypeStruct((tokens, width), bf16),
    )(x, gain)


def shards(tokens, cotangent, lengths, ln1_gain, w_qkv, w_out, ln2_gain, w_up, w_down):
    side = lax.axis_index("stream")
    _, rows_dev, length, width = tokens.shape
    assert rows_dev == 2
    swap = [(0, 1), (1, 0)]

    def pair_up(field):
        own = jnp.take(field[0], side, axis=0)
        away = lax.ppermute(jnp.take(field[0], 1 - side, axis=0), "stream", swap)
        return jnp.concatenate([own, away], axis=0)

    def hand_back(field):
        own, away = field[:length], lax.ppermute(field[length:], "stream", swap)
        first = side == 0
        return jnp.stack([jnp.where(first, own, away), jnp.where(first, away, own)])[None]

    w_qkv_all = lax.all_gather(w_qkv, "batch", axis=0, tiled=True)
    gain_one = lax.all_gather(ln1_gain, "batch", axis=0, tiled=True)[None]
    gain_two = lax.all_gather(ln2_gain, "batch", axis=0, tiled=True)[None]
    w_out_all = lax.all_gather(w_out, "batch", axis=0, tiled=True)
    w_up_all = lax.all_gather(w_up, "batch", axis=0, tiled=True)
    w_down_all = lax.all_gather(w_down, "batch", axis=0, tiled=True)

    x = pair_up(tokens)
    grad = pair_up(cotangent)
    cosine, sine = rotary_tables(length)
    tables = mask_tables(length, jnp.take(lengths, side))
    side_array = side.reshape(1).astype(jnp.int32)

    qkv = project(x, gain_one, w_qkv_all, cosine, sine)
    qkv4 = qkv.reshape(3, 2, length, width)
    mixed, logs = attend(side_array, qkv4, tables)
    mixed2 = mixed.reshape(2 * length, width)
    out, act, du, h2, dmid, dbr, dmix, dgain_two = feed(
        x, mixed2, grad, gain_two, w_out_all, w_up_all, w_down_all, tile=512
    )
    dw_down = weight_grad(act, grad, 768, 768, "grad_down")
    dw_up = weight_grad(h2, du, 768, 768, "grad_up")
    dw_out = weight_grad(mixed2, dbr, 768, 768, "grad_out")
    dqkv = attend_back(side_array, qkv4, mixed, dmix.reshape(2, length, width), logs, tables, cosine, sine)
    hidden = norm_rows(x, gain_one)
    dqkv3 = dqkv.reshape(3, 2 * length, width)
    dw_q = [weight_grad(hidden, dqkv3[i], 768, 768, "grad_qkv") for i in range(3)]
    dx, dgain_one = project_back(x, gain_one, w_qkv_all, dqkv3, dmid)

    both = ("stream", "batch")
    peers = lax.axis_size("stream") * lax.axis_size("batch")
    share = width // peers
    packed = jnp.concatenate(
        [
            *dw_q,
            dw_out,
            dw_up,
            dw_down.reshape(peers, -1, share, width).swapaxes(1, 2).reshape(width, -1),
        ],
        axis=1,
    )
    summed = lax.psum_scatter(packed, both, scatter_dimension=0, tiled=True).astype(f32)
    pieces = jnp.split(summed, [3 * width, 4 * width, 4 * width + w_up.shape[1]], axis=1)
    pieces[3] = pieces[3].reshape(share, -1, width).swapaxes(0, 1)
    gains = lax.psum(jnp.stack([jnp.sum(dgain_one, axis=0), jnp.sum(dgain_two, axis=0)]), both)
    at = (side * lax.axis_size("batch") + lax.axis_index("batch")) * share
    gains = lax.dynamic_slice(gains, (0, at), (2, share))
    return (
        hand_back(out),
        hand_back(dx),
        gains[0],
        pieces[0].reshape(share, 3 * width),
        pieces[1].reshape(share, width),
        gains[1],
        pieces[2].reshape(share, -1),
        pieces[3].reshape(-1, width),
    )


def solution(mesh):
    token = P("stream", "batch", None, None)
    vector, matrix = P("batch"), P("batch", None)
    out_vector, out_matrix = P(("stream", "batch")), P(("stream", "batch"), None)
    return jax.shard_map(
        shards,
        mesh=mesh,
        in_specs=(token, token, vector, vector, matrix, matrix, vector, matrix, matrix),
        out_specs=(token, token, out_vector, out_matrix, out_matrix, out_vector, out_matrix, out_matrix),
        check_vma=False,
    )
```

time: 1300 us -> 654 us (0.50)
  matrix products: 492 us -> 0 us
  local copies, waits for them, and re-layouts: 344 us -> 44.9 us
  Pallas kernels: 0 us -> 276 us
  other arithmetic: 245 us -> 27.7 us
  blocking collectives: 79 us -> 199 us
  waiting for transfers between devices: 99.8 us -> 74.8 us
    dot_general x72 -> x0, matrix products: 492 us -> none  [the longest x4 59.6 us: group_backward(): jnp.einsum('qhd,khd->hqk', grad3, value3, preferred_element_type=jnp.floa...]
    pallas_call x0 -> x12, Pallas kernels: none -> 276 us  [the longest x1 87.4 us: attend_back(): pl.pallas_call(attend_back_kernel, name='attend_back', grid_spec=pltpu.Pr...]
    psum x0 -> x1, blocking collectives: none -> 165 us  [shards(): lax.psum(jnp.stack([jnp.sum(dgain_one, axis=0), jnp.sum(dgain_two, axis=0...]
    reshape x24 -> x1, local copies, waits for them, and re-layouts: 78.2 us -> 0.14 us  [shards(): pieces[3] = pieces[3].reshape(share, -1, width).swapaxes(0, 1)]
    convert_element_type x13 -> x3, other arithmetic: 75 us -> 2.18 us  [the longest x1 1.13 us: mask_tables(): noisy_query = (lane == blk - 1).astype(bf16)]
    ppermute x4, waiting for transfers between devices: 80.3 us -> 14.3 us  [the longest x2 14.3 us: pair_up(): away = lax.ppermute(jnp.take(field[0], 1 - side, axis=0), 'stream', swap)]
    all_gather x4, waiting for transfers between devices: 0.03 us -> 57.9 us  [the longest x1 54.1 us: shards(): w_down_all = lax.all_gather(w_down, 'batch', axis=0, tiled=True)]
    slice x42 -> x3, local copies, waits for them, and re-layouts: 69.6 us -> 12.3 us  [the longest x1 6.92 us: shards(): dqkv3[i]]
  transfers between devices with their start and end apart: 12 -> 9, of which waited for: 4 -> 3; matrix products, arithmetic and copies ran while one was open for 70% -> 6% of each run, Pallas kernels for 0% -> 13%
where the time goes in v1:
time: 654 us; the launch traced here: 643 us
  Pallas kernels  276 us (42%)
  blocking collectives  199 us (30%)
  waiting for transfers between devices  74.8 us (11%)
  local copies, waits for them, and re-layouts  44.9 us (7%)
  other arithmetic  27.7 us (4%)
  between operations  15.9 us (2%)
    psum x1, blocking collectives, shards(): lax.psum(jnp.stack([jnp.sum(dgain_one, axis=0), jnp.sum(dgain_two, axis=0...  165 us
    pallas_call x1, Pallas kernels, attend_back(): pl.pallas_call(attend_back_kernel, name='attend_back', grid_spec=pltpu.Pr...  87.4 us
    pallas_call x1, Pallas kernels, feed(): pl.pallas_call(functools.partial(feed_kernel, chunk=chunk), name='feed',...  62 us
    all_gather x1, waiting for transfers between devices, shards(): w_down_all = lax.all_gather(w_down, 'batch', axis=0, tiled=True)  54.1 us
    pallas_call x6, Pallas kernels, weight_grad(): pl.pallas_call(weight_kernel, name=name, grid=(dl // block_l, dr // block...  45.7 us
    pallas_call x1, Pallas kernels, attend(): pl.pallas_call(attend_kernel, name='attend', grid_spec=pltpu.PrefetchScal...  44.1 us
    unnamed x1, blocking collectives  34.1 us
    unnamed x71, local copies, waits for them, and re-layouts  17.5 us
  transfers between devices with their start and end apart: 9, of which 3 were waited for; matrix products, arithmetic and copies ran while one was open for 6% of the time, Pallas kernels for 13%

profile of v1, /device:TPU:0, one launch (start us, length us, event | category | flops | bytes accessed | tf_op | source)
XLA Modules:
  0.0 643.5 jit_solution(13980844077951594217)
XLA Ops:
  10.0 3.5 select_bitcast_fusion.5
  20.2 34.1 %all-reduce.2 = (bf16[768]{0:T(1024)(128)(2,1)S(1)}, bf16[768]{0:T(1024)(128)(2,1)S(1)}) all-reduce(bf16[768]{0:T(1024)(128)(2,1)S(1)} %dynamic-update-slice.2, bf16[768]{0:T(1024)(128)(2,1)S(1)} %dynamic-update-slice.3), channel_id=1, replica_groups=mesh['stream'=2,'batch'=16] {'batch'}, use_global_device_ids=true, to_apply=%add | all-reduce | flops 1536 | bytes 6144
  62.1 3.3 pad_maximum_fusion.x_ref
  65.4 5.2 norm_rows.1.left_ref
  70.6 14.3 %collective-permute-done.1 = bf16[1024,768]{1,0:T(8,128)(2,1)} collective-permute-done((bf16[1024,768]{1,0:T(8,128)(2,1)S(1)}, bf16[1024,768]{1,0:T(8,128)(2,1)}, u32[]{:S(2)}, u32[]{:S(2)}) %collective-permute-start.1) | collective-permute-done | bytes 1572896 | tf_op jit(solution)/shard_map/ppermute | solution.py:490
  84.8 4.0 pad_maximum_fusion.1.grad_ref.right_ref
  91.0 14.2 %project.1 = bf16[3,2048,768]{2,1,0:T(8,128)(2,1)} custom-call(bf16[2048,768]{1,0:T(8,128)(2,1)S(1)} %copy-done, bf16[1,768]{1,0:T(2,128)(2,1)S(1)} %copy-done.14, bf16[768,2304]{1,0:T(8,128)(2,1)} %all-gather.5.cloned.1.call-done.w_ref, f32[1024,128]{1,0:T(8,128)S(1)} %copy-done.4, f32[1024,128]{1,0:T(8,128)S(1)} %copy-done.6), custom_call_target="tpu_custom_call" | custom-call | flops 7247757312 | bytes 16121856 | tf_op jit(solution)/shard_map/project/pallas_call | solution.py:72
  105.1 44.1 %attend.1 = (bf16[2,1024,768]{2,1,0:T(8,128)(2,1)S(1)}, f32[2,6,2,1024]{3,2,1,0:T(2,128)S(1)}) custom-call(s32[1]{0:T(128)} %bitcast.3.side_ref, bf16[3,2,1024,768]{3,2,1,0:T(8,128)(2,1)} %bitcast.62, bf16[1024,128]{1,0:T(8,128)(2,1)S(1)} %copy-done.12, bf16[1024,128]{1,0:T(8,128)(2,1)S(1)} %copy-done.10, bf16[1024,128]{1,0:T(8,128)(2,1)S(1)} %copy-done.8, ...), custom_call_target="tpu_custom_call" | custom-call | flops 6442450944 | bytes 12582912 | tf_op jit(solution)/shard_map/attend/pallas_call | solution.py:162
  151.0 3.8 all-gather.9.cloned.1.call-done.wu_ref
  154.7 54.1 %all-gather.11.cloned.1.call-done.wd_ref = bf16[3072,768]{1,0:T(8,128)(2,1)} async-done(((bf16[192,768]{1,0:T(8,128)(2,1)}), bf16[3072,768]{1,0:T(8,128)(2,1)}) %all-gather.11.cloned.1.call-update) | async-done | bytes 4718608 | tf_op jit(solution)/shard_map/all_gather | solution.py:503
  208.8 62.0 %feed.1 = (bf16[2048,768]{1,0:T(8,128)(2,1)}, bf16[2048,3072]{1,0:T(8,128)(2,1)}, bf16[2048,3072]{1,0:T(8,128)(2,1)}, bf16[2048,768]{1,0:T(8,128)(2,1)}, f32[204...) custom-call(bf16[2048,768]{1,0:T(8,128)(2,1)} %pad_maximum_fusion.x_ref, ...), custom_call_target="tpu_custom_call" | custom-call | flops 43486543872 | bytes 53477376 | tf_op jit(solution)/shard_map/feed/pallas_call | solution.py:369
  270.8 4.7 grad_out.1
  275.5 13.6 %grad_down.1 = bf16[3072,768]{1,0:T(8,128)(2,1)} custom-call(bf16[2048,3072]{1,0:T(8,128)(2,1)} %get-tuple-element.32.left_ref, bf16[2048,768]{1,0:T(8,128)(2,1)S(1)} %copy-done.3), custom_call_target="tpu_custom_call" | custom-call | flops 9663676416 | bytes 20447232 | tf_op jit(solution)/shard_map/grad_down/pallas_call | solution.py:400
  289.2 4.7 copy.20
  293.9 3.2 copy.22
  297.1 87.4 %attend_back.1 = bf16[3,2,1024,768]{3,2,1,0:T(8,128)(2,1)} custom-call(s32[1]{0:T(128)} %bitcast.3.side_ref, bf16[3,2,1024,768]{3,2,1,0:T(8,128)(2,1)} %bitcast.63, bf16[2,1024,768]{2,1,0:T(8,128)(2,1)S(1)} %copy-done.16, bf16[2,1024,768]{2,1,0:T(8,128)(2,1)} %bitcast.64, f32[2,6,2,1024]{3,2,1,0:T(2,128)S(1)} %get-tuple-element.24.log_ref, ...), custom_call_target="tpu_custom_call" | custom-call | flops 16106127360 | bytes 23592960 | tf_op jit(solution)/shard_map/attend_back/pallas_call | solution.py:284
  384.6 6.9 %fusion.4 = (bf16[1,2,1024,768]{3,2,1,0:T(8,128)(2,1)}, bf16[1,2,1024,768]{3,2,1,0:T(8,128)(2,1)}, bf16[1,2,1024,768]{3,2,1,0:T(8,128)(2,1)}) fusion(bf16[3,2,1024,768]{3,2,1,0:T(8,128)(2,1)} %attend_back.1), kind=kLoop, calls=%fused_computation.43 | loop fusion | bytes 18874368 | tf_op jit(solution)/shard_map/slice | solution.py:524
  391.8 4.5 grad_qkv.5
  396.4 4.5 grad_qkv.4
  400.9 4.7 grad_qkv.3
  406.8 13.6 %grad_up.1 = bf16[768,3072]{1,0:T(8,128)(2,1)} custom-call(bf16[2048,768]{1,0:T(8,128)(2,1)S(1)} %copy-done.17, bf16[2048,3072]{1,0:T(8,128)(2,1)} %get-tuple-element.31.right_ref), custom_call_target="tpu_custom_call" | custom-call | flops 9663676416 | bytes 20447232 | tf_op jit(solution)/shard_map/grad_up/pallas_call | solution.py:400
  430.8 17.1 %project_back.1 = (f32[2048,768]{1,0:T(8,128)}, f32[8,768]{1,0:T(8,128)S(1)}) custom-call(bf16[2048,768]{1,0:T(8,128)(2,1)S(1)} %copy-done.1, bf16[1,768]{1,0:T(2,128)(2,1)S(1)} %copy-done.14, bf16[768,2304]{1,0:T(8,128)(2,1)} %all-gather.5.cloned.1.call-done.w_ref, bf16[3,2048,768]{2,1,0:T(8,128)(2,1)} %bitcast.51, f32[2048,768]{1,0:T(8,128)} %get-tuple-element.25.dmid_ref), custom_call_target="tpu_custom_call" | custom-call | flops 7247757312 | bytes 25165824 | tf_op jit(solution)/shard_map/project_back/pallas_call | solution.py:442
  447.8 4.1 slice.33
  455.3 165.3 %psum.7 = f32[2,768]{1,0:T(2,128)S(1)} all-reduce(f32[2,768]{1,0:T(2,128)S(1)} %pad_maximum_fusion.4), channel_id=1, replica_groups=mesh['stream'=2,'batch'=16] {'stream','batch'}, use_global_device_ids=true, to_apply=%region_2.4 | all-reduce | flops 1536 | bytes 12288 | tf_op jit(solution)/shard_map/psum | solution.py:542
  (123 shorter events, 50.8 us)
Async XLA Ops:
  7.2 81.7 %all-gather.5.cloned.1.call-start = ((), (), s32[]{:S(2)}) async-start(), calls=%async_computation.1 | async-start | bytes 3760128 | tf_op jit(solution)/shard_map/all_gather | solution.py:498
  7.9 143.1 %all-gather.7.cloned.1.call-start = ((), (), s32[]{:S(2)}) async-start(), calls=%async_computation.2 | async-start | bytes 1253376 | tf_op jit(solution)/shard_map/all_gather | solution.py:501
  8.7 146.1 %all-gather.9.cloned.1.call-start = ((), (), s32[]{:S(2)}) async-start(), calls=%async_computation.3 | async-start | bytes 5013504 | tf_op jit(solution)/shard_map/all_gather | solution.py:502
  9.4 199.5 %all-gather.11.cloned.1.call-start = ((), (), s32[]{:S(2)}) async-start(), calls=%async_computation.4 | async-start | bytes 5013504 | tf_op jit(solution)/shard_map/all_gather | solution.py:503
  10.0 620.9 %reduce-scatter.2.cloned.1.call-start = ((), (), s32[]{:S(2)}) async-start(), calls=%async_computation.5 | async-start | bytes 14598144 | tf_op jit(solution)/shard_map/reduce_scatter | solution.py:539
  10.0 6.4 copy-start.19
  13.5 48.6 %collective-permute-start = (bf16[1024,768]{1,0:T(8,128)(2,1)}, bf16[1024,768]{1,0:T(8,128)(2,1)}, u32[]{:S(2)}, u32[]{:S(2)}) collective-permute-start(bf16[1024,768]{1,0:T(8,128)(2,1)} %get-tuple-element.67), channel_id=1, source_target_pairs={{0,16},{16,0},{1,17},{17,1},{2,18},{18,2},{3,19},{19,3},{4,20},{20... | collective-permute-start | bytes 4718600 | tf_op jit(solution)/shard_map/ppermute | solution.py:490
  16.4 3.6 copy-start.24
  17.9 67.0 %collective-permute-start.1 = (bf16[1024,768]{1,0:T(8,128)(2,1)S(1)}, bf16[1024,768]{1,0:T(8,128)(2,1)}, u32[]{:S(2)}, u32[]{:S(2)}) collective-permute-start(bf16[1024,768]{1,0:T(8,128)(2,1)S(1)} %get-tuple-element.65), channel_id=1, source_target_pairs={{0,16},{16,0},{1,17},{17,1},{2,18},{18,2},{3,19},{19,3},{4,20},{20... | collective-permute-start | bytes 4718600 | tf_op jit(solution)/shard_map/ppermute | solution.py:490
  84.8 4.0 copy-start
  84.8 4.0 copy-start.14
  90.9 14.2 %copy-start.8 = (bf16[1024,128]{1,0:T(8,128)(2,1)S(1)}, bf16[1024,128]{1,0:T(8,128)(2,1)}, u32[]{:S(2)}) copy-start(bf16[1024,128]{1,0:T(8,128)(2,1)} %get-tuple-element.71.mk_ref) | copy-start | bytes 786436
  90.9 14.2 %copy-start.10 = (bf16[1024,128]{1,0:T(8,128)(2,1)S(1)}, bf16[1024,128]{1,0:T(8,128)(2,1)}, u32[]{:S(2)}) copy-start(bf16[1024,128]{1,0:T(8,128)(2,1)} %get-tuple-element.77.nq_ref) | copy-start | bytes 786436
  90.9 14.2 %copy-start.12 = (bf16[1024,128]{1,0:T(8,128)(2,1)S(1)}, bf16[1024,128]{1,0:T(8,128)(2,1)}, u32[]{:S(2)}) copy-start(bf16[1024,128]{1,0:T(8,128)(2,1)} %get-tuple-element.78.cq_ref) | copy-start | bytes 786436
  208.8 62.0 %copy-start.16 = (bf16[2,1024,768]{2,1,0:T(8,128)(2,1)S(1)}, bf16[2,1024,768]{2,1,0:T(8,128)(2,1)}, u32[]{:S(2)}) copy-start(bf16[2,1024,768]{2,1,0:T(8,128)(2,1)} %copy-done.15) | copy-start | bytes 9437188
  270.8 4.7 copy-start.3
  384.6 7.3 %copy-start.2 = (bf16[2048,768]{1,0:T(8,128)(2,1)S(1)}, bf16[2048,768]{1,0:T(8,128)(2,1)}, u32[]{:S(2)}) copy-start(bf16[2048,768]{1,0:T(8,128)(2,1)} %norm_rows.1.left_ref) | copy-start | bytes 9437188
  400.9 5.9 copy-start.17
  422.7 3.7 slice-start
  447.8 5.3 copy-start.20
  452.0 173.4 %collective-permute-start.3 = (f32[1024,768]{1,0:T(8,128)}, f32[1024,768]{1,0:T(8,128)}, u32[]{:S(2)}, u32[]{:S(2)}) collective-permute-start(f32[1024,768]{1,0:T(8,128)} %slice.33), channel_id=1, source_target_pairs={{0,16},{16,0},{1,17},{17,1},{2,18},{18,2},{3,19},{19,3},{4,20},{20... | collective-permute-start | bytes 9437192 | tf_op jit(solution)/shard_map/ppermute | solution.py:494
  453.2 172.2 %slice-start.2 = ((s8[6291456]{0:T(1024)(128)(4,1)}), s8[2097152]{0:T(1024)(128)(4,1)S(1)}, s32[]{:S(2)}) async-start(s8[6291456]{0:T(1024)(128)(4,1)} %bitcast.52), calls=%async_computation.8 | async-start | bytes 4194304
  454.4 166.8 %collective-permute-start.2 = (bf16[1024,768]{1,0:T(8,128)(2,1)}, bf16[1024,768]{1,0:T(8,128)(2,1)}, u32[]{:S(2)}, u32[]{:S(2)}) collective-permute-start(bf16[1024,768]{1,0:T(8,128)(2,1)} %slice.31), channel_id=1, source_target_pairs={{0,16},{16,0},{1,17},{17,1},{2,18},{18,2},{3,19},{19,3},{4,20},{20... | collective-permute-start | bytes 4718600 | tf_op jit(solution)/shard_map/ppermute | solution.py:494
  621.2 4.2 slice-start.3
  (15 other events, 37.9 us)
Sparse Core Ops, SparseCore 0:
  10.3 49.9 all-gather.4
  62.6 37.3 all-gather.6
  102.3 52.3 all-gather.8
  156.9 51.9 all-gather.10
  429.0 180.8 reduce-scatter.1

commit v2 on v1

--- a/solution.py
+++ b/solution.py
@@ -46,12 +46,23 @@
     return jnp.where(low, pltpu.roll(x, LANES - HD // 2, 1), pltpu.roll(x, HD // 2, 1))
 
 
-def project_kernel(x_ref, gain_ref, w_ref, cos_ref, sin_ref, out_ref):
-    x = x_ref[...].astype(f32)
+def row_specs(tile, width, half):
+    own = pl.BlockSpec((None, None, tile, width), lambda i, s: (0, s[0], jnp.minimum(i, half - 1), 0))
+    away = pl.BlockSpec((tile, width), lambda i, s: (jnp.maximum(i - half, 0), 0))
+    return own, away
+
+
+def read_rows(own_ref, away_ref, half):
+    return jnp.where(pl.program_id(0) < half, own_ref[...], away_ref[...])
+
+
+def project_kernel(side_ref, own_ref, away_ref, gain_ref, w_ref, cos_ref, sin_ref, out_ref, hidden_ref, *, half):
+    x = read_rows(own_ref, away_ref, half).astype(f32)
     width = x.shape[1]
     center = x - jnp.mean(x, axis=1, keepdims=True)
     spread = jnp.mean(center * center, axis=1, keepdims=True)
     hidden = (center * lax.rsqrt(spread + 1e-5) * gain_ref[...].astype(f32)).astype(bf16)
+    hidden_ref[...] = hidden
     cosine, sine = cos_ref[...], sin_ref[...]
     for part in range(3):
         rows = mm(hidden, w_ref[:, part * width : (part + 1) * width])
@@ -65,28 +76,34 @@
             out_ref[part, :, cols] = field.astype(bf16)
 
 
-def project(x, gain, w, cosine, sine, tile=256):
-    tokens, width = x.shape
-    length = cosine.shape[0]
-    per = length // tile
+def project(side, own, away, gain, w, cosine, sine, tile=512):
+    length, width = away.shape
+    tokens, half = 2 * length, length // tile
+    table = pl.BlockSpec((tile, LANES), lambda i, s: (lax.rem(i, half), 0))
     return pl.pallas_call(
-        project_kernel,
+        functools.partial(project_kernel, half=half),
         name="project",
-        grid=(tokens // tile,),
-        in_specs=[
-            pl.BlockSpec((tile, width), lambda i: (i, 0)),
-            pl.BlockSpec((1, width), lambda i: (0, 0)),
-            pl.BlockSpec((width, 3 * width), lambda i: (0, 0), pipeline_mode=pl.Buffered(1)),
-            pl.BlockSpec((tile, LANES), lambda i: (lax.rem(i, per), 0)),
-            pl.BlockSpec((tile, LANES), lambda i: (lax.rem(i, per), 0)),
-        ],
-        out_specs=pl.BlockSpec((3, tile, width), lambda i: (0, i, 0)),
-        out_shape=jax.ShapeDtypeStruct((3, tokens, width), bf16),
+        grid_spec=pltpu.PrefetchScalarGridSpec(
+            num_scalar_prefetch=1,
+            grid=(2 * half,),
+            in_specs=[
+                *row_specs(tile, width, half),
+                pl.BlockSpec((1, width), lambda i, s: (0, 0)),
+                pl.BlockSpec((width, 3 * width), lambda i, s: (0, 0), pipeline_mode=pl.Buffered(1)),
+                table,
+                table,
+            ],
+            out_specs=[
+                pl.BlockSpec((3, tile, width), lambda i, s: (0, i, 0)),
+                pl.BlockSpec((tile, width), lambda i, s: (i, 0)),
+            ],
+        ),
+        out_shape=[jax.ShapeDtypeStruct((3, tokens, width), bf16), jax.ShapeDtypeStruct((tokens, width), bf16)],
         compiler_params=pltpu.CompilerParams(vmem_limit_bytes=48 << 20),
         cost_estimate=pl.CostEstimate(
-            flops=6 * tokens * width * width, bytes_accessed=tokens * width * 8 + 6 * width * width, transcendentals=0
-        ),
-    )(x, gain, w, cosine, sine)
+            flops=6 * tokens * width * width, bytes_accessed=tokens * width * 10 + 6 * width * width, transcendentals=0
+        ),
+    )(side, own, away, gain, w, cosine, sine)
 
 
 def mask_tables(length, row_length):
@@ -189,12 +206,8 @@
     )(side, qkv, *tables)
 
 
-def split3(x):
-    hi = x.astype(bf16)
-    rest = x - hi.astype(f32)
-    mid = rest.astype(bf16)
-    lo = (rest - mid.astype(f32)).astype(bf16)
-    return hi, mid, lo
+def attend_back_next(side_ref, _, *refs):
+    attend_back_kernel(side_ref, *refs)
 
 
 def attend_back_kernel(side_ref, qkv_ref, o_ref, do_ref, log_ref, cq_ref, nq_ref, mk_ref, dk_ref, cos_ref, sin_ref,
@@ -275,19 +288,25 @@
     dqkv_ref[0, noisy] = finish(dq[1].T, True, 0.125)
 
 
-def attend_back(side, qkv, mixed, grad, logs, tables, cosine, sine):
+def attend_back(side, into, first, pairs, qkv, mixed, grad, logs, tables, cosine, sine):
     _, copies, length, width = qkv.shape
-    pairs = width // LANES
     table_spec = pl.BlockSpec((length, LANES), lambda i, s: (0, 0), pipeline_mode=pl.Buffered(1))
-    row_spec = pl.BlockSpec((copies, length, LANES), lambda i, s: (0, 0, i))
-    three = pl.BlockSpec((3, copies, length, LANES), lambda i, s: (0, 0, 0, i))
+    row_spec = pl.BlockSpec((copies, length, LANES), lambda i, s: (0, 0, i + first))
+    three = pl.BlockSpec((3, copies, length, LANES), lambda i, s: (0, 0, 0, i + first))
+    begun = [] if into is None else [into]
     return pl.pallas_call(
-        attend_back_kernel,
+        attend_back_next if begun else attend_back_kernel,
         name="attend_back",
         grid_spec=pltpu.PrefetchScalarGridSpec(
             num_scalar_prefetch=1,
             grid=(pairs,),
-            in_specs=[three, row_spec, row_spec, pl.BlockSpec((copies, 1, 2, length), lambda i, s: (0, i, 0, 0))]
+            in_specs=[
+                *[pl.BlockSpec(memory_space=pl.ANY)] * len(begun),
+                three,
+                row_spec,
+                row_spec,
+                pl.BlockSpec((copies, 1, 2, length), lambda i, s: (0, i + first, 0, 0)),
+            ]
             + [table_spec] * 6,
             out_specs=three,
             scratch_shapes=[
@@ -304,45 +323,83 @@
             ],
         ),
         out_shape=jax.ShapeDtypeStruct((3, copies, length, width), bf16),
+        input_output_aliases={1: 0} if begun else {},
         compiler_params=pltpu.CompilerParams(vmem_limit_bytes=48 << 20),
         cost_estimate=pl.CostEstimate(
-            flops=20 * length * length * width, bytes_accessed=30 * length * width, transcendentals=length * length * 12
-        ),
-    )(side, qkv, mixed, grad, logs, *tables, cosine, sine)
+            flops=20 * length * length * LANES * pairs,
+            bytes_accessed=32 * length * LANES * pairs,
+            transcendentals=4 * length * length * pairs,
+        ),
+    )(side, *begun, qkv, mixed, grad, logs, *tables, cosine, sine)
 
 
 ROOT = math.sqrt(2.0 / math.pi)
 
 
-def feed_kernel(x_ref, mixed_ref, grad_ref, gain_ref, wo_ref, wu_ref, wd_ref,
-                out_ref, act_ref, du_ref, h2_ref, dmid_ref, dbr_ref, dmix_ref, dgain_ref, *, chunk):
-    width, ff = wu_ref.shape
+def feed_kernel(side_ref, x_own, x_away, mixed_ref, g_own, g_away, gain_ref, rest_ref,
+                out_own, out_away, act_ref, du_ref, h2_ref, dmid_ref, dbr_ref, dmix_ref, dgain_ref,
+                wo_ref, wu_ref, wd_ref, sems, *, half):
+    groups, rows, width = wo_ref.shape
+    fold = wd_ref.shape[1]
+    ff = fold * width
+
+    def fetch(n):
+        cols = rest_ref.at[:, :, n * width : (n + 1) * width]
+        if n == 0:
+            into = wo_ref
+        elif n <= fold:
+            into = wu_ref.at[n - 1]
+        else:
+            into = wd_ref.at[:, n - 1 - fold]
+        return pltpu.make_async_copy(cols, into, sems.at[n])
+
+    @pl.when(pl.program_id(0) == 0)
+    def _():
+        for n in range(1 + 2 * fold):
+            fetch(n).start()
+        for n in range(1 + 2 * fold):
+            fetch(n).wait()
+
+    def down(c):
+        per = groups // fold
+        return wd_ref[c * per : (c + 1) * per].reshape(width, width)
+
+    wo = wo_ref[...].reshape(width, width)
     gain = gain_ref[...].astype(f32)
-    middle = x_ref[...].astype(f32) + mm(mixed_ref[...], wo_ref[...])
+    middle = read_rows(x_own, x_away, half).astype(f32) + mm(mixed_ref[...], wo)
     center = middle - jnp.mean(middle, axis=1, keepdims=True)
     spread = jnp.mean(center * center, axis=1, keepdims=True)
     inv = lax.rsqrt(spread + 1e-5)
     norm = center * inv
     hidden = (norm * gain).astype(bf16)
     h2_ref[...] = hidden
-    grad = grad_ref[...]
+    grad = read_rows(g_own, g_away, half)
     out = middle
     dh = jnp.zeros_like(middle)
-    for c in range(ff // chunk):
-        cols = slice(c * chunk, (c + 1) * chunk)
-        u = mm(hidden, wu_ref[:, cols])
-        da = mm_t(grad, wd_ref[cols, :]).astype(bf16).astype(f32)
+    for c in range(fold):
+        cols = slice(c * width, (c + 1) * width)
+        up = wu_ref[c].reshape(width, width)
+        u = mm(hidden, up)
+        da = mm_t(grad, down(c)).astype(bf16).astype(f32)
         sq = u * u
         t = jnp.tanh(u * (ROOT + (ROOT * 0.044715) * sq))
-        half = 0.5 + 0.5 * t
-        act = (u * half).astype(bf16)
-        slope = half + (u * (half * (1.0 - t))) * (ROOT + (3 * ROOT * 0.044715) * sq)
+        part = 0.5 + 0.5 * t
+        act = (u * part).astype(bf16)
+        slope = part + (u * (part * (1.0 - t))) * (ROOT + (3 * ROOT * 0.044715) * sq)
         du = (da * slope).astype(bf16)
         act_ref[:, cols] = act
         du_ref[:, cols] = du
-        out = out + mm(act, wd_ref[cols, :])
-        dh = dh + mm_t(du, wu_ref[:, cols])
-    out_ref[...] = out.astype(bf16)
+        out = out + mm(act, down(c))
+        dh = dh + mm_t(du, up)
+    low = out.astype(bf16)
+
+    @pl.when(pl.program_id(0) < half)
+    def _():
+        out_own[...] = low
+
+    @pl.when(pl.program_id(0) >= half)
+    def _():
+        out_away[...] = low
 
     @pl.when(pl.program_id(0) == 0)
     def _():
@@ -356,24 +413,40 @@
     dmid_ref[...] = dmid
     dbr = dmid.astype(bf16)
     dbr_ref[...] = dbr
-    dmix_ref[...] = mm_t(dbr, wo_ref[...]).astype(bf16)
-
-
-def feed(x, mixed, grad, gain, wo, wu, wd, tile=256, chunk=768):
-    tokens, width = x.shape
-    ff = wu.shape[1]
-    row = pl.BlockSpec((tile, width), lambda i: (i, 0))
-    wide = pl.BlockSpec((tile, ff), lambda i: (i, 0))
+    dmix_ref[...] = mm_t(dbr, wo).astype(bf16)
+
+
+def feed(side, x_own, x_away, mixed, g_own, g_away, gain, rest, tile=512):
+    tokens, width = mixed.shape
+    groups, rows, columns = rest.shape
+    fold = (columns // width - 1) // 2
+    ff = fold * width
+    half = tokens // 2 // tile
+    row = pl.BlockSpec((tile, width), lambda i, s: (i, 0))
+    wide = pl.BlockSpec((tile, ff), lambda i, s: (i, 0))
+    own, away = row_specs(tile, width, half)
+
     def keep(shape):
-        return pl.BlockSpec(shape, lambda i: (0, 0), pipeline_mode=pl.Buffered(1))
+        return pl.BlockSpec(shape, lambda i, s: (0, 0), pipeline_mode=pl.Buffered(1))
+
     return pl.pallas_call(
-        functools.partial(feed_kernel, chunk=chunk),
+        functools.partial(feed_kernel, half=half),
         name="feed",
-        grid=(tokens // tile,),
-        in_specs=[row, row, row, keep((1, width)), keep((width, width)), keep((width, ff)), keep((ff, width))],
-        out_specs=[row, wide, wide, row, row, row, row, pl.BlockSpec((8, width), lambda i: (0, 0))],
+        grid_spec=pltpu.PrefetchScalarGridSpec(
+            num_scalar_prefetch=1,
+            grid=(2 * half,),
+            in_specs=[own, away, row, own, away, keep((1, width)), pl.BlockSpec(memory_space=pl.ANY)],
+            out_specs=[own, away, wide, wide, row, row, row, row, pl.BlockSpec((8, width), lambda i, s: (0, 0))],
+            scratch_shapes=[
+                pltpu.VMEM((groups, rows, width), bf16),
+                pltpu.VMEM((fold, groups, rows, width), bf16),
+                pltpu.VMEM((groups, fold, rows, width), bf16),
+                pltpu.SemaphoreType.DMA((1 + 2 * fold,)),
+            ],
+        ),
         out_shape=[
-            jax.ShapeDtypeStruct((tokens, width), bf16),
+            jax.ShapeDtypeStruct((1, 2, tokens // 2, width), bf16),
+            jax.ShapeDtypeStruct((tokens // 2, width), bf16),
             jax.ShapeDtypeStruct((tokens, ff), bf16),
             jax.ShapeDtypeStruct((tokens, ff), bf16),
             jax.ShapeDtypeStruct((tokens, width), bf16),
@@ -387,34 +460,87 @@
             flops=tokens * width * (4 * width + 8 * ff), bytes_accessed=tokens * (width * 18 + ff * 4),
             transcendentals=tokens * ff
         ),
-    )(x, mixed, grad, gain, wo, wu, wd)
-
-
-def weight_kernel(left_ref, right_ref, out_ref):
-    out_ref[...] = t_mm(left_ref[...], right_ref[...]).astype(bf16)
-
-
-def weight_grad(left, right, block_l, block_r, name):
+    )(side, x_own, x_away, mixed, g_own, g_away, gain, rest)
+
+
+def weight_kernel(me_ref, left_ref, *refs, share, split):
+    right_refs, (keep_ref, send_ref, scr) = refs[:-3], refs[-3:]
+    if split:
+        own_ref, away_ref = right_refs
+        half = own_ref.shape[0]
+        total = t_mm(left_ref[:half], own_ref[...]) + t_mm(left_ref[half:], away_ref[...])
+    else:
+        total = t_mm(left_ref[...], right_refs[0][...])
+    slabs = total.shape[0] // share
+    scr[...] = total.reshape(scr.shape)
+    low_me = lax.rem(me_ref[0], slabs)
+    for slot in range(slabs):
+        source = jnp.bitwise_xor(low_me, slot)
+        into = send_ref if slot % 2 else keep_ref
+        into[slot // 2] = scr[source].astype(bf16)
+
+
+def weight_grad_columns(me, left, right, part, block, share, name):
     tokens, dl = left.shape
-    dr = right.shape[1]
+    dr = right.shape[2]
+    peers = dl // share
+    shape = (peers // 2, share, dr)
+    out = pl.BlockSpec((peers // 2, share, block), lambda j, m: (0, 0, j))
     return pl.pallas_call(
-        weight_kernel,
+        functools.partial(weight_kernel, share=share, split=False),
         name=name,
-        grid=(dl // block_l, dr // block_r),
-        in_specs=[
-            pl.BlockSpec((tokens, block_l), lambda i, j: (0, i)),
-            pl.BlockSpec((tokens, block_r), lambda i, j: (0, j)),
-        ],
-        out_specs=pl.BlockSpec((block_l, block_r), lambda i, j: (i, j)),
-        out_shape=jax.ShapeDtypeStruct((dl, dr), bf16),
+        grid_spec=pltpu.PrefetchScalarGridSpec(
+            num_scalar_prefetch=1,
+            grid=(dr // block,),
+            in_specs=[
+                pl.BlockSpec((tokens, dl), lambda j, m: (0, 0), pipeline_mode=pl.Buffered(1)),
+                pl.BlockSpec((None, tokens, block), lambda j, m: (part, 0, j)),
+            ],
+            out_specs=[out, out],
+            scratch_shapes=[pltpu.VMEM((peers, share, block), f32)],
+        ),
+        out_shape=[jax.ShapeDtypeStruct(shape, bf16)] * 2,
         compiler_params=pltpu.CompilerParams(vmem_limit_bytes=48 << 20),
         cost_estimate=pl.CostEstimate(
             flops=2 * tokens * dl * dr, bytes_accessed=2 * tokens * (dl + dr) + 2 * dl * dr, transcendentals=0
         ),
-    )(left, right)
-
-
-def project_back_kernel(x_ref, gain_ref, w_ref, dqkv_ref, dmid_ref, dx_ref, dgain_ref):
+    )(me, left, right)
+
+
+def weight_grad_rows(me, left, own, away, block, share, name):
+    tokens, dl = left.shape
+    length, dr = away.shape
+    slabs = block // share
+    steps = dl // block
+    shape = (steps * slabs // 2, share, dr)
+    out = pl.BlockSpec((slabs // 2, share, dr), lambda j, m: (j, 0, 0))
+
+    def place(j, m):
+        return (0, jnp.bitwise_xor(j, lax.div(m[0], slabs)))
+
+    return pl.pallas_call(
+        functools.partial(weight_kernel, share=share, split=True),
+        name=name,
+        grid_spec=pltpu.PrefetchScalarGridSpec(
+            num_scalar_prefetch=1,
+            grid=(steps,),
+            in_specs=[
+                pl.BlockSpec((tokens, block), place),
+                pl.BlockSpec((None, None, length, dr), lambda j, m: (0, m[1], 0, 0), pipeline_mode=pl.Buffered(1)),
+                pl.BlockSpec((length, dr), lambda j, m: (0, 0), pipeline_mode=pl.Buffered(1)),
+            ],
+            out_specs=[out, out],
+            scratch_shapes=[pltpu.VMEM((slabs, share, dr), f32)],
+        ),
+        out_shape=[jax.ShapeDtypeStruct(shape, bf16)] * 2,
+        compiler_params=pltpu.CompilerParams(vmem_limit_bytes=48 << 20),
+        cost_estimate=pl.CostEstimate(
+            flops=2 * tokens * dl * dr, bytes_accessed=2 * tokens * (dl + dr) + 2 * dl * dr, transcendentals=0
+        ),
+    )(me, left, own, away)
+
+
+def project_back_kernel(side_ref, x_ref, gain_ref, w_ref, dqkv_ref, dmid_ref, dx_ref, dgain_ref):
     x = x_ref[...].astype(f32)
     width = x.shape[1]
     center = x - jnp.mean(x, axis=1, keepdims=True)
@@ -431,127 +557,270 @@
 
     dgain_ref[...] += jnp.sum((dh * norm).reshape(-1, 8, width), axis=0)
     e = dh * gain_ref[...].astype(f32)
-    dx_ref[...] = dmid_ref[...] + inv * (
+    dx_ref[...] = (dmid_ref[...] + inv * (
         e - jnp.mean(e, axis=1, keepdims=True) - norm * jnp.mean(e * norm, axis=1, keepdims=True)
-    )
-
-
-def project_back(x, gain, w, dqkv, dmid, tile=256):
-    tokens, width = x.shape
-    row = pl.BlockSpec((tile, width), lambda i: (i, 0))
+    )).astype(dx_ref.dtype)
+
+
+def project_back(side, x, gain, w, dqkv, dmid, away, tile=256):
+    width = x.shape[-1]
+    length = dmid.shape[0] // 2
+    half = length // tile
+    first = half if away else 0
+    if away:
+        x_spec = pl.BlockSpec((tile, width), lambda i, s: (i, 0))
+        out_spec, out_shape = x_spec, jax.ShapeDtypeStruct((length, width), bf16)
+    else:
+        x_spec = pl.BlockSpec((None, None, tile, width), lambda i, s: (0, s[0], i, 0))
+        out_spec, out_shape = x_spec, jax.ShapeDtypeStruct((1, 2, length, width), f32)
     return pl.pallas_call(
         project_back_kernel,
-        name="project_back",
-        grid=(tokens // tile,),
-        in_specs=[
-            row,
-            pl.BlockSpec((1, width), lambda i: (0, 0)),
-            pl.BlockSpec((width, 3 * width), lambda i: (0, 0), pipeline_mode=pl.Buffered(1)),
-            pl.BlockSpec((3, tile, width), lambda i: (0, i, 0)),
-            row,
-        ],
-        out_specs=[row, pl.BlockSpec((8, width), lambda i: (0, 0))],
-        out_shape=[jax.ShapeDtypeStruct((tokens, width), f32), jax.ShapeDtypeStruct((8, width), f32)],
+        name="project_back_away" if away else "project_back_own",
+        grid_spec=pltpu.PrefetchScalarGridSpec(
+            num_scalar_prefetch=1,
+            grid=(half,),
+            in_specs=[
+                x_spec,
+                pl.BlockSpec((1, width), lambda i, s: (0, 0)),
+                pl.BlockSpec((width, 3 * width), lambda i, s: (0, 0), pipeline_mode=pl.Buffered(1)),
+                pl.BlockSpec((3, tile, width), lambda i, s: (0, i + first, 0)),
+                pl.BlockSpec((tile, width), lambda i, s: (i + first, 0)),
+            ],
+            out_specs=[out_spec, pl.BlockSpec((8, width), lambda i, s: (0, 0))],
+        ),
+        out_shape=[out_shape, jax.ShapeDtypeStruct((8, width), f32)],
         compiler_params=pltpu.CompilerParams(vmem_limit_bytes=48 << 20),
         cost_estimate=pl.CostEstimate(
-            flops=6 * tokens * width * width, bytes_accessed=tokens * width * 16, transcendentals=0
-        ),
-    )(x, gain, w, dqkv, dmid)
-
-
-def norm_kernel(x_ref, gain_ref, out_ref):
-    x = x_ref[...].astype(f32)
-    center = x - jnp.mean(x, axis=1, keepdims=True)
-    spread = jnp.mean(center * center, axis=1, keepdims=True)
-    out_ref[...] = (center * lax.rsqrt(spread + 1e-5) * gain_ref[...].astype(f32)).astype(bf16)
-
-
-def norm_rows(x, gain, tile=512):
-    tokens, width = x.shape
-    row = pl.BlockSpec((tile, width), lambda i: (i, 0))
+            flops=6 * length * width * width, bytes_accessed=length * width * 16, transcendentals=0
+        ),
+    )(side, x, gain, w, dqkv, dmid)
+
+
+def flip(x, bit):
+    axis, by = ("stream", 1) if bit < 0 else ("batch", 1 << bit)
+    return lax.ppermute(x, axis, [(i, i ^ by) for i in range(lax.axis_size(axis))])
+
+
+class SlabSum:
+    def __init__(self, pair, order):
+        keep, send = pair
+        bits = lax.axis_size("batch").bit_length() - 1
+        self.left = [-1, *range(bits - 1, 0, -1)]
+        self.order = list(order)
+        self.keep = keep.reshape(*[2] * bits, *keep.shape[1:])
+        self.got = flip(send.reshape(self.keep.shape), 0)
+
+    def step(self):
+        if not self.order:
+            self.keep = self.keep.astype(f32) + self.got.astype(f32)
+            return self.keep
+        bit = self.order.pop(0)
+        at = self.left.index(bit)
+        self.left.remove(bit)
+        halves = [
+            lax.index_in_dim(self.keep, i, at, False) + lax.index_in_dim(self.got, i, at, False) for i in range(2)
+        ]
+        self.keep = halves[0]
+        self.got = flip(halves[1], bit)
+        return self.keep
+
+    def finish(self):
+        while self.keep.dtype != f32:
+            self.step()
+        return self.keep
+
+
+def after(value, *others):
+    return lax.optimization_barrier((value, *others))[0]
+
+
+def all_sum(x):
+    for bit in range(-1, lax.axis_size("batch").bit_length() - 1):
+        x = x + flip(x, bit)
+    return x
+
+
+def gather_kernel(shard_ref, gain_ref, w_ref, gains_ref, local_sems, send_sems, recv_sems, *, plans):
+    side, me = lax.axis_index("stream"), lax.axis_index("batch")
+    bits = sorted(plans[0][2])
+    barrier = pltpu.get_barrier_semaphore()
+    for bit in bits:
+        pl.semaphore_signal(
+            barrier, inc=1, device_id=(side, jnp.bitwise_xor(me, 1 << bit)), device_id_type=pl.DeviceIdType.MESH
+        )
+    pl.semaphore_wait(barrier, len(bits))
+    sources, targets = [shard_ref, gain_ref], [w_ref, gains_ref]
+    local = [pltpu.make_async_copy(sources[n], targets[n].at[me], local_sems.at[n]) for n in range(2)]
+    for copy in local:
+        copy.start()
+
+    def copies(plan, step):
+        which, cols, order = plans[plan]
+        held = [0]
+        for bit in order[:step]:
+            held += [h ^ (1 << bit) for h in held]
+        done = []
+        for n, h in enumerate(held):
+            slab = jnp.bitwise_xor(me, h)
+            at = targets[which].at[slab, :, cols]
+            number = (1 << step) - 1 + n
+            done.append(
+                pltpu.make_async_remote_copy(
+                    src_ref=sources[which].at[:, cols] if h == 0 else at,
+                    dst_ref=at,
+                    send_sem=send_sems.at[plan, number],
+                    recv_sem=recv_sems.at[plan, number],
+                    device_id=(side, jnp.bitwise_xor(me, 1 << order[step])),
+                    device_id_type=pl.DeviceIdType.MESH,
+                )
+            )
+        return done
+
+    for step in range(len(bits)):
+        for plan in range(len(plans)):
+            if step:
+                for copy in copies(plan, step - 1):
+                    copy.wait_recv()
+            for copy in copies(plan, step):
+                copy.start()
+    for plan in range(len(plans)):
+        for copy in copies(plan, len(bits) - 1):
+            copy.wait_recv()
+    for plan in range(len(plans)):
+        for step in range(len(bits)):
+            for copy in copies(plan, step):
+                copy.wait_send()
+    for copy in local:
+        copy.wait()
+
+
+def gather(shard, gains):
+    peers = lax.axis_size("batch")
+    rows, columns = shard.shape
+    cut = columns // 1024 * 896
+    plans = (
+        (0, slice(0, cut), (3, 2, 1, 0)),
+        (0, slice(cut, columns), (1, 3, 2, 0)),
+        (1, slice(0, gains.shape[1]), (1, 3, 2, 0)),
+    )
+    anywhere = pl.BlockSpec(memory_space=pl.ANY)
     return pl.pallas_call(
-        norm_kernel,
-        name="norm_rows",
-        grid=(tokens // tile,),
-        in_specs=[row, pl.BlockSpec((1, width), lambda i: (0, 0))],
-        out_specs=row,
-        out_shape=jax.ShapeDtypeStruct((tokens, width), bf16),
-    )(x, gain)
+        functools.partial(gather_kernel, plans=plans),
+        name="gather",
+        in_specs=[anywhere, anywhere],
+        out_specs=[anywhere, anywhere],
+        out_shape=[
+            jax.ShapeDtypeStruct((peers, rows, columns), bf16),
+            jax.ShapeDtypeStruct((peers, *gains.shape), bf16),
+        ],
+        scratch_shapes=[
+            pltpu.SemaphoreType.DMA((2,)),
+            pltpu.SemaphoreType.DMA((len(plans), peers - 1)),
+            pltpu.SemaphoreType.DMA((len(plans), peers - 1)),
+        ],
+        compiler_params=pltpu.CompilerParams(collective_id=0, has_side_effects=True),
+        cost_estimate=pl.CostEstimate(flops=0, bytes_accessed=8 * peers * rows * columns, transcendentals=0),
+    )(shard, gains)
 
 
 def shards(tokens, cotangent, lengths, ln1_gain, w_qkv, w_out, ln2_gain, w_up, w_down):
     side = lax.axis_index("stream")
+    at = lax.axis_index("batch")
     _, rows_dev, length, width = tokens.shape
     assert rows_dev == 2
-    swap = [(0, 1), (1, 0)]
-
-    def pair_up(field):
-        own = jnp.take(field[0], side, axis=0)
-        away = lax.ppermute(jnp.take(field[0], 1 - side, axis=0), "stream", swap)
-        return jnp.concatenate([own, away], axis=0)
-
-    def hand_back(field):
-        own, away = field[:length], lax.ppermute(field[length:], "stream", swap)
-        first = side == 0
-        return jnp.stack([jnp.where(first, own, away), jnp.where(first, away, own)])[None]
-
-    w_qkv_all = lax.all_gather(w_qkv, "batch", axis=0, tiled=True)
-    gain_one = lax.all_gather(ln1_gain, "batch", axis=0, tiled=True)[None]
-    gain_two = lax.all_gather(ln2_gain, "batch", axis=0, tiled=True)[None]
-    w_out_all = lax.all_gather(w_out, "batch", axis=0, tiled=True)
-    w_up_all = lax.all_gather(w_up, "batch", axis=0, tiled=True)
-    w_down_all = lax.all_gather(w_down, "batch", axis=0, tiled=True)
-
-    x = pair_up(tokens)
-    grad = pair_up(cotangent)
+    ff = w_up.shape[1]
+    peers = lax.axis_size("batch")
+    small = peers == 16 and width % (16 * peers) == 0
+    side_array = side.reshape(1).astype(jnp.int32)
+    index = side * peers + at
+    me = jnp.stack([index if small else 0 * index, side]).astype(jnp.int32)
+    share = width // (2 * peers)
+
+    x_away = flip(lax.dynamic_index_in_dim(tokens[0], 1 - side, 0, False), -1)
+    g_away = flip(lax.dynamic_index_in_dim(cotangent[0], 1 - side, 0, False), -1)
+    if small:
+        rows = width // peers
+        gains = jnp.zeros((16, LANES), bf16)
+        gains = gains.at[0, :rows].set(ln1_gain).at[1, :rows].set(ln2_gain)
+        w_qkv_all, gains = gather(w_qkv, gains)
+        w_qkv_all = w_qkv_all.reshape(width, 3 * width)
+        gain_one, gain_two = (gains[:, n, :rows].reshape(1, width) for n in range(2))
+        down = w_down.reshape(-1, rows, width).swapaxes(0, 1).reshape(rows, ff)
+        rest = lax.all_gather(jnp.concatenate([w_out, w_up, down], axis=1), "batch", axis=0, tiled=True)
+        rest = rest.reshape(peers, rows, -1)
+    else:
+        def whole(x):
+            return lax.all_gather(x, "batch", axis=0, tiled=True)
+
+        w_qkv_all = whole(w_qkv)
+        gain_one, gain_two = whole(ln1_gain)[None], whole(ln2_gain)[None]
+        down = whole(w_down).reshape(16, -1, width // 16, width).swapaxes(1, 2).reshape(width, ff)
+        rest = jnp.concatenate([whole(w_out), whole(w_up), down], axis=1).reshape(16, width // 16, -1)
+
     cosine, sine = rotary_tables(length)
     tables = mask_tables(length, jnp.take(lengths, side))
-    side_array = side.reshape(1).astype(jnp.int32)
-
-    qkv = project(x, gain_one, w_qkv_all, cosine, sine)
+    qkv, hidden = project(side_array, tokens, x_away, gain_one, w_qkv_all, cosine, sine)
     qkv4 = qkv.reshape(3, 2, length, width)
     mixed, logs = attend(side_array, qkv4, tables)
     mixed2 = mixed.reshape(2 * length, width)
-    out, act, du, h2, dmid, dbr, dmix, dgain_two = feed(
-        x, mixed2, grad, gain_two, w_out_all, w_up_all, w_down_all, tile=512
+    out, out_away, act, du, h2, dmid, dbr, dmix, dgain_two = feed(
+        side_array, tokens, x_away, mixed2, cotangent, g_away, gain_two, rest
     )
-    dw_down = weight_grad(act, grad, 768, 768, "grad_down")
-    dw_up = weight_grad(h2, du, 768, 768, "grad_up")
-    dw_out = weight_grad(mixed2, dbr, 768, 768, "grad_out")
-    dqkv = attend_back(side_array, qkv4, mixed, dmix.reshape(2, length, width), logs, tables, cosine, sine)
-    hidden = norm_rows(x, gain_one)
+
+    def place(result, away):
+        away = flip(away, -1).astype(result.dtype)
+        return lax.dynamic_update_slice(result, away[None, None], (0, 1 - side, 0, 0))
+
+    out = place(out, out_away)
+    cols_share = share if small else width // 32
+    down = weight_grad_rows(me, act, cotangent, g_away, width, ff // width * cols_share, "grad_down")
+    down = weight_grad_rows(me, act, cotangent, g_away, width, ff // width * cols_share, "grad_down")
+    if small:
+        down = SlabSum(down, (-1, 1, 2, 3))
+        h2 = after(h2, down.keep)
+    up = weight_grad_columns(me, h2, du[None], 0, width, cols_share, "grad_up")
+    if small:
+        up = SlabSum(up, (1, -1, 2, 3))
+        dbr = after(dbr, up.keep, down.step())
+    wo = weight_grad_columns(me, mixed2, dbr[None], 0, width, cols_share, "grad_out")
+    dgain_two = all_sum(jnp.sum(dgain_two, axis=0, keepdims=True))
+    dqkv = None
+    dmix = dmix.reshape(2, length, width)
+    if small:
+        wo = SlabSum(wo, (2, -1, 1, 3))
+        dmix = after(dmix, wo.keep, up.step())
+    plan = {1: "wo", 2: "down up wo", 3: "down up wo", 4: "down up wo", 5: "down up wo"}
+    for first in range(width // LANES):
+        if small and first in plan:
+            sums = {"down": down, "up": up, "wo": wo}
+            dmix = after(dmix, *[sums[n].step() for n in plan[first].split()])
+        dqkv = attend_back(side_array, dqkv, first, 1, qkv4, mixed, dmix, logs, tables, cosine, sine)
     dqkv3 = dqkv.reshape(3, 2 * length, width)
-    dw_q = [weight_grad(hidden, dqkv3[i], 768, 768, "grad_qkv") for i in range(3)]
-    dx, dgain_one = project_back(x, gain_one, w_qkv_all, dqkv3, dmid)
-
-    both = ("stream", "batch")
-    peers = lax.axis_size("stream") * lax.axis_size("batch")
-    share = width // peers
-    packed = jnp.concatenate(
-        [
-            *dw_q,
-            dw_out,
-            dw_up,
-            dw_down.reshape(peers, -1, share, width).swapaxes(1, 2).reshape(width, -1),
-        ],
-        axis=1,
-    )
-    summed = lax.psum_scatter(packed, both, scatter_dimension=0, tiled=True).astype(f32)
-    pieces = jnp.split(summed, [3 * width, 4 * width, 4 * width + w_up.shape[1]], axis=1)
-    pieces[3] = pieces[3].reshape(share, -1, width).swapaxes(0, 1)
-    gains = lax.psum(jnp.stack([jnp.sum(dgain_one, axis=0), jnp.sum(dgain_two, axis=0)]), both)
-    at = (side * lax.axis_size("batch") + lax.axis_index("batch")) * share
-    gains = lax.dynamic_slice(gains, (0, at), (2, share))
-    return (
-        hand_back(out),
-        hand_back(dx),
-        gains[0],
-        pieces[0].reshape(share, 3 * width),
-        pieces[1].reshape(share, width),
-        gains[1],
-        pieces[2].reshape(share, -1),
-        pieces[3].reshape(-1, width),
-    )
+    dx_away, dgain_away = project_back(side_array, x_away, gain_one, w_qkv_all, dqkv3, dmid, True)
+    later = after(dqkv3, dx_away)
+    parts = []
+    for n in range(3):
+        pair = weight_grad_columns(me, hidden, later, n, width, cols_share, "grad_qkv")
+        parts.append(SlabSum(pair, ((1, 2, -1, 3), (2, 1, -1, 3), (2, -1, 1, 3))[n]) if small else pair)
+        later = after(later, parts[-1].keep if small else pair[0])
+    dx, dgain_own = project_back(side_array, tokens, gain_one, w_qkv_all, later, dmid, False)
+    dgain_one = all_sum(jnp.sum(dgain_own + dgain_away, axis=0, keepdims=True))
+    dx = place(dx, dx_away)
+    if small:
+        wq = jnp.concatenate([part.finish() for part in parts], axis=1)
+        down, up, wo = down.finish(), up.finish(), wo.finish()
+    else:
+
+        def scatter(pair):
+            slots = jnp.stack(pair, axis=1)
+            rows = slots.reshape(-1, slots.shape[-1])
+            return lax.psum_scatter(rows, ("stream", "batch"), scatter_dimension=0, tiled=True).astype(f32)
+
+        down, up, wo, *parts = (scatter(pair) for pair in (down, up, wo, *parts))
+        wq = jnp.concatenate(parts, axis=1)
+    begin = index * share
+    dgain_one, dgain_two = (lax.dynamic_slice(g[0], (begin,), (share,)) for g in (dgain_one, dgain_two))
+    return out, dx, dgain_one, wq, wo, dgain_two, up, down
 
 
 def solution(mesh):

time: 654 us -> 582 us (0.89)
  blocking collectives: 199 us -> 0 us
  Pallas kernels: 276 us -> 379 us
  starting transfers between devices: 5.18 us -> 43 us
  waiting for transfers between devices: 74.8 us -> 93.9 us
  local copies, waits for them, and re-layouts: 44.9 us -> 26.4 us
  other arithmetic: 27.7 us -> 17.6 us
    psum x1 -> x0, blocking collectives: 165 us -> none  [shards(): lax.psum(jnp.stack([jnp.sum(dgain_one, axis=0), jnp.sum(dgain_two, axis=0...]
    pallas_call x11 -> x17, Pallas kernels: 232 us -> 334 us  [the longest x6 102 us: attend_back(): pl.pallas_call(attend_back_next if begun else attend_back_kernel, name='a...]
    ppermute x4 -> x44, waiting for transfers between devices: 14.3 us -> 93.9 us  [flip(): lax.ppermute(x, axis, [(i, i ^ by) for i in range(lax.axis_size(axis))])]
    all_gather x4 -> x1, waiting for transfers between devices: 57.9 us -> 0.01 us  [shards(): lax.all_gather(jnp.concatenate([w_out, w_up, down], axis=1), 'batch', axi...]
    ppermute x4 -> x44, starting transfers between devices: 4.99 us -> 43 us  [flip(): lax.ppermute(x, axis, [(i, i ^ by) for i in range(lax.axis_size(axis))])]
    unnamed x1 -> x0, blocking collectives: 34.1 us -> none
    slice x3 -> x4, local copies, waits for them, and re-layouts: 12.3 us -> 1.13 us  [the longest x1 0.89 us: shards(): gains[:, n, :rows].reshape(1, width)]
    add x0 -> x38, other arithmetic: none -> 9.94 us  [the longest x24 6.33 us: step(): lax.index_in_dim(self.keep, i, at, False)]
  transfers between devices with their start and end apart: 9 -> 45, of which waited for: 3 -> 19; matrix products, arithmetic and copies ran while one was open for 6% -> 5% of each run, Pallas kernels for 13% -> 50%
where the time goes in v2:
time: 582 us; the launch traced here: 575 us
  Pallas kernels  379 us (65%)
  waiting for transfers between devices  93.9 us (16%)
  starting transfers between devices  43 us (7%)
  local copies, waits for them, and re-layouts  26.4 us (5%)
  other arithmetic  17.6 us (3%)
  between operations  15.9 us (3%)
    pallas_call x6, Pallas kernels, attend_back(): pl.pallas_call(attend_back_next if begun else attend_back_kernel, name='a...  102 us
    ppermute x44, waiting for transfers between devices, flip(): lax.ppermute(x, axis, [(i, i ^ by) for i in range(lax.axis_size(axis))])  93.9 us
    pallas_call x1, Pallas kernels, feed(): pl.pallas_call(functools.partial(feed_kernel, half=half), name='feed', gr...  75.5 us
    pallas_call x1, Pallas kernels, gather(): pl.pallas_call(functools.partial(gather_kernel, plans=plans), name='gathe...  72.9 us
    pallas_call x1, Pallas kernels, attend(): pl.pallas_call(attend_kernel, name='attend', grid_spec=pltpu.PrefetchScal...  44.1 us
    ppermute x44, starting transfers between devices, flip(): lax.ppermute(x, axis, [(i, i ^ by) for i in range(lax.axis_size(axis))])  43 us
    pallas_call x5, Pallas kernels, weight_grad_columns(): pl.pallas_call(functools.partial(weight_kernel, share=share, split=False)...  35.8 us
    pallas_call x2, Pallas kernels, project_back(): pl.pallas_call(project_back_kernel, name='project_back_away' if away else...  19.2 us
  transfers between devices with their start and end apart: 45, of which 19 were waited for; matrix products, arithmetic and copies ran while one was open for 5% of the time, Pallas kernels for 50%

profile of v2, /device:TPU:0, one launch (start us, length us, event | category | flops | bytes accessed | tf_op | source)
XLA Modules:
  0.0 575.3 jit_solution(14251678357764826895)
XLA Ops:
  18.5 72.9 %gather.6 = (bf16[16,48,2304]{2,1,0:T(8,128)(2,1)}, bf16[16,16,128]{2,1,0:T(8,128)(2,1)}) custom-call(bf16[48,2304]{1,0:T(8,128)(2,1)} %shard_ref.1, bf16[16,128]{1,0:T(8,128)(2,1)} %copy-done.25), custom_call_target="tpu_custom_call" | custom-call | bytes 14155776 | tf_op jit(solution)/shard_map/gather/pallas_call | solution.py:707
  97.4 14.1 %project.1 = (bf16[3,2048,768]{2,1,0:T(8,128)(2,1)}, bf16[2048,768]{1,0:T(8,128)(2,1)S(1)}) custom-call(s32[1]{0:T(128)} %bitcast.side_ref, bf16[1,2,1024,768]{3,2,1,0:T(8,128)(2,1)} %x_ref.1, bf16[1024,768]{1,0:T(8,128)(2,1)} %collective-permute-done.away_ref.x_away.x_ref, bf16[1,768]{1,0:T(2,128)(2,1)S(1)} %reshape_squeeze.6.gain_ref, ...), custom_call_target="tpu_custom_call" | custom-call | flops 7247757312 | bytes 19267584 | tf_op jit(solution)/shard_map/project/pallas_call | solution.py:83
  113.1 44.1 %attend.1 = (bf16[2,1024,768]{2,1,0:T(8,128)(2,1)S(1)}, f32[2,6,2,1024]{3,2,1,0:T(2,128)S(1)}) custom-call(s32[1]{0:T(128)} %bitcast.side_ref, bf16[3,2,1024,768]{3,2,1,0:T(8,128)(2,1)} %bitcast.267, bf16[1024,128]{1,0:T(8,128)(2,1)S(1)} %get-tuple-element.179.cq_ref.refs_4_, bf16[1024,128]{1,0:T(8,128)(2,1)S(1)} %get-tuple-element.178.nq_ref.refs_5_, ...), custom_call_target="tpu_custom_call" | custom-call | flops 6442450944 | bytes 12582912 | tf_op jit(solution)/shard_map/attend/pallas_call | solution.py:179
  160.1 75.5 %feed.1 = (bf16[1,2,1024,768]{3,2,1,0:T(8,128)(2,1)}, bf16[1024,768]{1,0:T(8,128)(2,1)}, bf16[2048,3072]{1,0:T(8,128)(2,1)}, bf16[2048,3072]{1,0:T(8,128)(2,1)},...) custom-call(s32[1]{0:T(128)} %bitcast.side_ref, ...), custom_call_target="tpu_custom_call" | custom-call | flops 43486543872 | bytes 53477376 | tf_op jit(solution)/shard_map/feed/pallas_call | solution.py:432
  237.0 14.8 %grad_down.1 = (bf16[16,96,768]{2,1,0:T(8,128)(2,1)S(1)}, bf16[16,96,768]{2,1,0:T(8,128)(2,1)}) custom-call(s32[2]{0:T(128)S(1)} %pad_add_fusion.me_ref, bf16[2048,3072]{1,0:T(8,128)(2,1)} %get-tuple-element.83.left_ref, bf16[1,2,1024,768]{3,2,1,0:T(8,128)(2,1)} %refs_0_.1, bf16[1024,768]{1,0:T(8,128)(2,1)S(1)} %copy-done.20), custom_call_target="tpu_custom_call" | custom-call | flops 9663676416 | bytes 20447232 | tf_op jit(solution)/shard_map/grad_down/pallas_call | solution.py:521
  254.1 14.8 %grad_up.1 = (bf16[16,24,3072]{2,1,0:T(8,128)(2,1)S(1)}, bf16[16,24,3072]{2,1,0:T(8,128)(2,1)S(1)}) custom-call(s32[2]{0:T(128)S(1)} %pad_add_fusion.me_ref, bf16[2048,768]{1,0:T(8,128)(2,1)} %get-tuple-element.80.left_ref, bf16[1,2048,3072]{2,1,0:T(8,128)(2,1)} %bitcast.293), custom_call_target="tpu_custom_call" | custom-call | flops 9663676416 | bytes 20447232 | tf_op jit(solution)/shard_map/grad_up/pallas_call | solution.py:489
  274.1 5.2 grad_out.1
  300.8 17.1 %attend_back.6._ = bf16[3,2,1024,768]{3,2,1,0:T(8,128)(2,1)} custom-call(s32[1]{0:T(128)} %bitcast.side_ref, bf16[3,2,1024,768]{3,2,1,0:T(8,128)(2,1)} %bitcast.268, bf16[2,1024,768]{2,1,0:T(8,128)(2,1)S(1)} %copy-done.1, bf16[2,1024,768]{2,1,0:T(8,128)(2,1)} %bitcast.274, f32[2,6,2,1024]{3,2,1,0:T(2,128)S(1)} %get-tuple-element.89.log_ref.refs_3_, ...), custom_call_target="tpu_custom_call" | custom-call | flops 2684354560 | bytes 4194304 | tf_op jit(solution)/shard_map/attend_back/pallas_call | solution.py:297
  317.9 33.6 %collective-permute-done.13 = bf16[2,2,24,768]{3,2,1,0:T(8,128)(2,1)S(1)} collective-permute-done((bf16[2,2,24,768]{3,2,1,0:T(8,128)(2,1)S(1)}, bf16[2,2,24,768]{3,2,1,0:T(8,128)(2,1)S(1)}, u32[]{:S(2)}, u32[]{:S(2)}) %collective-permute-start.13) | collective-permute-done | bytes 147488 | tf_op jit(solution)/shard_map/ppermute | solution.py:601
  353.2 16.9 %attend_back.7._ = bf16[3,2,1024,768]{3,2,1,0:T(8,128)(2,1)} custom-call(s32[1]{0:T(128)} %bitcast.side_ref, bf16[3,2,1024,768]{3,2,1,0:T(8,128)(2,1)} %attend_back.6._, bf16[3,2,1024,768]{3,2,1,0:T(8,128)(2,1)} %bitcast.269, bf16[2,1024,768]{2,1,0:T(8,128)(2,1)S(1)} %copy-done.1, bf16[2,1024,768]{2,1,0:T(8,128)(2,1)} %bitcast.275, ...), custom_call_target="tpu_custom_call", output_to_operand_aliasing={{}: (1, {})} | custom-call | flops 2684354560 | bytes 4194304 | tf_op jit(solution)/shard_map/attend_back/pallas_call | solution.py:297
  376.6 16.9 %attend_back.8._ = bf16[3,2,1024,768]{3,2,1,0:T(8,128)(2,1)} custom-call(s32[1]{0:T(128)} %bitcast.side_ref, bf16[3,2,1024,768]{3,2,1,0:T(8,128)(2,1)} %attend_back.7._, bf16[3,2,1024,768]{3,2,1,0:T(8,128)(2,1)} %bitcast.270, bf16[2,1024,768]{2,1,0:T(8,128)(2,1)S(1)} %copy-done.1, bf16[2,1024,768]{2,1,0:T(8,128)(2,1)} %bitcast.276, ...), custom_call_target="tpu_custom_call", output_to_operand_aliasing={{}: (1, {})} | custom-call | flops 2684354560 | bytes 4194304 | tf_op jit(solution)/shard_map/attend_back/pallas_call | solution.py:297
  393.8 17.2 %attend_back.9._ = bf16[3,2,1024,768]{3,2,1,0:T(8,128)(2,1)} custom-call(s32[1]{0:T(128)} %bitcast.side_ref, bf16[3,2,1024,768]{3,2,1,0:T(8,128)(2,1)} %attend_back.8._, bf16[3,2,1024,768]{3,2,1,0:T(8,128)(2,1)} %bitcast.271, bf16[2,1024,768]{2,1,0:T(8,128)(2,1)S(1)} %copy-done.1, bf16[2,1024,768]{2,1,0:T(8,128)(2,1)} %bitcast.277, ...), custom_call_target="tpu_custom_call", output_to_operand_aliasing={{}: (1, {})} | custom-call | flops 2684354560 | bytes 4194304 | tf_op jit(solution)/shard_map/attend_back/pallas_call | solution.py:297
  414.2 7.0 %collective-permute-done.10 = bf16[2,96,768]{2,1,0:T(8,128)(2,1)S(1)} collective-permute-done((bf16[2,96,768]{2,1,0:T(8,128)(2,1)S(1)}, bf16[2,96,768]{2,1,0:T(8,128)(2,1)S(1)}, u32[]{:S(2)}, u32[]{:S(2)}) %collective-permute-start.10) | collective-permute-done | bytes 294944 | tf_op jit(solution)/shard_map/ppermute | solution.py:601
  424.0 4.7 collective-permute-done.15
  429.5 17.0 %attend_back.10._ = bf16[3,2,1024,768]{3,2,1,0:T(8,128)(2,1)} custom-call(s32[1]{0:T(128)} %bitcast.side_ref, bf16[3,2,1024,768]{3,2,1,0:T(8,128)(2,1)} %attend_back.9._, bf16[3,2,1024,768]{3,2,1,0:T(8,128)(2,1)} %bitcast.272, bf16[2,1024,768]{2,1,0:T(8,128)(2,1)S(1)} %copy-done.1, bf16[2,1024,768]{2,1,0:T(8,128)(2,1)} %bitcast.278, ...), custom_call_target="tpu_custom_call", output_to_operand_aliasing={{}: (1, {})} | custom-call | flops 2684354560 | bytes 4194304 | tf_op jit(solution)/shard_map/attend_back/pallas_call | solution.py:297
  446.5 16.9 %attend_back.11 = bf16[3,2,1024,768]{3,2,1,0:T(8,128)(2,1)} custom-call(s32[1]{0:T(128)} %bitcast.side_ref, bf16[3,2,1024,768]{3,2,1,0:T(8,128)(2,1)} %attend_back.10._, bf16[3,2,1024,768]{3,2,1,0:T(8,128)(2,1)} %bitcast.273, bf16[2,1024,768]{2,1,0:T(8,128)(2,1)S(1)} %copy-done.1, bf16[2,1024,768]{2,1,0:T(8,128)(2,1)} %bitcast.279, ...), custom_call_target="tpu_custom_call", output_to_operand_aliasing={{}: (1, {})} | custom-call | flops 2684354560 | bytes 4194304 | tf_op jit(solution)/shard_map/attend_back/pallas_call | solution.py:297
  463.4 9.4 %project_back_away.1 = (bf16[1024,768]{1,0:T(8,128)(2,1)S(1)}, f32[8,768]{1,0:T(8,128)S(1)}) custom-call(s32[1]{0:T(128)} %bitcast.side_ref, bf16[1024,768]{1,0:T(8,128)(2,1)} %collective-permute-done.away_ref.x_away.x_ref, bf16[1,768]{1,0:T(2,128)(2,1)S(1)} %reshape_squeeze.6.gain_ref, bf16[768,2304]{1,0:T(8,128)(2,1)} %bitcast.281, ...), custom_call_target="tpu_custom_call" | custom-call | flops 3623878656 | bytes 12582912 | tf_op jit(solution)/shard_map/project_back_away/pallas_call | solution.py:576
  472.8 5.2 grad_qkv.3
  478.0 5.2 grad_qkv.4
  483.2 5.5 grad_qkv.5
  488.7 9.8 %project_back_own.1 = (f32[1,2,1024,768]{3,2,1,0:T(8,128)}, f32[8,768]{1,0:T(8,128)S(1)}) custom-call(s32[1]{0:T(128)} %bitcast.side_ref, bf16[1,2,1024,768]{3,2,1,0:T(8,128)(2,1)S(1)} %copy-done.14, bf16[1,768]{1,0:T(2,128)(2,1)S(1)} %reshape_squeeze.6.gain_ref, bf16[768,2304]{1,0:T(8,128)(2,1)} %bitcast.282, bf16[3,2048,768]{2,1,0:T(8,128)(2,1)} %bitcast.266, ...), custom_call_target="tpu_custom_call" | custom-call | flops 3623878656 | bytes 12582912 | tf_op jit(solution)/shard_map/project_back_own/pallas_call | solution.py:576
  521.9 3.9 collective-permute-done.25
  530.9 3.7 collective-permute-done.35
  538.4 16.2 %collective-permute-done.36 = bf16[2,2,24,768]{3,2,1,0:T(8,128)(2,1)S(1)} collective-permute-done((bf16[2,2,24,768]{3,2,1,0:T(8,128)(2,1)S(1)}, bf16[2,2,24,768]{3,2,1,0:T(8,128)(2,1)S(1)}, u32[]{:S(2)}, u32[]{:S(2)}) %collective-permute-start.36) | collective-permute-done | bytes 147488 | tf_op jit(solution)/shard_map/ppermute | solution.py:601
  (226 shorter events, 111.9 us)
Async XLA Ops:
  7.2 151.8 %all-gather.2.cloned.1.call-start = ((), (), s32[]{:S(2)}) async-start(), calls=%async_computation | async-start | bytes 11280384 | tf_op jit(solution)/shard_map/all_gather | solution.py:749
  12.9 84.5 %collective-permute-start = (bf16[1024,768]{1,0:T(8,128)(2,1)}, bf16[1024,768]{1,0:T(8,128)(2,1)}, u32[]{:S(2)}, u32[]{:S(2)}) collective-permute-start(bf16[1024,768]{1,0:T(8,128)(2,1)} %dynamic-slice_bitcast_fusion.1), channel_id=1, source_target_pairs={{0,16},{16,0},{1,17},{17,1},{2,18},{18,2},{3,19},{19,3},{4,20},{20... | collective-permute-start | bytes 4718600 | tf_op jit(solution)/shard_map/ppermute | solution.py:601
  17.1 141.8 %collective-permute-start.1 = (bf16[1024,768]{1,0:T(8,128)(2,1)}, bf16[1024,768]{1,0:T(8,128)(2,1)S(1)}, u32[]{:S(2)}, u32[]{:S(2)}) collective-permute-start(bf16[1024,768]{1,0:T(8,128)(2,1)} %dynamic-slice_bitcast_fusion), channel_id=1, source_target_pairs={{0,16},{16,0},{1,17},{17,1},{2,18},{18,2},{3,19},{19,3},{4,20},{20... | collective-permute-start | bytes 4718600 | tf_op jit(solution)/shard_map/ppermute | solution.py:601
  253.6 17.8 %collective-permute-start.3 = (bf16[2,2,2,2,96,768]{5,4,2,1,3,0:T(8,128)(2,1)S(1)}, bf16[2,2,2,2,96,768]{5,4,2,1,3,0:T(8,128)(2,1)S(1)}, u32[]{:S(2)}, u32[]{:S(2)}) collective-permute-start(bf16[2,2,2,2,96,768]{5,4,2,1,3,0:T(8,128)(2,1)S(1)} %copy.62), channel_id=1, source_target_pairs={{0,1},{1,0},{2,3},{3,2},{4,5},{5,4},{6,7},{7,6},{8,9},{9,8},{10,11... | collective-permute-start | bytes 7077896 | tf_op jit(solution)/shard_map/ppermute | solution.py:601
  271.1 22.2 %collective-permute-start.5 = (bf16[2,2,2,2,24,3072]{5,4,2,1,3,0:T(8,128)(2,1)}, bf16[2,2,2,2,24,3072]{5,4,2,1,3,0:T(8,128)(2,1)}, u32[]{:S(2)}, u32[]{:S(2)}) collective-permute-start(bf16[2,2,2,2,24,3072]{5,4,2,1,3,0:T(8,128)(2,1)} %copy.66), channel_id=1, source_target_pairs={{0,1},{1,0},{2,3},{3,2},{4,5},{5,4},{6,7},{7,6},{8,9},{9,8},{10,11... | collective-permute-start | bytes 7077896 | tf_op jit(solution)/shard_map/ppermute | solution.py:601
  286.3 220.7 %collective-permute-start.2 = (bf16[1024,768]{1,0:T(8,128)(2,1)}, bf16[1024,768]{1,0:T(8,128)(2,1)}, u32[]{:S(2)}, u32[]{:S(2)}) collective-permute-start(bf16[1024,768]{1,0:T(8,128)(2,1)} %get-tuple-element.77), channel_id=1, source_target_pairs={{0,16},{16,0},{1,17},{17,1},{2,18},{18,2},{3,19},{19,3},{4,20},{20... | collective-permute-start | bytes 4718600 | tf_op jit(solution)/shard_map/ppermute | solution.py:601
  289.9 210.1 %collective-permute-start.42 = (f32[1,768]{1,0:T(1,128)S(1)}, f32[1,768]{1,0:T(1,128)}, u32[]{:S(2)}, u32[]{:S(2)}) collective-permute-start(f32[1,768]{1,0:T(1,128)S(1)} %add.483), channel_id=1, source_target_pairs={{0,4},{1,5},{2,6},{3,7},{4,0},{5,1},{6,2},{7,3},{8,12},{9,13},{10,... | collective-permute-start | bytes 9224 | tf_op jit(solution)/shard_map/ppermute | solution.py:601
  295.9 74.3 %collective-permute-start.6 = (bf16[2,2,2,24,3072]{4,3,2,1,0:T(8,128)(2,1)S(1)}, bf16[2,2,2,24,3072]{4,3,2,1,0:T(8,128)(2,1)S(1)}, u32[]{:S(2)}, u32[]{:S(2)}) collective-permute-start(bf16[2,2,2,24,3072]{4,3,2,1,0:T(8,128)(2,1)S(1)} %get-tuple-element.132), channel_id=1, source_target_pairs={{0,2},{1,3},{2,0},{3,1},{4,6},{5,7},{6,4},{7,5},{8,10},{9,11},{10,... | collective-permute-start | bytes 3538952 | tf_op jit(solution)/shard_map/ppermute | solution.py:601
  296.0 79.7 %collective-permute-start.4 = (bf16[2,2,2,96,768]{4,3,1,0,2:T(8,128)(2,1)S(1)}, bf16[2,2,2,96,768]{4,3,1,0,2:T(8,128)(2,1)S(1)}, u32[]{:S(2)}, u32[]{:S(2)}) collective-permute-start(bf16[2,2,2,96,768]{4,3,1,0,2:T(8,128)(2,1)S(1)} %copy-done.22), channel_id=1, source_target_pairs={{0,16},{16,0},{1,17},{17,1},{2,18},{18,2},{3,19},{19,3},{4,20},{20... | collective-permute-start | bytes 3538952 | tf_op jit(solution)/shard_map/ppermute | solution.py:601
  299.3 52.1 %collective-permute-start.13 = (bf16[2,2,24,768]{3,2,1,0:T(8,128)(2,1)S(1)}, bf16[2,2,24,768]{3,2,1,0:T(8,128)(2,1)S(1)}, u32[]{:S(2)}, u32[]{:S(2)}) collective-permute-start(bf16[2,2,24,768]{3,2,1,0:T(8,128)(2,1)S(1)} %get-tuple-element.163), channel_id=1, source_target_pairs={{0,16},{16,0},{1,17},{17,1},{2,18},{18,2},{3,19},{19,3},{4,20},{20... | collective-permute-start | bytes 442376 | tf_op jit(solution)/shard_map/ppermute | solution.py:601
  351.5 18.6 %collective-permute-start.14 = (bf16[2,24,768]{2,1,0:T(8,128)(2,1)S(1)}, bf16[2,24,768]{2,1,0:T(8,128)(2,1)S(1)}, u32[]{:S(2)}, u32[]{:S(2)}) collective-permute-start(bf16[2,24,768]{2,1,0:T(8,128)(2,1)S(1)} %get-tuple-element.172), channel_id=1, source_target_pairs={{0,2},{1,3},{2,0},{3,1},{4,6},{5,7},{6,4},{7,5},{8,10},{9,11},{10,... | collective-permute-start | bytes 221192 | tf_op jit(solution)/shard_map/ppermute | solution.py:601
  370.4 23.2 %collective-permute-start.11 = (bf16[2,2,24,3072]{3,2,1,0:T(8,128)(2,1)S(1)}, bf16[2,2,24,3072]{3,2,1,0:T(8,128)(2,1)S(1)}, u32[]{:S(2)}, u32[]{:S(2)}) collective-permute-start(bf16[2,2,24,3072]{3,2,1,0:T(8,128)(2,1)S(1)} %get-tuple-element.133), channel_id=1, source_target_pairs={{0,16},{16,0},{1,17},{17,1},{2,18},{18,2},{3,19},{19,3},{4,20},{20... | collective-permute-start | bytes 1769480 | tf_op jit(solution)/shard_map/ppermute | solution.py:601
  375.8 35.2 %collective-permute-start.9 = (bf16[2,2,96,768]{3,2,1,0:T(8,128)(2,1)S(1)}, bf16[2,2,96,768]{3,2,1,0:T(8,128)(2,1)S(1)}, u32[]{:S(2)}, u32[]{:S(2)}) collective-permute-start(bf16[2,2,96,768]{3,2,1,0:T(8,128)(2,1)S(1)} %get-tuple-element.135), channel_id=1, source_target_pairs={{0,2},{1,3},{2,0},{3,1},{4,6},{5,7},{6,4},{7,5},{8,10},{9,11},{10,... | collective-permute-start | bytes 1769480 | tf_op jit(solution)/shard_map/ppermute | solution.py:601
  393.6 19.4 %collective-permute-start.12 = (bf16[2,24,3072]{2,1,0:T(8,128)(2,1)S(1)}, bf16[2,24,3072]{2,1,0:T(8,128)(2,1)S(1)}, u32[]{:S(2)}, u32[]{:S(2)}) collective-permute-start(bf16[2,24,3072]{2,1,0:T(8,128)(2,1)S(1)} %get-tuple-element.144), channel_id=1, source_target_pairs={{0,4},{1,5},{2,6},{3,7},{4,0},{5,1},{6,2},{7,3},{8,12},{9,13},{10,... | collective-permute-start | bytes 884744 | tf_op jit(solution)/shard_map/ppermute | solution.py:601
  411.1 10.0 %collective-permute-start.10 = (bf16[2,96,768]{2,1,0:T(8,128)(2,1)S(1)}, bf16[2,96,768]{2,1,0:T(8,128)(2,1)S(1)}, u32[]{:S(2)}, u32[]{:S(2)}) collective-permute-start(bf16[2,96,768]{2,1,0:T(8,128)(2,1)S(1)} %get-tuple-element.146), channel_id=1, source_target_pairs={{0,4},{1,5},{2,6},{3,7},{4,0},{5,1},{6,2},{7,3},{8,12},{9,13},{10,... | collective-permute-start | bytes 884744 | tf_op jit(solution)/shard_map/ppermute | solution.py:601
  413.0 10.2 %collective-permute-start.16 = (bf16[24,3072]{1,0:T(8,128)(2,1)S(1)}, bf16[24,3072]{1,0:T(8,128)(2,1)S(1)}, u32[]{:S(2)}, u32[]{:S(2)}) collective-permute-start(bf16[24,3072]{1,0:T(8,128)(2,1)S(1)} %fusion.20), channel_id=1, source_target_pairs={{0,8},{1,9},{2,10},{3,11},{4,12},{5,13},{6,14},{7,15},{8,0},{9,1},... | collective-permute-start | bytes 442376 | tf_op jit(solution)/shard_map/ppermute | solution.py:601
  510.0 9.6 %collective-permute-start.29 = (bf16[2,2,2,2,24,768]{5,4,1,3,0,2:T(8,128)(2,1)S(1)}, bf16[2,2,2,2,24,768]{5,4,1,3,0,2:T(8,128)(2,1)S(1)}, u32[]{:S(2)}, u32[]{:S(2)}) collective-permute-start(bf16[2,2,2,2,24,768]{5,4,1,3,0,2:T(8,128)(2,1)S(1)} %copy.75), channel_id=1, source_target_pairs={{0,1},{1,0},{2,3},{3,2},{4,5},{5,4},{6,7},{7,6},{8,9},{9,8},{10,11... | collective-permute-start | bytes 1769480 | tf_op jit(solution)/shard_map/ppermute | solution.py:601
  514.5 50.5 %collective-permute-start.18 = (bf16[1024,768]{1,0:T(8,128)(2,1)S(1)}, bf16[1024,768]{1,0:T(8,128)(2,1)S(1)}, u32[]{:S(2)}, u32[]{:S(2)}) collective-permute-start(bf16[1024,768]{1,0:T(8,128)(2,1)S(1)} %copy-done.18), channel_id=1, source_target_pairs={{0,16},{16,0},{1,17},{17,1},{2,18},{18,2},{3,19},{19,3},{4,20},{20... | collective-permute-start | bytes 4718600 | tf_op jit(solution)/shard_map/ppermute | solution.py:601
  519.6 10.0 %collective-permute-start.30 = (bf16[2,2,2,24,768]{4,3,1,2,0:T(8,128)(2,1)S(1)}, bf16[2,2,2,24,768]{4,3,1,2,0:T(8,128)(2,1)S(1)}, u32[]{:S(2)}, u32[]{:S(2)}) collective-permute-start(bf16[2,2,2,24,768]{4,3,1,2,0:T(8,128)(2,1)S(1)} %get-tuple-element.158), channel_id=1, source_target_pairs={{0,4},{1,5},{2,6},{3,7},{4,0},{5,1},{6,2},{7,3},{8,12},{9,13},{10,... | collective-permute-start | bytes 884744 | tf_op jit(solution)/shard_map/ppermute | solution.py:601
  520.2 14.4 %collective-permute-start.35 = (bf16[2,2,2,24,768]{4,3,2,1,0:T(8,128)(2,1)S(1)}, bf16[2,2,2,24,768]{4,3,2,1,0:T(8,128)(2,1)S(1)}, u32[]{:S(2)}, u32[]{:S(2)}) collective-permute-start(bf16[2,2,2,24,768]{4,3,2,1,0:T(8,128)(2,1)S(1)} %get-tuple-element.142), channel_id=1, source_target_pairs={{0,4},{1,5},{2,6},{3,7},{4,0},{5,1},{6,2},{7,3},{8,12},{9,13},{10,... | collective-permute-start | bytes 884744 | tf_op jit(solution)/shard_map/ppermute | solution.py:601
  525.8 10.4 %collective-permute-start.26 = (bf16[2,2,24,768]{3,2,1,0:T(8,128)(2,1)S(1)}, bf16[2,2,24,768]{3,2,1,0:T(8,128)(2,1)S(1)}, u32[]{:S(2)}, u32[]{:S(2)}) collective-permute-start(bf16[2,2,24,768]{3,2,1,0:T(8,128)(2,1)S(1)} %get-tuple-element.150), channel_id=1, source_target_pairs={{0,4},{1,5},{2,6},{3,7},{4,0},{5,1},{6,2},{7,3},{8,12},{9,13},{10,... | collective-permute-start | bytes 442376 | tf_op jit(solution)/shard_map/ppermute | solution.py:601
  534.6 20.0 %collective-permute-start.36 = (bf16[2,2,24,768]{3,2,1,0:T(8,128)(2,1)S(1)}, bf16[2,2,24,768]{3,2,1,0:T(8,128)(2,1)S(1)}, u32[]{:S(2)}, u32[]{:S(2)}) collective-permute-start(bf16[2,2,24,768]{3,2,1,0:T(8,128)(2,1)S(1)} %get-tuple-element.162), channel_id=1, source_target_pairs={{0,16},{16,0},{1,17},{17,1},{2,18},{18,2},{3,19},{19,3},{4,20},{20... | collective-permute-start | bytes 442376 | tf_op jit(solution)/shard_map/ppermute | solution.py:601
  536.2 20.0 %collective-permute-start.27 = (bf16[2,24,768]{2,1,0:T(8,128)(2,1)S(1)}, bf16[2,24,768]{2,1,0:T(8,128)(2,1)S(1)}, u32[]{:S(2)}, u32[]{:S(2)}) collective-permute-start(bf16[2,24,768]{2,1,0:T(8,128)(2,1)S(1)} %get-tuple-element.166), channel_id=1, source_target_pairs={{0,16},{16,0},{1,17},{17,1},{2,18},{18,2},{3,19},{19,3},{4,20},{20... | collective-permute-start | bytes 221192 | tf_op jit(solution)/shard_map/ppermute | solution.py:601
  537.8 19.9 %collective-permute-start.32 = (bf16[2,24,768]{2,1,0:T(8,128)(2,1)S(1)}, bf16[2,24,768]{2,1,0:T(8,128)(2,1)S(1)}, u32[]{:S(2)}, u32[]{:S(2)}) collective-permute-start(bf16[2,24,768]{2,1,0:T(8,128)(2,1)S(1)} %get-tuple-element.168), channel_id=1, source_target_pairs={{0,16},{16,0},{1,17},{17,1},{2,18},{18,2},{3,19},{19,3},{4,20},{20... | collective-permute-start | bytes 221192 | tf_op jit(solution)/shard_map/ppermute | solution.py:601
  (53 other events, 414.9 us)
Sparse Core Ops, SparseCore 0:
  10.3 109.5 all-gather.1

commit v3 on v2

--- a/solution.py
+++ b/solution.py
@@ -206,14 +206,167 @@
     )(side, qkv, *tables)
 
 
-def attend_back_next(side_ref, _, *refs):
-    attend_back_kernel(side_ref, *refs)
-
-
-def attend_back_kernel(side_ref, qkv_ref, o_ref, do_ref, log_ref, cq_ref, nq_ref, mk_ref, dk_ref, cos_ref, sin_ref,
+MESH = pl.DeviceIdType.MESH
+
+
+def partner(bit):
+    side, at = lax.axis_index("stream"), lax.axis_index("batch")
+    return (1 - side, at) if bit < 0 else (side, jnp.bitwise_xor(at, 1 << bit))
+
+
+def greet(bits):
+    barrier = pltpu.get_barrier_semaphore()
+    for bit in bits:
+        pl.semaphore_signal(barrier, inc=1, device_id=partner(bit), device_id_type=MESH)
+    pl.semaphore_wait(barrier, len(bits))
+
+
+class SlabSum:
+    def __init__(self, order, keep, send, got, sems, load=None):
+        self.order, self.keep, self.send, self.got, self.sems, self.load = (0, *order), keep, send, got, sems, load
+
+    @staticmethod
+    def scratch(slots, share, columns):
+        steps = slots.bit_length()
+        return [
+            *[pltpu.VMEM((max(slots >> n, 1), share, columns), bf16) for n in (0, *range(steps))],
+            pltpu.SemaphoreType.DMA((2 * steps + 1,)),
+        ]
+
+    def copy(self, step):
+        count = self.got[step].shape[0]
+        return pltpu.make_async_remote_copy(
+            src_ref=self.send if step == 0 else self.keep.at[pl.ds(count, count)],
+            dst_ref=self.got[step],
+            send_sem=self.sems.at[2 * step],
+            recv_sem=self.sems.at[2 * step + 1],
+            device_id=partner(self.order[step]),
+            device_id_type=MESH,
+        )
+
+    def loading(self):
+        return pltpu.make_async_copy(self.load, self.keep, self.sems.at[2 * len(self.order)])
+
+    def start(self):
+        self.copy(0).start()
+        if self.load is not None:
+            self.loading().start()
+
+    def step(self, step):
+        if step == 1 and self.load is not None:
+            self.loading().wait()
+        self.copy(step - 1).wait_recv()
+        got = self.got[step - 1]
+
+        @pl.loop(0, got.shape[0])
+        def _(n):
+            self.keep[n] = (self.keep[n].astype(f32) + got[n].astype(f32)).astype(bf16)
+
+        self.copy(step).start()
+
+    def finish(self, out_ref, columns=slice(None)):
+        last = len(self.order) - 1
+        self.copy(last).wait_recv()
+        out_ref[:, columns] = self.keep[0].astype(f32) + self.got[last][0].astype(f32)
+        for step in range(len(self.order)):
+            self.copy(step).wait_send()
+
+
+class GainSum:
+    bits = (-1, 0, 1, 2, 3)
+
+    def __init__(self, held, got, sems):
+        self.held, self.got, self.sems = held, got, sems
+
+    @staticmethod
+    def scratch(width):
+        steps = len(GainSum.bits)
+        return [
+            pltpu.VMEM((steps, 8, width), f32),
+            pltpu.VMEM((steps, 8, width), f32),
+            pltpu.SemaphoreType.DMA((2 * steps,)),
+        ]
+
+    def copy(self, step):
+        return pltpu.make_async_remote_copy(
+            src_ref=self.held.at[step],
+            dst_ref=self.got.at[step],
+            send_sem=self.sems.at[2 * step],
+            recv_sem=self.sems.at[2 * step + 1],
+            device_id=partner(self.bits[step]),
+            device_id_type=MESH,
+        )
+
+    def start(self, value):
+        self.held[0] = value
+        self.copy(0).start()
+
+    def step(self, step):
+        self.copy(step - 1).wait_recv()
+        self.held[step] = self.held[step - 1] + self.got[step - 1]
+        self.copy(step).start()
+
+    def finish(self, out_ref):
+        last = len(self.bits) - 1
+        self.copy(last).wait_recv()
+        out_ref[...] = self.held[last] + self.got[last]
+        for step in range(len(self.bits)):
+            self.copy(step).wait_send()
+
+
+DOWN, UP, OUT = (-1, 1, 2, 3), (1, -1, 2, 3), (2, -1, 1, 3)
+QKV = ((1, 2, 3, -1), (2, 1, 3, -1), (2, 3, 1, -1))
+
+
+def attend_back_sum_kernel(*refs, orders):
+    count = len(orders)
+    core, refs = refs[:10], refs[10:]
+    pairs, gain_ref, refs = refs[: 2 * count], refs[2 * count], refs[2 * count + 1 :]
+    dqkv_ref, refs = refs[0], refs[1:]
+    outs, gain_out, refs = refs[:count], refs[count], refs[count + 1 :]
+    own, refs = refs[:10], refs[10:]
+    per = len(refs[:-3]) // count
+    sums = []
+    for n, order in enumerate(orders):
+        keep, *got, sems = refs[n * per : (n + 1) * per]
+        sums.append(SlabSum(order, keep, pairs[2 * n + 1], got, sems, load=pairs[2 * n]))
+    gain = GainSum(*refs[-3:])
+    down, up, wo = sums
+    step = pl.program_id(0)
+
+    @pl.when(step == 0)
+    def _():
+        greet(GainSum.bits)
+        for one in sums:
+            one.start()
+        gain.start(gain_ref[...])
+
+    for at, plan in {
+        1: ((down, 1), (up, 1), (wo, 1), (gain, 1)),
+        2: ((wo, 2), (gain, 2)),
+        3: ((down, 2), (up, 2), (wo, 3), (gain, 3)),
+        4: ((down, 3), (up, 3), (wo, 4), (gain, 4)),
+        5: ((down, 4), (up, 4)),
+    }.items():
+
+        @pl.when(step == at)
+        def _():
+            for one, number in plan:
+                one.step(number)
+
+    attend_back_kernel(*core, dqkv_ref, *own)
+
+    @pl.when(step == pl.num_programs(0) - 1)
+    def _():
+        for one, out_ref in zip(sums, outs):
+            one.finish(out_ref)
+        gain.finish(gain_out)
+
+
+def attend_back_kernel(qkv_ref, o_ref, do_ref, log_ref, cq_ref, nq_ref, mk_ref, dk_ref, cos_ref, sin_ref,
                        dqkv_ref, qa, qz, ka, kd, kt, doz, dsum, dq, dkc, dvc):
     length = o_ref.shape[1]
-    clean = side_ref[0]
+    clean = lax.axis_index("stream")
     noisy = 1 - clean
     tiles = length // TILE
     low = low_lanes((length, LANES))
@@ -288,27 +441,45 @@
     dqkv_ref[0, noisy] = finish(dq[1].T, True, 0.125)
 
 
-def attend_back(side, into, first, pairs, qkv, mixed, grad, logs, tables, cosine, sine):
+def attend_back(qkv, mixed, grad, logs, tables, cosine, sine, pairs=None, gain=None):
     _, copies, length, width = qkv.shape
-    table_spec = pl.BlockSpec((length, LANES), lambda i, s: (0, 0), pipeline_mode=pl.Buffered(1))
-    row_spec = pl.BlockSpec((copies, length, LANES), lambda i, s: (0, 0, i + first))
-    three = pl.BlockSpec((3, copies, length, LANES), lambda i, s: (0, 0, 0, i + first))
-    begun = [] if into is None else [into]
+    steps = width // LANES
+    table_spec = pl.BlockSpec((length, LANES), lambda i: (0, 0), pipeline_mode=pl.Buffered(1))
+    row_spec = pl.BlockSpec((copies, length, LANES), lambda i: (0, 0, i))
+    three = pl.BlockSpec((3, copies, length, LANES), lambda i: (0, 0, 0, i))
+    anywhere = pl.BlockSpec(memory_space=pl.ANY)
+
+    def fixed(shape):
+        return pl.BlockSpec(shape, lambda i: (0, 0), pipeline_mode=pl.Buffered(1))
+
+    more_in, more_specs, more_shapes, more_out, more_scratch = [], [], [], [], []
+    body, params = attend_back_kernel, {}
+    if pairs is not None:
+        assert steps == 6
+        body = functools.partial(attend_back_sum_kernel, orders=(DOWN, UP, OUT))
+        params = dict(collective_id=1, has_side_effects=True)
+        for keep, send in pairs:
+            slots, share, columns = keep.shape
+            more_in += [keep, send]
+            more_specs += [anywhere] * 2
+            more_shapes.append(jax.ShapeDtypeStruct((share, columns), f32))
+            more_out.append(fixed((share, columns)))
+            more_scratch += SlabSum.scratch(slots, share, columns)
+        more_in.append(gain)
+        more_specs.append(fixed((8, width)))
+        more_shapes.append(jax.ShapeDtypeStruct((8, width), f32))
+        more_out.append(fixed((8, width)))
+        more_scratch += GainSum.scratch(width)
     return pl.pallas_call(
-        attend_back_next if begun else attend_back_kernel,
+        body,
         name="attend_back",
         grid_spec=pltpu.PrefetchScalarGridSpec(
-            num_scalar_prefetch=1,
-            grid=(pairs,),
-            in_specs=[
-                *[pl.BlockSpec(memory_space=pl.ANY)] * len(begun),
-                three,
-                row_spec,
-                row_spec,
-                pl.BlockSpec((copies, 1, 2, length), lambda i, s: (0, i + first, 0, 0)),
-            ]
-            + [table_spec] * 6,
-            out_specs=three,
+            num_scalar_prefetch=0,
+            grid=(steps,),
+            in_specs=[three, row_spec, row_spec, pl.BlockSpec((copies, 1, 2, length), lambda i: (0, i, 0, 0))]
+            + [table_spec] * 6
+            + more_specs,
+            out_specs=[three, *more_out],
             scratch_shapes=[
                 pltpu.VMEM((3, 2, length, LANES), bf16),
                 pltpu.VMEM((2, 2, length, LANES), bf16),
@@ -320,17 +491,15 @@
                 pltpu.VMEM((2, LANES, length), f32),
                 pltpu.VMEM((length, LANES), f32),
                 pltpu.VMEM((length, LANES), f32),
+                *more_scratch,
             ],
         ),
-        out_shape=jax.ShapeDtypeStruct((3, copies, length, width), bf16),
-        input_output_aliases={1: 0} if begun else {},
-        compiler_params=pltpu.CompilerParams(vmem_limit_bytes=48 << 20),
+        out_shape=[jax.ShapeDtypeStruct((3, copies, length, width), bf16), *more_shapes],
+        compiler_params=pltpu.CompilerParams(vmem_limit_bytes=60 << 20, **params),
         cost_estimate=pl.CostEstimate(
-            flops=20 * length * length * LANES * pairs,
-            bytes_accessed=32 * length * LANES * pairs,
-            transcendentals=4 * length * length * pairs,
-        ),
-    )(side, *begun, qkv, mixed, grad, logs, *tables, cosine, sine)
+            flops=20 * length * length * width, bytes_accessed=30 * length * width, transcendentals=length * length * 12
+        ),
+    )(qkv, mixed, grad, logs, *tables, cosine, sine, *more_in)
 
 
 ROOT = math.sqrt(2.0 / math.pi)
@@ -463,7 +632,15 @@
     )(side, x_own, x_away, mixed, g_own, g_away, gain, rest)
 
 
-def weight_kernel(me_ref, left_ref, *refs, share, split):
+def arranged(slot, order):
+    return sum((slot >> bit & 1) << (len(order) - 1 - n) for n, bit in enumerate(order))
+
+
+def weight_kernel(me_ref, left_ref, *refs, share, split, order):
+    weight_slabs(me_ref[0], left_ref, *refs, share=share, split=split, order=order)
+
+
+def weight_slabs(me, left_ref, *refs, share, split, order):
     right_refs, (keep_ref, send_ref, scr) = refs[:-3], refs[-3:]
     if split:
         own_ref, away_ref = right_refs
@@ -473,28 +650,28 @@
         total = t_mm(left_ref[...], right_refs[0][...])
     slabs = total.shape[0] // share
     scr[...] = total.reshape(scr.shape)
-    low_me = lax.rem(me_ref[0], slabs)
+    low_me = lax.rem(me, slabs)
     for slot in range(slabs):
         source = jnp.bitwise_xor(low_me, slot)
         into = send_ref if slot % 2 else keep_ref
-        into[slot // 2] = scr[source].astype(bf16)
-
-
-def weight_grad_columns(me, left, right, part, block, share, name):
+        into[arranged(slot // 2, order)] = scr[source].astype(bf16)
+
+
+def weight_grad_columns(me, left, right, block, share, order, name):
     tokens, dl = left.shape
-    dr = right.shape[2]
+    dr = right.shape[1]
     peers = dl // share
     shape = (peers // 2, share, dr)
     out = pl.BlockSpec((peers // 2, share, block), lambda j, m: (0, 0, j))
     return pl.pallas_call(
-        functools.partial(weight_kernel, share=share, split=False),
+        functools.partial(weight_kernel, share=share, split=False, order=order),
         name=name,
         grid_spec=pltpu.PrefetchScalarGridSpec(
             num_scalar_prefetch=1,
             grid=(dr // block,),
             in_specs=[
                 pl.BlockSpec((tokens, dl), lambda j, m: (0, 0), pipeline_mode=pl.Buffered(1)),
-                pl.BlockSpec((None, tokens, block), lambda j, m: (part, 0, j)),
+                pl.BlockSpec((tokens, block), lambda j, m: (0, j)),
             ],
             out_specs=[out, out],
             scratch_shapes=[pltpu.VMEM((peers, share, block), f32)],
@@ -512,14 +689,16 @@
     length, dr = away.shape
     slabs = block // share
     steps = dl // block
-    shape = (steps * slabs // 2, share, dr)
-    out = pl.BlockSpec((slabs // 2, share, dr), lambda j, m: (j, 0, 0))
+    assert steps == 4
+    shape = (2, slabs // 2, 2, share, dr)
+    out = pl.BlockSpec((None, slabs // 2, None, share, dr), lambda j, m: (lax.div(j, 2), 0, lax.rem(j, 2), 0, 0))
+    bits = (slabs // 2).bit_length() - 1
 
     def place(j, m):
         return (0, jnp.bitwise_xor(j, lax.div(m[0], slabs)))
 
     return pl.pallas_call(
-        functools.partial(weight_kernel, share=share, split=True),
+        functools.partial(weight_kernel, share=share, split=True, order=tuple(range(bits))),
         name=name,
         grid_spec=pltpu.PrefetchScalarGridSpec(
             num_scalar_prefetch=1,
@@ -538,6 +717,79 @@
             flops=2 * tokens * dl * dr, bytes_accessed=2 * tokens * (dl + dr) + 2 * dl * dr, transcendentals=0
         ),
     )(me, left, own, away)
+
+
+def qkv_grad_kernel(hidden_ref, dqkv_ref, gain_ref, out_ref, gain_out, scr, *refs, share):
+    count = len(QKV)
+    width = scr.shape[-1]
+    per = len(refs[:-3]) // count
+    sums = []
+    for n, order in enumerate(QKV):
+        send, keep, *got, sems = refs[n * per : (n + 1) * per]
+        sums.append(SlabSum(order, keep, send, got, sems))
+    gain = GainSum(*refs[-3:])
+    me = lax.axis_index("stream") * lax.axis_size("batch") + lax.axis_index("batch")
+    step = pl.program_id(0)
+
+    @pl.when(step == 0)
+    def _():
+        greet(GainSum.bits)
+        gain.start(gain_ref[...])
+
+    for n, one in enumerate(sums):
+
+        @pl.when(step == n)
+        def _():
+            weight_slabs(me, hidden_ref, dqkv_ref, one.keep, one.send, scr, share=share, split=False, order=tuple(
+                {-1: 3, 1: 0, 2: 1, 3: 2}[bit] for bit in QKV[n]
+            ))
+            one.start()
+            for earlier in range(n):
+                sums[earlier].step(n - earlier)
+            if n:
+                gain.step(n)
+
+    @pl.when(step == count - 1)
+    def _():
+        for number in range(2, 5 + count - 1):
+            for n, one in enumerate(sums):
+                now = number - n
+                if count - 1 - n < now < 5:
+                    one.step(now)
+            if count - 1 < number < 5:
+                gain.step(number)
+        for n, one in enumerate(sums):
+            one.finish(out_ref, slice(n * width, (n + 1) * width))
+        gain.finish(gain_out)
+
+
+def qkv_grad(hidden, dqkv, gain, share):
+    tokens, width = hidden.shape
+    slots = width // share // 2
+    fixed = pl.BlockSpec((8, width), lambda j: (0, 0), pipeline_mode=pl.Buffered(1))
+    scratch = []
+    for _ in range(3):
+        scratch += [pltpu.VMEM((slots, share, width), bf16), *SlabSum.scratch(slots, share, width)]
+    return pl.pallas_call(
+        functools.partial(qkv_grad_kernel, share=share),
+        name="grad_qkv",
+        grid_spec=pltpu.PrefetchScalarGridSpec(
+            num_scalar_prefetch=0,
+            grid=(3,),
+            in_specs=[
+                pl.BlockSpec((tokens, width), lambda j: (0, 0), pipeline_mode=pl.Buffered(1)),
+                pl.BlockSpec((None, tokens, width), lambda j: (j, 0, 0)),
+                fixed,
+            ],
+            out_specs=[pl.BlockSpec((share, 3 * width), lambda j: (0, 0), pipeline_mode=pl.Buffered(1)), fixed],
+            scratch_shapes=[pltpu.VMEM((2 * slots, share, width), f32), *scratch, *GainSum.scratch(width)],
+        ),
+        out_shape=[jax.ShapeDtypeStruct((share, 3 * width), f32), jax.ShapeDtypeStruct((8, width), f32)],
+        compiler_params=pltpu.CompilerParams(vmem_limit_bytes=60 << 20, collective_id=2, has_side_effects=True),
+        cost_estimate=pl.CostEstimate(
+            flops=6 * tokens * width * width, bytes_accessed=8 * tokens * width, transcendentals=0
+        ),
+    )(hidden, dqkv, gain)
 
 
 def project_back_kernel(side_ref, x_ref, gain_ref, w_ref, dqkv_ref, dmid_ref, dx_ref, dgain_ref):
@@ -601,43 +853,8 @@
     return lax.ppermute(x, axis, [(i, i ^ by) for i in range(lax.axis_size(axis))])
 
 
-class SlabSum:
-    def __init__(self, pair, order):
-        keep, send = pair
-        bits = lax.axis_size("batch").bit_length() - 1
-        self.left = [-1, *range(bits - 1, 0, -1)]
-        self.order = list(order)
-        self.keep = keep.reshape(*[2] * bits, *keep.shape[1:])
-        self.got = flip(send.reshape(self.keep.shape), 0)
-
-    def step(self):
-        if not self.order:
-            self.keep = self.keep.astype(f32) + self.got.astype(f32)
-            return self.keep
-        bit = self.order.pop(0)
-        at = self.left.index(bit)
-        self.left.remove(bit)
-        halves = [
-            lax.index_in_dim(self.keep, i, at, False) + lax.index_in_dim(self.got, i, at, False) for i in range(2)
-        ]
-        self.keep = halves[0]
-        self.got = flip(halves[1], bit)
-        return self.keep
-
-    def finish(self):
-        while self.keep.dtype != f32:
-            self.step()
-        return self.keep
-
-
 def after(value, *others):
     return lax.optimization_barrier((value, *others))[0]
-
-
-def all_sum(x):
-    for bit in range(-1, lax.axis_size("batch").bit_length() - 1):
-        x = x + flip(x, bit)
-    return x
 
 
 def gather_kernel(shard_ref, gain_ref, w_ref, gains_ref, local_sems, send_sems, recv_sems, *, plans):
@@ -772,52 +989,45 @@
         return lax.dynamic_update_slice(result, away[None, None], (0, 1 - side, 0, 0))
 
     out = place(out, out_away)
-    cols_share = share if small else width // 32
-    down = weight_grad_rows(me, act, cotangent, g_away, width, ff // width * cols_share, "grad_down")
-    down = weight_grad_rows(me, act, cotangent, g_away, width, ff // width * cols_share, "grad_down")
+    unit = share if small else width // 32
+    places = {-1: 3, 1: 0, 2: 1, 3: 2}
+
+    def columns_grad(left, right, order, name):
+        return weight_grad_columns(me, left, right, width, unit, [places[bit] for bit in order], name)
+
+    down = weight_grad_rows(me, act, cotangent, g_away, width, ff // width * unit, "grad_down")
+    down = [part.reshape(16, -1, width) for part in down]
+    up = columns_grad(h2, du, UP, "grad_up")
+    wo = columns_grad(mixed2, dbr, OUT, "grad_out")
+    dmix = after(dmix.reshape(2, length, width), out)
+    common = qkv4, mixed, dmix, logs, tables, cosine, sine
     if small:
-        down = SlabSum(down, (-1, 1, 2, 3))
-        h2 = after(h2, down.keep)
-    up = weight_grad_columns(me, h2, du[None], 0, width, cols_share, "grad_up")
-    if small:
-        up = SlabSum(up, (1, -1, 2, 3))
-        dbr = after(dbr, up.keep, down.step())
-    wo = weight_grad_columns(me, mixed2, dbr[None], 0, width, cols_share, "grad_out")
-    dgain_two = all_sum(jnp.sum(dgain_two, axis=0, keepdims=True))
-    dqkv = None
-    dmix = dmix.reshape(2, length, width)
-    if small:
-        wo = SlabSum(wo, (2, -1, 1, 3))
-        dmix = after(dmix, wo.keep, up.step())
-    plan = {1: "wo", 2: "down up wo", 3: "down up wo", 4: "down up wo", 5: "down up wo"}
-    for first in range(width // LANES):
-        if small and first in plan:
-            sums = {"down": down, "up": up, "wo": wo}
-            dmix = after(dmix, *[sums[n].step() for n in plan[first].split()])
-        dqkv = attend_back(side_array, dqkv, first, 1, qkv4, mixed, dmix, logs, tables, cosine, sine)
+        dqkv, down, up, wo, dgain_two = attend_back(*common, (down, up, wo), dgain_two)
+    else:
+        dqkv, = attend_back(*common)
     dqkv3 = dqkv.reshape(3, 2 * length, width)
     dx_away, dgain_away = project_back(side_array, x_away, gain_one, w_qkv_all, dqkv3, dmid, True)
-    later = after(dqkv3, dx_away)
-    parts = []
-    for n in range(3):
-        pair = weight_grad_columns(me, hidden, later, n, width, cols_share, "grad_qkv")
-        parts.append(SlabSum(pair, ((1, 2, -1, 3), (2, 1, -1, 3), (2, -1, 1, 3))[n]) if small else pair)
-        later = after(later, parts[-1].keep if small else pair[0])
-    dx, dgain_own = project_back(side_array, tokens, gain_one, w_qkv_all, later, dmid, False)
-    dgain_one = all_sum(jnp.sum(dgain_own + dgain_away, axis=0, keepdims=True))
+    dx, dgain_own = project_back(side_array, tokens, gain_one, w_qkv_all, dqkv3, dmid, False)
+    dgain_one = dgain_own + dgain_away
+    if small:
+        wq, dgain_one = qkv_grad(hidden, dqkv3, dgain_one, share)
     dx = place(dx, dx_away)
-    if small:
-        wq = jnp.concatenate([part.finish() for part in parts], axis=1)
-        down, up, wo = down.finish(), up.finish(), wo.finish()
-    else:
-
-        def scatter(pair):
+    dgain_one, dgain_two = (jnp.sum(g, axis=0, keepdims=True) for g in (dgain_one, dgain_two))
+    if not small:
+
+        def scatter(pair, order):
             slots = jnp.stack(pair, axis=1)
-            rows = slots.reshape(-1, slots.shape[-1])
+            natural = [arranged(n, order) for n in range(16)]
+            rows = slots[jnp.array(natural)].reshape(-1, slots.shape[-1])
             return lax.psum_scatter(rows, ("stream", "batch"), scatter_dimension=0, tiled=True).astype(f32)
 
-        down, up, wo, *parts = (scatter(pair) for pair in (down, up, wo, *parts))
+        parts = [columns_grad(hidden, dqkv3[n], QKV[n], "grad_qkv") for n in range(3)]
+        down, up, wo, *parts = (
+            scatter(pair, [places[bit] for bit in order])
+            for pair, order in zip((down, up, wo, *parts), (DOWN, UP, OUT, *QKV))
+        )
         wq = jnp.concatenate(parts, axis=1)
+        dgain_one, dgain_two = lax.psum((dgain_one, dgain_two), ("stream", "batch"))
     begin = index * share
     dgain_one, dgain_two = (lax.dynamic_slice(g[0], (begin,), (share,)) for g in (dgain_one, dgain_two))
     return out, dx, dgain_one, wq, wo, dgain_two, up, down

time: 582 us -> 472 us (0.81)
  waiting for transfers between devices: 93.9 us -> 0.03 us
  starting transfers between devices: 43 us -> 5.12 us
  Pallas kernels: 379 us -> 410 us
  other arithmetic: 17.6 us -> 10.2 us
    ppermute x44 -> x4, waiting for transfers between devices: 93.9 us -> 0.01 us  [flip(): lax.ppermute(x, axis, [(i, i ^ by) for i in range(lax.axis_size(axis))])]
    pallas_call x12 -> x5, Pallas kernels: 153 us -> 195 us  [the longest x1 95.2 us: attend_back(): pl.pallas_call(body, name='attend_back', grid_spec=pltpu.PrefetchScalarGr...]
    ppermute x44 -> x4, starting transfers between devices: 43 us -> 5.09 us  [flip(): lax.ppermute(x, axis, [(i, i ^ by) for i in range(lax.axis_size(axis))])]
    pallas_call x1, Pallas kernels: 75.5 us -> 64.7 us  [feed(): pl.pallas_call(functools.partial(feed_kernel, half=half), name='feed', gr...]
    add x38 -> x1, other arithmetic: 9.94 us -> 0.61 us  [shards(): dgain_one = dgain_own + dgain_away]
  transfers between devices with their start and end apart: 45 -> 5, of which waited for: 19 -> 0; matrix products, arithmetic and copies ran while one was open for 5% -> 3% of each run, Pallas kernels for 50% -> 52%
where the time goes in v3:
time: 472 us; the launch traced here: 465 us
  Pallas kernels  410 us (87%)
  local copies, waits for them, and re-layouts  24.2 us (5%)
  between operations  15.5 us (3%)
  other arithmetic  10.2 us (2%)
  starting transfers between devices  5.12 us (1%)
    pallas_call x1, Pallas kernels, attend_back(): pl.pallas_call(body, name='attend_back', grid_spec=pltpu.PrefetchScalarGr...  95.2 us
    pallas_call x1, Pallas kernels, gather(): pl.pallas_call(functools.partial(gather_kernel, plans=plans), name='gathe...  72.5 us
    pallas_call x1, Pallas kernels, feed(): pl.pallas_call(functools.partial(feed_kernel, half=half), name='feed', gr...  64.7 us
    pallas_call x1, Pallas kernels, qkv_grad(): pl.pallas_call(functools.partial(qkv_grad_kernel, share=share), name='gra...  63.8 us
    pallas_call x1, Pallas kernels, attend(): pl.pallas_call(attend_kernel, name='attend', grid_spec=pltpu.PrefetchScal...  44.3 us
    pallas_call x2, Pallas kernels, weight_grad_columns(): pl.pallas_call(functools.partial(weight_kernel, share=share, split=False,...  20 us
    pallas_call x2, Pallas kernels, project_back(): pl.pallas_call(project_back_kernel, name='project_back_away' if away else...  19.4 us
    pallas_call x1, Pallas kernels, weight_grad_rows(): pl.pallas_call(functools.partial(weight_kernel, share=share, split=True,...  15.8 us
  transfers between devices with their start and end apart: 5, of which 0 were waited for; matrix products, arithmetic and copies ran while one was open for 3% of the time, Pallas kernels for 52%

profile of v3, /device:TPU:0, one launch (start us, length us, event | category | flops | bytes accessed | tf_op | source)
XLA Modules:
  0.0 465.2 jit_solution(3903655078006986099)
XLA Ops:
  8.2 1.9 pad_maximum_fusion
  10.2 2.8 dynamic-slice_bitcast_fusion.1
  13.0 2.9 collective-permute-start
  18.6 72.5 %gather.6 = (bf16[16,48,2304]{2,1,0:T(8,128)(2,1)}, bf16[16,16,128]{2,1,0:T(8,128)(2,1)}) custom-call(bf16[48,2304]{1,0:T(8,128)(2,1)} %shard_ref.1, bf16[16,128]{1,0:T(8,128)(2,1)} %copy-done.24), custom_call_target="tpu_custom_call" | custom-call | bytes 14155776 | tf_op jit(solution)/shard_map/gather/pallas_call | solution.py:924
  92.7 1.9 fusion
  97.1 14.4 %project.1 = (bf16[3,2048,768]{2,1,0:T(8,128)(2,1)}, bf16[2048,768]{1,0:T(8,128)(2,1)S(1)}) custom-call(s32[1]{0:T(128)} %bitcast.side_ref, bf16[1,2,1024,768]{3,2,1,0:T(8,128)(2,1)} %x_ref.1, bf16[1024,768]{1,0:T(8,128)(2,1)S(1)} %collective-permute-done.away_ref.x_away.x_ref, bf16[1,768]{1,0:T(2,128)(2,1)S(1)} %reshape_squeeze.6.gain_ref, ...), custom_call_target="tpu_custom_call" | custom-call | flops 7247757312 | bytes 19267584 | tf_op jit(solution)/shard_map/project/pallas_call | solution.py:83
  111.5 1.6 copy-done.14
  113.2 44.3 %attend.1 = (bf16[2,1024,768]{2,1,0:T(8,128)(2,1)S(1)}, f32[2,6,2,1024]{3,2,1,0:T(2,128)S(1)}) custom-call(s32[1]{0:T(128)} %bitcast.side_ref, bf16[3,2,1024,768]{3,2,1,0:T(8,128)(2,1)} %bitcast.42, bf16[1024,128]{1,0:T(8,128)(2,1)S(1)} %get-tuple-element.117.cq_ref.refs_4_, bf16[1024,128]{1,0:T(8,128)(2,1)S(1)} %get-tuple-element.116.nq_ref.refs_5_, ...), custom_call_target="tpu_custom_call" | custom-call | flops 6442450944 | bytes 12582912 | tf_op jit(solution)/shard_map/attend/pallas_call | solution.py:179
  157.5 1.7 copy-done.9
  159.8 64.7 %feed.1 = (bf16[1,2,1024,768]{3,2,1,0:T(8,128)(2,1)}, bf16[1024,768]{1,0:T(8,128)(2,1)}, bf16[2048,3072]{1,0:T(8,128)(2,1)}, bf16[2048,3072]{1,0:T(8,128)(2,1)},...) custom-call(s32[1]{0:T(128)} %bitcast.side_ref, ...), custom_call_target="tpu_custom_call" | custom-call | flops 43486543872 | bytes 53477376 | tf_op jit(solution)/shard_map/feed/pallas_call | solution.py:601
  224.6 1.4 collective-permute-start.2
  226.0 5.2 %grad_out.1 = (bf16[16,24,768]{2,1,0:T(8,128)(2,1)S(1)}, bf16[16,24,768]{2,1,0:T(8,128)(2,1)S(1)}) custom-call(s32[2]{0:T(128)S(1)} %pad_add_fusion.me_ref, bf16[2048,768]{1,0:T(8,128)(2,1)S(1)} %bitcast.29, bf16[2048,768]{1,0:T(8,128)(2,1)} %get-tuple-element.81.refs_0_), custom_call_target="tpu_custom_call" | custom-call | flops 2415919104 | bytes 7471104 | tf_op jit(solution)/shard_map/grad_out/pallas_call | solution.py:666
  232.0 14.8 %grad_up.1 = (bf16[16,24,3072]{2,1,0:T(8,128)(2,1)S(1)}, bf16[16,24,3072]{2,1,0:T(8,128)(2,1)S(1)}) custom-call(s32[2]{0:T(128)S(1)} %pad_add_fusion.me_ref, bf16[2048,768]{1,0:T(8,128)(2,1)} %get-tuple-element.77.left_ref, bf16[2048,3072]{1,0:T(8,128)(2,1)} %get-tuple-element.78.refs_0_), custom_call_target="tpu_custom_call" | custom-call | flops 9663676416 | bytes 20447232 | tf_op jit(solution)/shard_map/grad_up/pallas_call | solution.py:666
  246.9 1.4 copy-done.15
  248.2 1.4 copy-done.16
  249.6 15.8 %grad_down.1 = (bf16[2,4,2,96,768]{4,3,2,1,0:T(8,128)(2,1)S(1)}, bf16[2,4,2,96,768]{4,3,2,1,0:T(8,128)(2,1)}) custom-call(s32[2]{0:T(128)S(1)} %pad_add_fusion.me_ref, bf16[2048,3072]{1,0:T(8,128)(2,1)} %get-tuple-element.74.left_ref, bf16[1,2,1024,768]{3,2,1,0:T(8,128)(2,1)} %refs_0_.1, bf16[1024,768]{1,0:T(8,128)(2,1)} %collective-permute-done.1.g_away.refs_1_), custom_call_target="tpu_custom_call" | custom-call | flops 9663676416 | bytes 20447232 | tf_op jit(solution)/shard_map/grad_down/pallas_call | solution.py:700
  265.4 1.4 copy-done.11
  267.0 1.7 copy-done.28
  268.6 95.2 %attend_back.1 = (bf16[3,2,1024,768]{3,2,1,0:T(8,128)(2,1)}, f32[96,768]{1,0:T(8,128)}, f32[24,3072]{1,0:T(8,128)}, f32[24,768]{1,0:T(8,128)}, f32[8,768]{1,0:T(8,128)}) custom-call(bf16[3,2,1024,768]{3,2,1,0:T(8,128)(2,1)} %bitcast.43, bf16[2,1024,768]{2,1,0:T(8,128)(2,1)} %copy-done.9, bf16[2,1024,768]{2,1,0:T(8,128)(2,1)} %bitcast.44, ...), custom_call_target="tpu_custom_call" | custom-call | flops 16106127360 | bytes 23592960 | tf_op jit(solution)/shard_map/attend_back/pallas_call | solution.py:473
  363.9 1.4 copy-done.2
  365.3 9.6 %project_back_away.1 = (bf16[1024,768]{1,0:T(8,128)(2,1)}, f32[8,768]{1,0:T(8,128)S(1)}) custom-call(s32[1]{0:T(128)} %bitcast.side_ref, bf16[1024,768]{1,0:T(8,128)(2,1)S(1)} %copy-done.2, bf16[1,768]{1,0:T(2,128)(2,1)S(1)} %reshape_squeeze.6.gain_ref, bf16[768,2304]{1,0:T(8,128)(2,1)} %bitcast.35, bf16[3,2048,768]{2,1,0:T(8,128)(2,1)} %bitcast.31, ...), custom_call_target="tpu_custom_call" | custom-call | flops 3623878656 | bytes 12582912 | tf_op jit(solution)/shard_map/project_back_away/pallas_call | solution.py:828
  375.6 9.7 %project_back_own.1 = (f32[1,2,1024,768]{3,2,1,0:T(8,128)}, f32[8,768]{1,0:T(8,128)S(1)}) custom-call(s32[1]{0:T(128)} %bitcast.side_ref, bf16[1,2,1024,768]{3,2,1,0:T(8,128)(2,1)S(1)} %copy-done, bf16[1,768]{1,0:T(2,128)(2,1)S(1)} %reshape_squeeze.6.gain_ref, bf16[768,2304]{1,0:T(8,128)(2,1)} %bitcast.36, bf16[3,2048,768]{2,1,0:T(8,128)(2,1)} %bitcast.32, ...), custom_call_target="tpu_custom_call" | custom-call | flops 3623878656 | bytes 12582912 | tf_op jit(solution)/shard_map/project_back_own/pallas_call | solution.py:828
  386.0 63.8 %grad_qkv.1 = (f32[24,2304]{1,0:T(8,128)}, f32[8,768]{1,0:T(8,128)}) custom-call(bf16[2048,768]{1,0:T(8,128)(2,1)} %copy-done.14, bf16[3,2048,768]{2,1,0:T(8,128)(2,1)} %bitcast.33, f32[8,768]{1,0:T(8,128)} %add.66.gain_ref), custom_call_target="tpu_custom_call" | custom-call | flops 7247757312 | bytes 12582912 | tf_op jit(solution)/shard_map/grad_qkv/pallas_call | solution.py:773
  451.9 3.3 convert_dynamic-update-slice_fusion
  (89 shorter events, 14.8 us)
Async XLA Ops:
  7.2 152.7 %all-gather.2.cloned.1.call-start = ((), (), s32[]{:S(2)}) async-start(), calls=%async_computation | async-start | bytes 11280384 | tf_op jit(solution)/shard_map/all_gather | solution.py:966
  10.1 5.8 %copy-start.18 = (bf16[1,2,1024,768]{3,2,1,0:T(8,128)(2,1)S(1)}, bf16[1,2,1024,768]{3,2,1,0:T(8,128)(2,1)}, u32[]{:S(2)}) copy-start(bf16[1,2,1024,768]{3,2,1,0:T(8,128)(2,1)} %refs_0_.1) | copy-start | bytes 9437188
  10.1 7.1 %copy-start.29 = (s32[2]{0:T(128)S(1)}, s32[2]{0:T(128)}, u32[]{:S(2)}) copy-start(s32[2]{0:T(128)} %param.15) | copy-start | bytes 28
  10.1 7.7 %copy-start.25 = (bf16[48]{0:T(256)(128)(2,1)S(1)}, bf16[48]{0:T(256)(128)(2,1)}, u32[]{:S(2)}) copy-start(bf16[48]{0:T(256)(128)(2,1)} %param.16) | copy-start | bytes 292
  10.2 7.7 %copy-start.26 = (bf16[48]{0:T(256)(128)(2,1)S(1)}, bf16[48]{0:T(256)(128)(2,1)}, u32[]{:S(2)}) copy-start(bf16[48]{0:T(256)(128)(2,1)} %param.19) | copy-start | bytes 292
  13.0 84.1 %collective-permute-start = (bf16[1024,768]{1,0:T(8,128)(2,1)}, bf16[1024,768]{1,0:T(8,128)(2,1)S(1)}, u32[]{:S(2)}, u32[]{:S(2)}) collective-permute-start(bf16[1024,768]{1,0:T(8,128)(2,1)} %dynamic-slice_bitcast_fusion.1), channel_id=1, source_target_pairs={{0,16},{16,0},{1,17},{17,1},{2,18},{18,2},{3,19},{19,3},{4,20},{20... | collective-permute-start | bytes 4718600 | tf_op jit(solution)/shard_map/ppermute | solution.py:853
  17.2 142.6 %collective-permute-start.1 = (bf16[1024,768]{1,0:T(8,128)(2,1)}, bf16[1024,768]{1,0:T(8,128)(2,1)}, u32[]{:S(2)}, u32[]{:S(2)}) collective-permute-start(bf16[1024,768]{1,0:T(8,128)(2,1)} %dynamic-slice_bitcast_fusion), channel_id=1, source_target_pairs={{0,16},{16,0},{1,17},{17,1},{2,18},{18,2},{3,19},{19,3},{4,20},{20... | collective-permute-start | bytes 4718600 | tf_op jit(solution)/shard_map/ppermute | solution.py:853
  95.5 16.0 %copy-start.3 = (f32[1024,128]{1,0:T(8,128)}, f32[1024,128]{1,0:T(8,128)S(1)}, u32[]{:S(2)}) copy-start(f32[1024,128]{1,0:T(8,128)S(1)} %get-tuple-element.118.cos_ref.refs_8_) | copy-start | bytes 1572868
  95.5 16.0 %copy-start.4 = (f32[1024,128]{1,0:T(8,128)}, f32[1024,128]{1,0:T(8,128)S(1)}, u32[]{:S(2)}) copy-start(f32[1024,128]{1,0:T(8,128)S(1)} %get-tuple-element.119.sin_ref.refs_9_) | copy-start | bytes 1572868
  95.9 17.3 %copy-start.5 = (bf16[1024,128]{1,0:T(8,128)(2,1)}, bf16[1024,128]{1,0:T(8,128)(2,1)S(1)}, u32[]{:S(2)}) copy-start(bf16[1024,128]{1,0:T(8,128)(2,1)S(1)} %get-tuple-element.111.dk_ref.refs_7_) | copy-start | bytes 786436
  95.9 17.3 %copy-start.6 = (bf16[1024,128]{1,0:T(8,128)(2,1)}, bf16[1024,128]{1,0:T(8,128)(2,1)S(1)}, u32[]{:S(2)}) copy-start(bf16[1024,128]{1,0:T(8,128)(2,1)S(1)} %get-tuple-element.112.mk_ref.refs_6_) | copy-start | bytes 786436
  97.1 16.1 %copy-start.7 = (bf16[1024,128]{1,0:T(8,128)(2,1)}, bf16[1024,128]{1,0:T(8,128)(2,1)S(1)}, u32[]{:S(2)}) copy-start(bf16[1024,128]{1,0:T(8,128)(2,1)S(1)} %get-tuple-element.116.nq_ref.refs_5_) | copy-start | bytes 786436
  97.1 16.1 %copy-start.8 = (bf16[1024,128]{1,0:T(8,128)(2,1)}, bf16[1024,128]{1,0:T(8,128)(2,1)S(1)}, u32[]{:S(2)}) copy-start(bf16[1024,128]{1,0:T(8,128)(2,1)S(1)} %get-tuple-element.117.cq_ref.refs_4_) | copy-start | bytes 786436
  97.1 14.4 %copy-start.1 = (bf16[1024,768]{1,0:T(8,128)(2,1)}, bf16[1024,768]{1,0:T(8,128)(2,1)S(1)}, u32[]{:S(2)}) copy-start(bf16[1024,768]{1,0:T(8,128)(2,1)S(1)} %collective-permute-done.away_ref.x_away.x_ref) | copy-start | bytes 4718596
  159.8 66.1 %copy-start.10 = (bf16[2,1024,768]{2,1,0:T(8,128)(2,1)S(1)}, bf16[2,1024,768]{2,1,0:T(8,128)(2,1)}, u32[]{:S(2)}) copy-start(bf16[2,1024,768]{2,1,0:T(8,128)(2,1)} %copy-done.9) | copy-start | bytes 9437188
  224.6 42.2 %collective-permute-start.2 = (bf16[1024,768]{1,0:T(8,128)(2,1)}, bf16[1024,768]{1,0:T(8,128)(2,1)S(1)}, u32[]{:S(2)}, u32[]{:S(2)}) collective-permute-start(bf16[1024,768]{1,0:T(8,128)(2,1)} %get-tuple-element.70), channel_id=1, source_target_pairs={{0,16},{16,0},{1,17},{17,1},{2,18},{18,2},{3,19},{19,3},{4,20},{20... | collective-permute-start | bytes 4718600 | tf_op jit(solution)/shard_map/ppermute | solution.py:853
  232.0 14.8 %copy-start.12 = (bf16[16,24,768]{2,1,0:T(8,128)(2,1)}, bf16[16,24,768]{2,1,0:T(8,128)(2,1)S(1)}, u32[]{:S(2)}) copy-start(bf16[16,24,768]{2,1,0:T(8,128)(2,1)S(1)} %get-tuple-element.82.refs_14_) | copy-start | bytes 1769476
  249.6 17.2 %copy-start.27 = (bf16[1,2,1024,768]{3,2,1,0:T(8,128)(2,1)S(1)}, bf16[1,2,1024,768]{3,2,1,0:T(8,128)(2,1)}, u32[]{:S(2)}) copy-start(bf16[1,2,1024,768]{3,2,1,0:T(8,128)(2,1)} %get-tuple-element.69) | copy-start | bytes 9437188
  365.3 10.4 %copy-start = (bf16[1,2,1024,768]{3,2,1,0:T(8,128)(2,1)S(1)}, bf16[1,2,1024,768]{3,2,1,0:T(8,128)(2,1)}, u32[]{:S(2)}) copy-start(bf16[1,2,1024,768]{3,2,1,0:T(8,128)(2,1)} %x_ref.1) | copy-start | bytes 9437188
  374.9 77.0 %collective-permute-start.3 = (bf16[1024,768]{1,0:T(8,128)(2,1)}, bf16[1024,768]{1,0:T(8,128)(2,1)}, u32[]{:S(2)}, u32[]{:S(2)}) collective-permute-start(bf16[1024,768]{1,0:T(8,128)(2,1)} %get-tuple-element.88), channel_id=1, source_target_pairs={{0,16},{16,0},{1,17},{17,1},{2,18},{18,2},{3,19},{19,3},{4,20},{20... | collective-permute-start | bytes 4718600 | tf_op jit(solution)/shard_map/ppermute | solution.py:853
  386.0 64.7 %copy-start.23 = (f32[8,768]{1,0:T(8,128)S(1)}, f32[8,768]{1,0:T(8,128)}, u32[]{:S(2)}) copy-start(f32[8,768]{1,0:T(8,128)} %get-tuple-element.95) | copy-start | bytes 73732
  449.8 6.1 %copy-start.22 = (f32[24,768]{1,0:T(8,128)S(1)}, f32[24,768]{1,0:T(8,128)}, u32[]{:S(2)}) copy-start(f32[24,768]{1,0:T(8,128)} %get-tuple-element.134) | copy-start | bytes 221188
  449.8 6.7 %copy-start.20 = (f32[24,3072]{1,0:T(8,128)S(1)}, f32[24,3072]{1,0:T(8,128)}, u32[]{:S(2)}) copy-start(f32[24,3072]{1,0:T(8,128)} %get-tuple-element.136) | copy-start | bytes 884740
  449.9 7.4 %copy-start.19 = (f32[96,768]{1,0:T(8,128)S(1)}, f32[96,768]{1,0:T(8,128)}, u32[]{:S(2)}) copy-start(f32[96,768]{1,0:T(8,128)} %get-tuple-element.137) | copy-start | bytes 884740
  (11 other events, 18.0 us)
Sparse Core Ops, SparseCore 0:
  10.3 109.7 all-gather.1

commit v4 on v3

--- a/solution.py
+++ b/solution.py
@@ -46,6 +46,212 @@
     return jnp.where(low, pltpu.roll(x, LANES - HD // 2, 1), pltpu.roll(x, HD // 2, 1))
 
 
+MESH = pl.DeviceIdType.MESH
+
+
+def partner(bit):
+    side, at = lax.axis_index("stream"), lax.axis_index("batch")
+    return (1 - side, at) if bit < 0 else (side, jnp.bitwise_xor(at, 1 << bit))
+
+
+def greet(others):
+    barrier = pltpu.get_barrier_semaphore()
+    for other in others:
+        pl.semaphore_signal(barrier, inc=1, device_id=other, device_id_type=MESH)
+    pl.semaphore_wait(barrier, len(others))
+
+
+def line_partners():
+    side, at = lax.axis_index("stream"), lax.axis_index("batch")
+    return [partner(-1)] + [(side, jnp.bitwise_xor(at, mask)) for mask in (1, 2, 4, 8, 12)]
+
+
+class LineGather:
+    SENDS = 29
+
+    def __init__(self, chunks, send_sems, recv_sems, local_sems):
+        self.chunks, self.send_sems, self.recv_sems, self.local_sems = chunks, send_sems, recv_sems, local_sems
+        self.side, self.at = lax.axis_index("stream"), lax.axis_index("batch")
+        self.z = lax.div(self.at, 4)
+
+    @staticmethod
+    def scratch(count):
+        return [
+            pltpu.SemaphoreType.DMA((count, LineGather.SENDS)),
+            pltpu.SemaphoreType.DMA((count, 16)),
+            pltpu.SemaphoreType.DMA((count,)),
+        ]
+
+    def copy(self, chunk, shard, target, number, own=False):
+        source, place = self.chunks[chunk]
+        return pltpu.make_async_remote_copy(
+            src_ref=source if own else place(shard),
+            dst_ref=place(shard),
+            send_sem=self.send_sems.at[chunk, number],
+            recv_sem=self.recv_sems.at[chunk, shard],
+            device_id=(self.side, target),
+            device_id_type=MESH,
+        )
+
+    def local(self, chunk):
+        source, place = self.chunks[chunk]
+        return pltpu.make_async_copy(source, place(self.at), self.local_sems.at[chunk])
+
+    def sends(self, phase):
+        at, z = self.at, self.z
+        across, core = jnp.bitwise_xor(at, 2), jnp.bitwise_xor(at, 1)
+        up, down = (at + 4, z < 3), (at - 4, z > 0)
+        other = jnp.bitwise_xor
+        if phase == 0:
+            yield None, at, [(*up, 0), (*down, 1), (across, None, 2), (core, None, 3)]
+        if 1 <= phase <= 3:
+            n = 4 + 6 * (phase - 1)
+            yield z >= phase, at - 4 * phase, [(*up, n), (across, None, n + 1), (core, None, n + 2)]
+            yield z + phase <= 3, at + 4 * phase, [(*down, n + 3), (across, None, n + 4), (core, None, n + 5)]
+        if phase == 1:
+            yield None, across, [(core, None, 22)]
+        if 2 <= phase <= 4:
+            d, n = phase - 1, 23 + 2 * (phase - 2)
+            yield z >= d, other(at - 4 * d, 2), [(core, None, n)]
+            yield z + d <= 3, other(at + 4 * d, 2), [(core, None, n + 1)]
+
+    def each(self, phase, act):
+        for when, shard, sends in self.sends(phase):
+
+            def run():
+                act(shard, None, None)
+                for target, whether, number in sends:
+                    if whether is None:
+                        act(shard, target, number)
+                    else:
+                        pl.when(whether)(lambda: act(shard, target, number))
+
+            if when is None:
+                run()
+            else:
+                pl.when(when)(run)
+
+    def phase(self, chunk, phase):
+        def act(shard, target, number):
+            if target is None:
+                if phase == 0:
+                    self.local(chunk).start()
+                else:
+                    self.copy(chunk, shard, self.at, 0).wait_recv()
+            else:
+                self.copy(chunk, shard, target, number, own=phase == 0).start()
+
+        self.each(phase, act)
+
+    def finish(self):
+        for chunk in range(len(self.chunks)):
+            for n in range(8):
+                shard = jnp.bitwise_xor(lax.rem(self.at, 2), 1) + 2 * n
+                self.copy(chunk, shard, self.at, 0).wait_recv()
+            self.local(chunk).wait()
+            for phase in range(5):
+
+                def act(shard, target, number):
+                    if target is not None:
+                        self.copy(chunk, shard, target, number, own=phase == 0).wait_send()
+
+                self.each(phase, act)
+
+
+class SlabSum:
+    def __init__(self, order, keep, send, got, sems, load=None):
+        self.order, self.keep, self.send, self.got, self.sems, self.load = (0, *order), keep, send, got, sems, load
+
+    @staticmethod
+    def scratch(slots, share, columns):
+        steps = slots.bit_length()
+        return [
+            *[pltpu.VMEM((max(slots >> n, 1), share, columns), bf16) for n in (0, *range(steps))],
+            pltpu.SemaphoreType.DMA((2 * steps + 1,)),
+        ]
+
+    def copy(self, step):
+        count = self.got[step].shape[0]
+        return pltpu.make_async_remote_copy(
+            src_ref=self.send if step == 0 else self.keep.at[pl.ds(count, count)],
+            dst_ref=self.got[step],
+            send_sem=self.sems.at[2 * step],
+            recv_sem=self.sems.at[2 * step + 1],
+            device_id=partner(self.order[step]),
+            device_id_type=MESH,
+        )
+
+    def loading(self):
+        return pltpu.make_async_copy(self.load, self.keep, self.sems.at[2 * len(self.order)])
+
+    def start(self):
+        self.copy(0).start()
+        if self.load is not None:
+            self.loading().start()
+
+    def step(self, step):
+        if step == 1 and self.load is not None:
+            self.loading().wait()
+        self.copy(step - 1).wait_recv()
+        got = self.got[step - 1]
+
+        @pl.loop(0, got.shape[0])
+        def _(n):
+            self.keep[n] = (self.keep[n].astype(f32) + got[n].astype(f32)).astype(bf16)
+
+        self.copy(step).start()
+
+    def finish(self, out_ref, columns=slice(None)):
+        last = len(self.order) - 1
+        self.copy(last).wait_recv()
+        out_ref[:, columns] = self.keep[0].astype(f32) + self.got[last][0].astype(f32)
+        for step in range(len(self.order)):
+            self.copy(step).wait_send()
+
+
+ALL = (-1, 0, 1, 2, 3)
+
+
+class GainSum:
+    def __init__(self, bits, held, got, sems):
+        self.bits, self.held, self.got, self.sems = bits, held, got, sems
+
+    @staticmethod
+    def scratch(bits, width):
+        steps = len(bits)
+        return [
+            pltpu.VMEM((steps, 8, width), f32),
+            pltpu.VMEM((steps, 8, width), f32),
+            pltpu.SemaphoreType.DMA((2 * steps,)),
+        ]
+
+    def copy(self, step):
+        return pltpu.make_async_remote_copy(
+            src_ref=self.held.at[step],
+            dst_ref=self.got.at[step],
+            send_sem=self.sems.at[2 * step],
+            recv_sem=self.sems.at[2 * step + 1],
+            device_id=partner(self.bits[step]),
+            device_id_type=MESH,
+        )
+
+    def start(self, value):
+        self.held[0] = value
+        self.copy(0).start()
+
+    def step(self, step):
+        self.copy(step - 1).wait_recv()
+        self.held[step] = self.held[step - 1] + self.got[step - 1]
+        self.copy(step).start()
+
+    def finish(self, out_ref):
+        last = len(self.bits) - 1
+        self.copy(last).wait_recv()
+        out_ref[...] = self.held[last] + self.got[last]
+        for step in range(len(self.bits)):
+            self.copy(step).wait_send()
+
+
 def row_specs(tile, width, half):
     own = pl.BlockSpec((None, None, tile, width), lambda i, s: (0, s[0], jnp.minimum(i, half - 1), 0))
     away = pl.BlockSpec((tile, width), lambda i, s: (jnp.maximum(i - half, 0), 0))
@@ -57,15 +263,21 @@
 
 
 def project_kernel(side_ref, own_ref, away_ref, gain_ref, w_ref, cos_ref, sin_ref, out_ref, hidden_ref, *, half):
-    x = read_rows(own_ref, away_ref, half).astype(f32)
+    width = own_ref.shape[-1]
+    project_tile(read_rows(own_ref, away_ref, half), gain_ref[...], lambda part: w_ref[:, part * width : (part + 1) * width],
+                 cos_ref, sin_ref, out_ref, hidden_ref)
+
+
+def project_tile(x, gain, weights, cos_ref, sin_ref, out_ref, hidden_ref):
+    x = x.astype(f32)
     width = x.shape[1]
     center = x - jnp.mean(x, axis=1, keepdims=True)
     spread = jnp.mean(center * center, axis=1, keepdims=True)
-    hidden = (center * lax.rsqrt(spread + 1e-5) * gain_ref[...].astype(f32)).astype(bf16)
+    hidden = (center * lax.rsqrt(spread + 1e-5) * gain.astype(f32)).astype(bf16)
     hidden_ref[...] = hidden
     cosine, sine = cos_ref[...], sin_ref[...]
     for part in range(3):
-        rows = mm(hidden, w_ref[:, part * width : (part + 1) * width])
+        rows = mm(hidden, weights(part))
         for pair in range(width // LANES):
             cols = slice(pair * LANES, (pair + 1) * LANES)
             field = rows[:, cols]
@@ -106,6 +318,117 @@
     )(side, own, away, gain, w, cosine, sine)
 
 
+def first_kernel(shard_ref, gain_ref, tokens_ref, own_ref, cos_ref, sin_ref, qkv_ref, hidden_ref, away_out, w_out, gains_out,
+                 w_all, away, rows, swap_sems, out_sems, send_sems, recv_sems, local_sems, *gain_scratch, half):
+    side, at = lax.axis_index("stream"), lax.axis_index("batch")
+    step = pl.program_id(0)
+    width = own_ref.shape[-1]
+    tile = own_ref.shape[-2]
+    swap = pltpu.make_async_remote_copy(
+        src_ref=tokens_ref.at[0, 1 - side],
+        dst_ref=away,
+        send_sem=swap_sems.at[0],
+        recv_sem=swap_sems.at[1],
+        device_id=(1 - side, at),
+        device_id_type=MESH,
+    )
+
+    def chunk(n):
+        cols = slice(n * width, (n + 1) * width)
+        return shard_ref.at[:, cols], lambda shard: w_all.at[shard, :, cols]
+
+    weights = LineGather([chunk(n) for n in range(3)], send_sems, recv_sems, local_sems)
+    gain = GainSum((0, 1, 2, 3), *gain_scratch)
+    keeps = [
+        pltpu.make_async_copy(w_all, w_out, out_sems.at[0]),
+        pltpu.make_async_copy(away, away_out, out_sems.at[1]),
+    ]
+
+    @pl.when(step == 0)
+    def _():
+        greet(line_partners())
+        swap.start()
+        gain.start(gain_ref[...])
+        for phase in range(5):
+            for n in range(3):
+                weights.phase(n, phase)
+            if 1 <= phase <= 3:
+                gain.step(phase)
+        gain.finish(gains_out)
+        weights.finish()
+        keeps[0].start()
+
+    @pl.when(step == half)
+    def _():
+        swap.wait()
+        keeps[1].start()
+
+    @pl.when(step < half)
+    def _():
+        rows[...] = own_ref[...]
+
+    @pl.when(step >= half)
+    def _():
+        rows[...] = away[pl.ds(pl.multiple_of((step - half) * tile, tile), tile), :]
+
+    project_tile(rows[...], gains_out[0:1, :], lambda part: w_all[:, :, part * width : (part + 1) * width].reshape(width, width),
+                 cos_ref, sin_ref, qkv_ref, hidden_ref)
+
+    @pl.when(step == pl.num_programs(0) - 1)
+    def _():
+        for keep in keeps:
+            keep.wait()
+
+
+def first(shard, gain, tokens, cosine, sine, tile=512):
+    _, _, length, width = tokens.shape
+    rows = shard.shape[0]
+    half = length // tile
+    anywhere = pl.BlockSpec(memory_space=pl.ANY)
+    table = pl.BlockSpec((tile, LANES), lambda i: (lax.rem(i, half), 0))
+    small = pl.BlockSpec((8, width), lambda i: (0, 0))
+    return pl.pallas_call(
+        functools.partial(first_kernel, half=half),
+        name="first",
+        grid=(2 * half,),
+        in_specs=[
+            anywhere,
+            small,
+            anywhere,
+            pl.BlockSpec((None, None, tile, width), lambda i: (0, lax.axis_index("stream"), jnp.minimum(i, half - 1), 0)),
+            table,
+            table,
+        ],
+        out_specs=[
+            pl.BlockSpec((3, tile, width), lambda i: (0, i, 0)),
+            pl.BlockSpec((tile, width), lambda i: (i, 0)),
+            anywhere,
+            anywhere,
+            small,
+        ],
+        out_shape=[
+            jax.ShapeDtypeStruct((3, 2 * length, width), bf16),
+            jax.ShapeDtypeStruct((2 * length, width), bf16),
+            jax.ShapeDtypeStruct((length, width), bf16),
+            jax.ShapeDtypeStruct((16, rows, 3 * width), bf16),
+            jax.ShapeDtypeStruct((8, width), f32),
+        ],
+        scratch_shapes=[
+            pltpu.VMEM((16, rows, 3 * width), bf16),
+            pltpu.VMEM((length, width), bf16),
+            pltpu.VMEM((tile, width), bf16),
+            pltpu.SemaphoreType.DMA((2,)),
+            pltpu.SemaphoreType.DMA((2,)),
+            *LineGather.scratch(3),
+            *GainSum.scratch((0, 1, 2, 3), width),
+        ],
+        compiler_params=pltpu.CompilerParams(vmem_limit_bytes=48 << 20, collective_id=0, has_side_effects=True),
+        cost_estimate=pl.CostEstimate(
+            flops=12 * length * width * width, bytes_accessed=length * width * 24 + 12 * width * width, transcendentals=0
+        ),
+    )(shard, gain, tokens, tokens, cosine, sine)
+
+
 def mask_tables(length, row_length):
     pos = jnp.arange(length)
     blk = (pos // BLOCK)[:, None]
@@ -122,10 +445,73 @@
     return lax.broadcasted_iota(jnp.int32, shape, 1) < HD
 
 
-def attend_kernel(side_ref, qkv_ref, cq_ref, nq_ref, mk_ref, dk_ref, out_ref, log_ref,
-                  qa, ka, kd, va, s_scr):
+def attend_gather_kernel(qkv_ref, cq_ref, nq_ref, mk_ref, dk_ref, wo_ref, wu_ref, wd_ref, grad_ref,
+                         out_ref, log_ref, wo_all, wu_all, wd_all, away_ref,
+                         qa, ka, kd, va, s_scr, swap_sems, send_sems, recv_sems, local_sems):
+    side, at = lax.axis_index("stream"), lax.axis_index("batch")
+    step = pl.program_id(0)
+    wide, tall = wu_ref.shape[1] // 2, wd_ref.shape[0] // 2
+
+    def columns(n):
+        cols = slice(n * wide, (n + 1) * wide)
+        return wu_ref.at[:, cols], lambda shard: wu_all.at[shard, :, cols]
+
+    def rows(n):
+        part = slice(n * tall, (n + 1) * tall)
+        return wd_ref.at[part, :], lambda shard: wd_all.at[shard, part, :]
+
+    chunks = [(wo_ref, lambda shard: wo_all.at[shard]), columns(0), columns(1), rows(0), rows(1)]
+    weights = LineGather(chunks, send_sems, recv_sems, local_sems)
+    swap = pltpu.make_async_remote_copy(
+        src_ref=grad_ref.at[0, 1 - side],
+        dst_ref=away_ref,
+        send_sem=swap_sems.at[0],
+        recv_sem=swap_sems.at[1],
+        device_id=(1 - side, at),
+        device_id_type=MESH,
+    )
+    slots = 2 * SLOT_STEPS
+    plan = [[] for _ in range(slots + 1)]
+    items = [(chunk, phase) for phase in range(1, 5) for chunk in range(5)]
+    for n, item in enumerate(items):
+        plan[min(1 + n * SLOT_RATE // 16, slots)].append(item)
+
+    @pl.when(step == 0)
+    def _():
+        greet(line_partners())
+        for chunk in range(5):
+            weights.phase(chunk, 0)
+        swap.start()
+
+    def pass_on(slot):
+        for now in range(SLOT_STEPS):
+            if plan[2 * now + slot]:
+
+                @pl.when(step == now)
+                def _():
+                    for item in plan[2 * now + slot]:
+                        weights.phase(*item)
+
+    pass_on(0)
+    attend_kernel(qkv_ref, cq_ref, nq_ref, mk_ref, dk_ref, out_ref, log_ref, qa, ka, kd, va, s_scr,
+                  between=lambda: pass_on(1))
+
+    @pl.when(step == pl.num_programs(0) - 1)
+    def _():
+        for item in plan[slots]:
+            weights.phase(*item)
+        weights.finish()
+        swap.wait()
+
+
+SLOT_STEPS = 6
+SLOT_RATE = 11
+
+
+def attend_kernel(qkv_ref, cq_ref, nq_ref, mk_ref, dk_ref, out_ref, log_ref,
+                  qa, ka, kd, va, s_scr, between=lambda: None):
     length = out_ref.shape[1]
-    clean = side_ref[0]
+    clean = lax.axis_index("stream")
     noisy = 1 - clean
     tiles = length // TILE
     low = low_lanes((length, LANES))
@@ -144,6 +530,8 @@
         va[0, head, HD:] = ones
         va[1, head, HD:] = ones
     for copy in range(2):
+        if copy:
+            between()
         where_to = clean if copy == 0 else noisy
         for tile in range(tiles):
             rows = slice(tile * TILE, (tile + 1) * TILE)
@@ -172,146 +560,50 @@
             out_ref[where_to, rows, :] = jnp.concatenate(parts, axis=0).T.astype(bf16)
 
 
-def attend(side, qkv, tables):
+def attend(qkv, tables, shards=None, grad=None):
     _, copies, length, width = qkv.shape
     pairs = width // LANES
-    table_spec = pl.BlockSpec((length, LANES), lambda i, s: (0, 0))
+    table_spec = pl.BlockSpec((length, LANES), lambda i: (0, 0), pipeline_mode=pl.Buffered(1))
+    more_in, more_shapes, more_scratch = [], [], []
+    body, params = attend_kernel, {}
+    if shards is not None:
+        assert pairs == SLOT_STEPS
+        body = attend_gather_kernel
+        params = dict(collective_id=3, has_side_effects=True)
+        more_in = [*shards, grad]
+        more_shapes = [jax.ShapeDtypeStruct((16, *shard.shape), bf16) for shard in shards]
+        more_shapes.append(jax.ShapeDtypeStruct((length, width), bf16))
+        more_scratch = [pltpu.SemaphoreType.DMA((2,)), *LineGather.scratch(5)]
+    anywhere = pl.BlockSpec(memory_space=pl.ANY)
     return pl.pallas_call(
-        attend_kernel,
+        body,
         name="attend",
-        grid_spec=pltpu.PrefetchScalarGridSpec(
-            num_scalar_prefetch=1,
-            grid=(pairs,),
-            in_specs=[pl.BlockSpec((3, copies, length, LANES), lambda i, s: (0, 0, 0, i))] + [table_spec] * 4,
-            out_specs=[
-                pl.BlockSpec((copies, length, LANES), lambda i, s: (0, 0, i)),
-                pl.BlockSpec((copies, 1, 2, length), lambda i, s: (0, i, 0, 0)),
-            ],
-            scratch_shapes=[
-                pltpu.VMEM((3, 2, length, LANES), bf16),
-                pltpu.VMEM((2, length, LANES), bf16),
-                pltpu.VMEM((2, length, LANES), bf16),
-                pltpu.VMEM((2, 2, HD + 16, length), bf16),
-                pltpu.VMEM((2, length + TILE, TILE), f32),
-            ],
-        ),
+        grid=(pairs,),
+        in_specs=[pl.BlockSpec((3, copies, length, LANES), lambda i: (0, 0, 0, i)), *[table_spec] * 4,
+                  *[anywhere] * len(more_in)],
+        out_specs=[
+            pl.BlockSpec((copies, length, LANES), lambda i: (0, 0, i)),
+            pl.BlockSpec((copies, 1, 2, length), lambda i: (0, i, 0, 0)),
+            *[anywhere] * len(more_in),
+        ],
+        scratch_shapes=[
+            pltpu.VMEM((3, 2, length, LANES), bf16),
+            pltpu.VMEM((2, length, LANES), bf16),
+            pltpu.VMEM((2, length, LANES), bf16),
+            pltpu.VMEM((2, 2, HD + 16, length), bf16),
+            pltpu.VMEM((2, length + TILE, TILE), f32),
+            *more_scratch,
+        ],
         out_shape=[
             jax.ShapeDtypeStruct((copies, length, width), bf16),
             jax.ShapeDtypeStruct((copies, pairs, 2, length), f32),
+            *more_shapes,
         ],
-        compiler_params=pltpu.CompilerParams(vmem_limit_bytes=48 << 20),
+        compiler_params=pltpu.CompilerParams(vmem_limit_bytes=48 << 20, **params),
         cost_estimate=pl.CostEstimate(
             flops=8 * length * length * width, bytes_accessed=16 * length * width, transcendentals=length * length * 12
         ),
-    )(side, qkv, *tables)
-
-
-MESH = pl.DeviceIdType.MESH
-
-
-def partner(bit):
-    side, at = lax.axis_index("stream"), lax.axis_index("batch")
-    return (1 - side, at) if bit < 0 else (side, jnp.bitwise_xor(at, 1 << bit))
-
-
-def greet(bits):
-    barrier = pltpu.get_barrier_semaphore()
-    for bit in bits:
-        pl.semaphore_signal(barrier, inc=1, device_id=partner(bit), device_id_type=MESH)
-    pl.semaphore_wait(barrier, len(bits))
-
-
-class SlabSum:
-    def __init__(self, order, keep, send, got, sems, load=None):
-        self.order, self.keep, self.send, self.got, self.sems, self.load = (0, *order), keep, send, got, sems, load
-
-    @staticmethod
-    def scratch(slots, share, columns):
-        steps = slots.bit_length()
-        return [
-            *[pltpu.VMEM((max(slots >> n, 1), share, columns), bf16) for n in (0, *range(steps))],
-            pltpu.SemaphoreType.DMA((2 * steps + 1,)),
-        ]
-
-    def copy(self, step):
-        count = self.got[step].shape[0]
-        return pltpu.make_async_remote_copy(
-            src_ref=self.send if step == 0 else self.keep.at[pl.ds(count, count)],
-            dst_ref=self.got[step],
-            send_sem=self.sems.at[2 * step],
-            recv_sem=self.sems.at[2 * step + 1],
-            device_id=partner(self.order[step]),
-            device_id_type=MESH,
-        )
-
-    def loading(self):
-        return pltpu.make_async_copy(self.load, self.keep, self.sems.at[2 * len(self.order)])
-
-    def start(self):
-        self.copy(0).start()
-        if self.load is not None:
-            self.loading().start()
-
-    def step(self, step):
-        if step == 1 and self.load is not None:
-            self.loading().wait()
-        self.copy(step - 1).wait_recv()
-        got = self.got[step - 1]
-
-        @pl.loop(0, got.shape[0])
-        def _(n):
-            self.keep[n] = (self.keep[n].astype(f32) + got[n].astype(f32)).astype(bf16)
-
-        self.copy(step).start()
-
-    def finish(self, out_ref, columns=slice(None)):
-        last = len(self.order) - 1
-        self.copy(last).wait_recv()
-        out_ref[:, columns] = self.keep[0].astype(f32) + self.got[last][0].astype(f32)
-        for step in range(len(self.order)):
-            self.copy(step).wait_send()
-
-
-class GainSum:
-    bits = (-1, 0, 1, 2, 3)
-
-    def __init__(self, held, got, sems):
-        self.held, self.got, self.sems = held, got, sems
-
-    @staticmethod
-    def scratch(width):
-        steps = len(GainSum.bits)
-        return [
-            pltpu.VMEM((steps, 8, width), f32),
-            pltpu.VMEM((steps, 8, width), f32),
-            pltpu.SemaphoreType.DMA((2 * steps,)),
-        ]
-
-    def copy(self, step):
-        return pltpu.make_async_remote_copy(
-            src_ref=self.held.at[step],
-            dst_ref=self.got.at[step],
-            send_sem=self.sems.at[2 * step],
-            recv_sem=self.sems.at[2 * step + 1],
-            device_id=partner(self.bits[step]),
-            device_id_type=MESH,
-        )
-
-    def start(self, value):
-        self.held[0] = value
-        self.copy(0).start()
-
-    def step(self, step):
-        self.copy(step - 1).wait_recv()
-        self.held[step] = self.held[step - 1] + self.got[step - 1]
-        self.copy(step).start()
-
-    def finish(self, out_ref):
-        last = len(self.bits) - 1
-        self.copy(last).wait_recv()
-        out_ref[...] = self.held[last] + self.got[last]
-        for step in range(len(self.bits)):
-            self.copy(step).wait_send()
+    )(qkv, *tables, *more_in)
 
 
 DOWN, UP, OUT = (-1, 1, 2, 3), (1, -1, 2, 3), (2, -1, 1, 3)
@@ -330,13 +622,13 @@
     for n, order in enumerate(orders):
         keep, *got, sems = refs[n * per : (n + 1) * per]
         sums.append(SlabSum(order, keep, pairs[2 * n + 1], got, sems, load=pairs[2 * n]))
-    gain = GainSum(*refs[-3:])
+    gain = GainSum(ALL, *refs[-3:])
     down, up, wo = sums
     step = pl.program_id(0)
 
     @pl.when(step == 0)
     def _():
-        greet(GainSum.bits)
+        greet([partner(bit) for bit in ALL])
         for one in sums:
             one.start()
         gain.start(gain_ref[...])
@@ -469,7 +761,7 @@
         more_specs.append(fixed((8, width)))
         more_shapes.append(jax.ShapeDtypeStruct((8, width), f32))
         more_out.append(fixed((8, width)))
-        more_scratch += GainSum.scratch(width)
+        more_scratch += GainSum.scratch(ALL, width)
     return pl.pallas_call(
         body,
         name="attend_back",
@@ -505,29 +797,23 @@
 ROOT = math.sqrt(2.0 / math.pi)
 
 
-def feed_kernel(side_ref, x_own, x_away, mixed_ref, g_own, g_away, gain_ref, rest_ref,
+def feed_kernel(side_ref, x_own, x_away, mixed_ref, g_own, g_away, gain_ref, wo_all, wu_all, wd_all,
                 out_own, out_away, act_ref, du_ref, h2_ref, dmid_ref, dbr_ref, dmix_ref, dgain_ref,
                 wo_ref, wu_ref, wd_ref, sems, *, half):
     groups, rows, width = wo_ref.shape
-    fold = wd_ref.shape[1]
-    ff = fold * width
-
-    def fetch(n):
-        cols = rest_ref.at[:, :, n * width : (n + 1) * width]
-        if n == 0:
-            into = wo_ref
-        elif n <= fold:
-            into = wu_ref.at[n - 1]
-        else:
-            into = wd_ref.at[:, n - 1 - fold]
-        return pltpu.make_async_copy(cols, into, sems.at[n])
+    fold = wu_ref.shape[0]
 
     @pl.when(pl.program_id(0) == 0)
     def _():
-        for n in range(1 + 2 * fold):
-            fetch(n).start()
-        for n in range(1 + 2 * fold):
-            fetch(n).wait()
+        copies = [pltpu.make_async_copy(wo_all, wo_ref, sems.at[0])]
+        for n in range(fold):
+            cols = wu_all.at[:, :, n * width : (n + 1) * width]
+            copies.append(pltpu.make_async_copy(cols, wu_ref.at[n], sems.at[1 + n]))
+        copies.append(pltpu.make_async_copy(wd_all, wd_ref, sems.at[1 + fold]))
+        for copy in copies:
+            copy.start()
+        for copy in copies:
+            copy.wait()
 
     def down(c):
         per = groups // fold
@@ -585,11 +871,10 @@
     dmix_ref[...] = mm_t(dbr, wo).astype(bf16)
 
 
-def feed(side, x_own, x_away, mixed, g_own, g_away, gain, rest, tile=512):
+def feed(side, x_own, x_away, mixed, g_own, g_away, gain, weights, tile=512):
     tokens, width = mixed.shape
-    groups, rows, columns = rest.shape
-    fold = (columns // width - 1) // 2
-    ff = fold * width
+    groups, rows, ff = weights[1].shape
+    fold = ff // width
     half = tokens // 2 // tile
     row = pl.BlockSpec((tile, width), lambda i, s: (i, 0))
     wide = pl.BlockSpec((tile, ff), lambda i, s: (i, 0))
@@ -604,13 +889,13 @@
         grid_spec=pltpu.PrefetchScalarGridSpec(
             num_scalar_prefetch=1,
             grid=(2 * half,),
-            in_specs=[own, away, row, own, away, keep((1, width)), pl.BlockSpec(memory_space=pl.ANY)],
+            in_specs=[own, away, row, own, away, keep((1, width)), *[pl.BlockSpec(memory_space=pl.ANY)] * 3],
             out_specs=[own, away, wide, wide, row, row, row, row, pl.BlockSpec((8, width), lambda i, s: (0, 0))],
             scratch_shapes=[
                 pltpu.VMEM((groups, rows, width), bf16),
                 pltpu.VMEM((fold, groups, rows, width), bf16),
-                pltpu.VMEM((groups, fold, rows, width), bf16),
-                pltpu.SemaphoreType.DMA((1 + 2 * fold,)),
+                pltpu.VMEM((groups, fold * rows, width), bf16),
+                pltpu.SemaphoreType.DMA((2 + fold,)),
             ],
         ),
         out_shape=[
@@ -629,7 +914,7 @@
             flops=tokens * width * (4 * width + 8 * ff), bytes_accessed=tokens * (width * 18 + ff * 4),
             transcendentals=tokens * ff
         ),
-    )(side, x_own, x_away, mixed, g_own, g_away, gain, rest)
+    )(side, x_own, x_away, mixed, g_own, g_away, gain, *weights)
 
 
 def arranged(slot, order):
@@ -727,13 +1012,13 @@
     for n, order in enumerate(QKV):
         send, keep, *got, sems = refs[n * per : (n + 1) * per]
         sums.append(SlabSum(order, keep, send, got, sems))
-    gain = GainSum(*refs[-3:])
+    gain = GainSum(ALL, *refs[-3:])
     me = lax.axis_index("stream") * lax.axis_size("batch") + lax.axis_index("batch")
     step = pl.program_id(0)
 
     @pl.when(step == 0)
     def _():
-        greet(GainSum.bits)
+        greet([partner(bit) for bit in ALL])
         gain.start(gain_ref[...])
 
     for n, one in enumerate(sums):
@@ -782,7 +1067,7 @@
                 fixed,
             ],
             out_specs=[pl.BlockSpec((share, 3 * width), lambda j: (0, 0), pipeline_mode=pl.Buffered(1)), fixed],
-            scratch_shapes=[pltpu.VMEM((2 * slots, share, width), f32), *scratch, *GainSum.scratch(width)],
+            scratch_shapes=[pltpu.VMEM((2 * slots, share, width), f32), *scratch, *GainSum.scratch(ALL, width)],
         ),
         out_shape=[jax.ShapeDtypeStruct((share, 3 * width), f32), jax.ShapeDtypeStruct((8, width), f32)],
         compiler_params=pltpu.CompilerParams(vmem_limit_bytes=60 << 20, collective_id=2, has_side_effects=True),
@@ -857,89 +1142,6 @@
     return lax.optimization_barrier((value, *others))[0]
 
 
-def gather_kernel(shard_ref, gain_ref, w_ref, gains_ref, local_sems, send_sems, recv_sems, *, plans):
-    side, me = lax.axis_index("stream"), lax.axis_index("batch")
-    bits = sorted(plans[0][2])
-    barrier = pltpu.get_barrier_semaphore()
-    for bit in bits:
-        pl.semaphore_signal(
-            barrier, inc=1, device_id=(side, jnp.bitwise_xor(me, 1 << bit)), device_id_type=pl.DeviceIdType.MESH
-        )
-    pl.semaphore_wait(barrier, len(bits))
-    sources, targets = [shard_ref, gain_ref], [w_ref, gains_ref]
-    local = [pltpu.make_async_copy(sources[n], targets[n].at[me], local_sems.at[n]) for n in range(2)]
-    for copy in local:
-        copy.start()
-
-    def copies(plan, step):
-        which, cols, order = plans[plan]
-        held = [0]
-        for bit in order[:step]:
-            held += [h ^ (1 << bit) for h in held]
-        done = []
-        for n, h in enumerate(held):
-            slab = jnp.bitwise_xor(me, h)
-            at = targets[which].at[slab, :, cols]
-            number = (1 << step) - 1 + n
-            done.append(
-                pltpu.make_async_remote_copy(
-                    src_ref=sources[which].at[:, cols] if h == 0 else at,
-                    dst_ref=at,
-                    send_sem=send_sems.at[plan, number],
-                    recv_sem=recv_sems.at[plan, number],
-                    device_id=(side, jnp.bitwise_xor(me, 1 << order[step])),
-                    device_id_type=pl.DeviceIdType.MESH,
-                )
-            )
-        return done
-
-    for step in range(len(bits)):
-        for plan in range(len(plans)):
-            if step:
-                for copy in copies(plan, step - 1):
-                    copy.wait_recv()
-            for copy in copies(plan, step):
-                copy.start()
-    for plan in range(len(plans)):
-        for copy in copies(plan, len(bits) - 1):
-            copy.wait_recv()
-    for plan in range(len(plans)):
-        for step in range(len(bits)):
-            for copy in copies(plan, step):
-                copy.wait_send()
-    for copy in local:
-        copy.wait()
-
-
-def gather(shard, gains):
-    peers = lax.axis_size("batch")
-    rows, columns = shard.shape
-    cut = columns // 1024 * 896
-    plans = (
-        (0, slice(0, cut), (3, 2, 1, 0)),
-        (0, slice(cut, columns), (1, 3, 2, 0)),
-        (1, slice(0, gains.shape[1]), (1, 3, 2, 0)),
-    )
-    anywhere = pl.BlockSpec(memory_space=pl.ANY)
-    return pl.pallas_call(
-        functools.partial(gather_kernel, plans=plans),
-        name="gather",
-        in_specs=[anywhere, anywhere],
-        out_specs=[anywhere, anywhere],
-        out_shape=[
-            jax.ShapeDtypeStruct((peers, rows, columns), bf16),
-            jax.ShapeDtypeStruct((peers, *gains.shape), bf16),
-        ],
-        scratch_shapes=[
-            pltpu.SemaphoreType.DMA((2,)),
-            pltpu.SemaphoreType.DMA((len(plans), peers - 1)),
-            pltpu.SemaphoreType.DMA((len(plans), peers - 1)),
-        ],
-        compiler_params=pltpu.CompilerParams(collective_id=0, has_side_effects=True),
-        cost_estimate=pl.CostEstimate(flops=0, bytes_accessed=8 * peers * rows * columns, transcendentals=0),
-    )(shard, gains)
-
-
 def shards(tokens, cotangent, lengths, ln1_gain, w_qkv, w_out, ln2_gain, w_up, w_down):
     side = lax.axis_index("stream")
     at = lax.axis_index("batch")
@@ -953,35 +1155,33 @@
     me = jnp.stack([index if small else 0 * index, side]).astype(jnp.int32)
     share = width // (2 * peers)
 
-    x_away = flip(lax.dynamic_index_in_dim(tokens[0], 1 - side, 0, False), -1)
-    g_away = flip(lax.dynamic_index_in_dim(cotangent[0], 1 - side, 0, False), -1)
+    cosine, sine = rotary_tables(length)
+    tables = mask_tables(length, jnp.take(lengths, side))
     if small:
         rows = width // peers
-        gains = jnp.zeros((16, LANES), bf16)
-        gains = gains.at[0, :rows].set(ln1_gain).at[1, :rows].set(ln2_gain)
-        w_qkv_all, gains = gather(w_qkv, gains)
+        gains = jnp.zeros((8, width), f32)
+        gains = lax.dynamic_update_slice(gains, jnp.stack([ln1_gain, ln2_gain]).astype(f32), (0, at * rows))
+        qkv, hidden, x_away, w_qkv_all, gains = first(w_qkv, gains, tokens, cosine, sine)
+        qkv4 = qkv.reshape(3, 2, length, width)
         w_qkv_all = w_qkv_all.reshape(width, 3 * width)
-        gain_one, gain_two = (gains[:, n, :rows].reshape(1, width) for n in range(2))
-        down = w_down.reshape(-1, rows, width).swapaxes(0, 1).reshape(rows, ff)
-        rest = lax.all_gather(jnp.concatenate([w_out, w_up, down], axis=1), "batch", axis=0, tiled=True)
-        rest = rest.reshape(peers, rows, -1)
+        gain_one, gain_two = gains[0:1], gains[1:2]
+        mixed, logs, *weights, g_away = attend(qkv4, tables, (w_out, w_up, w_down), cotangent)
     else:
+
         def whole(x):
             return lax.all_gather(x, "batch", axis=0, tiled=True)
 
+        x_away = flip(lax.dynamic_index_in_dim(tokens[0], 1 - side, 0, False), -1)
+        g_away = flip(lax.dynamic_index_in_dim(cotangent[0], 1 - side, 0, False), -1)
         w_qkv_all = whole(w_qkv)
-        gain_one, gain_two = whole(ln1_gain)[None], whole(ln2_gain)[None]
-        down = whole(w_down).reshape(16, -1, width // 16, width).swapaxes(1, 2).reshape(width, ff)
-        rest = jnp.concatenate([whole(w_out), whole(w_up), down], axis=1).reshape(16, width // 16, -1)
-
-    cosine, sine = rotary_tables(length)
-    tables = mask_tables(length, jnp.take(lengths, side))
-    qkv, hidden = project(side_array, tokens, x_away, gain_one, w_qkv_all, cosine, sine)
-    qkv4 = qkv.reshape(3, 2, length, width)
-    mixed, logs = attend(side_array, qkv4, tables)
+        gain_one, gain_two = (whole(gain)[None].astype(f32) for gain in (ln1_gain, ln2_gain))
+        weights = [whole(w).reshape(16, -1, w.shape[1]) for w in (w_out, w_up, w_down)]
+        qkv, hidden = project(side_array, tokens, x_away, gain_one, w_qkv_all, cosine, sine)
+        qkv4 = qkv.reshape(3, 2, length, width)
+        mixed, logs = attend(qkv4, tables)
     mixed2 = mixed.reshape(2 * length, width)
     out, out_away, act, du, h2, dmid, dbr, dmix, dgain_two = feed(
-        side_array, tokens, x_away, mixed2, cotangent, g_away, gain_two, rest
+        side_array, tokens, x_away, mixed2, cotangent, g_away, gain_two, weights
     )
 
     def place(result, away):

time: 472 us -> 437 us (0.926)
  between operations: 15.5 us -> 1.9 us
  Pallas kernels: 410 us -> 398 us
    pallas_call x3 -> x2, Pallas kernels: 131 us -> 116 us  [the longest x1 65.6 us: attend(): pl.pallas_call(body, name='attend', grid=(pairs,), in_specs=[pl.BlockSpec...]
    pallas_call x1, Pallas kernels: 95.2 us -> 102 us  [attend_back(): pl.pallas_call(body, name='attend_back', grid_spec=pltpu.PrefetchScalarGr...]
    unnamed x64 -> x62, local copies, waits for them, and re-layouts: 15.4 us -> 17.1 us
  transfers between devices with their start and end apart: 5 -> 2, of which waited for: 0 -> 0; matrix products, arithmetic and copies ran while one was open for 3% -> 1% of each run, Pallas kernels for 52% -> 24%
where the time goes in v4:
time: 437 us; the launch traced here: 434 us
  Pallas kernels  398 us (91%)
  local copies, waits for them, and re-layouts  23.4 us (5%)
  other arithmetic  9.08 us (2%)
    pallas_call x1, Pallas kernels, attend_back(): pl.pallas_call(body, name='attend_back', grid_spec=pltpu.PrefetchScalarGr...  102 us
    pallas_call x1, Pallas kernels, attend(): pl.pallas_call(body, name='attend', grid=(pairs,), in_specs=[pl.BlockSpec...  65.6 us
    pallas_call x1, Pallas kernels, feed(): pl.pallas_call(functools.partial(feed_kernel, half=half), name='feed', gr...  64.4 us
    pallas_call x1, Pallas kernels, qkv_grad(): pl.pallas_call(functools.partial(qkv_grad_kernel, share=share), name='gra...  60.5 us
    pallas_call x1, Pallas kernels, first(): pl.pallas_call(functools.partial(first_kernel, half=half), name='first',...  50.8 us
    pallas_call x2, Pallas kernels, weight_grad_columns(): pl.pallas_call(functools.partial(weight_kernel, share=share, split=False,...  20 us
    pallas_call x2, Pallas kernels, project_back(): pl.pallas_call(project_back_kernel, name='project_back_away' if away else...  19.3 us
    unnamed x62, local copies, waits for them, and re-layouts  17.1 us
  transfers between devices with their start and end apart: 2, of which 0 were waited for; matrix products, arithmetic and copies ran while one was open for 1% of the time, Pallas kernels for 24%

profile of v4, /device:TPU:0, one launch (start us, length us, event | category | flops | bytes accessed | tf_op | source)
XLA Modules:
  0.0 433.9 jit_solution(14368135591532384450)
XLA Ops:
  0.7 1.3 dynamic-slice.2
  4.2 1.9 fusion
  7.6 50.8 %first.1 = (bf16[3,2048,768]{2,1,0:T(8,128)(2,1)}, bf16[2048,768]{1,0:T(8,128)(2,1)S(1)}, bf16[1024,768]{1,0:T(8,128)(2,1)S(1)}, bf16[16,48,2304]{2,1,0:T(8,128)(2,1)}, f32[8,768]{1,0:T(8,128)S(1)}) custom-call(bf16[48,2304]{1,0:T(8,128)(2,1)S(1)} %copy-done.11, f32[8,768]{1,0:T(8,128)S(1)} %dynamic_update_slice.9.gain_ref, bf16[1,2,1024,768]{3,2,1,0:T(8,128)(2,1)} %x_ref.1, ...), custom_call_target="tpu_custom_call" | custom-call | flops 7247757312 | bytes 25952256 | tf_op jit(solution)/shard_map/first/pallas_call | solution.py:390
  58.4 1.2 copy-done.1
  59.6 1.6 copy-done.19
  61.8 65.6 %attend.1 = (bf16[2,1024,768]{2,1,0:T(8,128)(2,1)}, f32[2,6,2,1024]{3,2,1,0:T(2,128)S(1)}, bf16[16,48,768]{2,1,0:T(8,128)(2,1)S(1)}, bf16[16,48,3072]{2,1,0:T(8,...) custom-call(bf16[3,2,1024,768]{3,2,1,0:T(8,128)(2,1)} %bitcast.28, ...), custom_call_target="tpu_custom_call" | custom-call | flops 6442450944 | bytes 12582912 | tf_op jit(solution)/shard_map/attend/pallas_call | solution.py:578
  127.4 1.1 copy-done.17
  128.6 1.0 copy-done.20
  130.2 64.4 %feed.1 = (bf16[1,2,1024,768]{3,2,1,0:T(8,128)(2,1)}, bf16[1024,768]{1,0:T(8,128)(2,1)}, bf16[2048,3072]{1,0:T(8,128)(2,1)}, bf16[2048,3072]{1,0:T(8,128)(2,1)},...) custom-call(s32[1]{0:T(128)} %bitcast.side_ref, ...), custom_call_target="tpu_custom_call" | custom-call | flops 43486543872 | bytes 53477376 | tf_op jit(solution)/shard_map/feed/pallas_call | solution.py:886
  195.4 5.2 %grad_out.1 = (bf16[16,24,768]{2,1,0:T(8,128)(2,1)S(1)}, bf16[16,24,768]{2,1,0:T(8,128)(2,1)S(1)}) custom-call(s32[2]{0:T(128)S(1)} %pad_add_fusion.me_ref, bf16[2048,768]{1,0:T(8,128)(2,1)S(1)} %bitcast.19, bf16[2048,768]{1,0:T(8,128)(2,1)} %get-tuple-element.67.refs_0_), custom_call_target="tpu_custom_call" | custom-call | flops 2415919104 | bytes 7471104 | tf_op jit(solution)/shard_map/grad_out/pallas_call | solution.py:951
  202.3 1.4 copy-done.18
  203.7 15.1 %grad_down.1 = (bf16[2,4,2,96,768]{4,3,2,1,0:T(8,128)(2,1)S(1)}, bf16[2,4,2,96,768]{4,3,2,1,0:T(8,128)(2,1)}) custom-call(s32[2]{0:T(128)S(1)} %pad_add_fusion.me_ref, bf16[2048,3072]{1,0:T(8,128)(2,1)} %get-tuple-element.60.left_ref, bf16[1,2,1024,768]{3,2,1,0:T(8,128)(2,1)} %refs_0_.1, bf16[1024,768]{1,0:T(8,128)(2,1)S(1)} %copy-done.18), custom_call_target="tpu_custom_call" | custom-call | flops 9663676416 | bytes 20447232 | tf_op jit(solution)/shard_map/grad_down/pallas_call | solution.py:985
  218.8 1.4 copy-done.14
  220.2 14.8 %grad_up.1 = (bf16[16,24,3072]{2,1,0:T(8,128)(2,1)S(1)}, bf16[16,24,3072]{2,1,0:T(8,128)(2,1)S(1)}) custom-call(s32[2]{0:T(128)S(1)} %pad_add_fusion.me_ref, bf16[2048,768]{1,0:T(8,128)(2,1)} %get-tuple-element.63.left_ref, bf16[2048,3072]{1,0:T(8,128)(2,1)} %get-tuple-element.64.refs_0_), custom_call_target="tpu_custom_call" | custom-call | flops 9663676416 | bytes 20447232 | tf_op jit(solution)/shard_map/grad_up/pallas_call | solution.py:951
  235.0 1.4 copy-done.21
  236.4 1.4 copy-done.22
  237.8 2.7 bitcast_dynamic-update-slice_fusion
  240.5 101.8 %attend_back.1 = (bf16[3,2,1024,768]{3,2,1,0:T(8,128)(2,1)}, f32[96,768]{1,0:T(8,128)}, f32[24,3072]{1,0:T(8,128)}, f32[24,768]{1,0:T(8,128)}, f32[8,768]{1,0:T(8,128)}) custom-call(bf16[3,2,1024,768]{3,2,1,0:T(8,128)(2,1)} %bitcast.29, bf16[2,1024,768]{2,1,0:T(8,128)(2,1)} %get-tuple-element.48.refs_1_, bf16[2,1024,768]{2,1,0:T(8,128)(2,1)} %bitcast.30, ...), custom_call_target="tpu_custom_call" | custom-call | flops 16106127360 | bytes 23592960 | tf_op jit(solution)/shard_map/attend_back/pallas_call | solution.py:765
  342.3 1.4 copy-done.2
  343.7 9.6 %project_back_away.1 = (bf16[1024,768]{1,0:T(8,128)(2,1)}, f32[8,768]{1,0:T(8,128)S(1)}) custom-call(s32[1]{0:T(128)} %bitcast.side_ref, bf16[1024,768]{1,0:T(8,128)(2,1)S(1)} %copy-done.2, f32[1,768]{1,0:T(1,128)S(1)} %get-tuple-element.95.gain_ref, bf16[768,2304]{1,0:T(8,128)(2,1)} %bitcast.24, bf16[3,2048,768]{2,1,0:T(8,128)(2,1)} %bitcast.21, ...), custom_call_target="tpu_custom_call" | custom-call | flops 3623878656 | bytes 12582912 | tf_op jit(solution)/shard_map/project_back_away/pallas_call | solution.py:1113
  353.3 1.4 collective-permute-start.1
  354.7 9.7 %project_back_own.1 = (f32[1,2,1024,768]{3,2,1,0:T(8,128)}, f32[8,768]{1,0:T(8,128)S(1)}) custom-call(s32[1]{0:T(128)} %bitcast.side_ref, bf16[1,2,1024,768]{3,2,1,0:T(8,128)(2,1)S(1)} %copy-done, f32[1,768]{1,0:T(1,128)S(1)} %get-tuple-element.95.gain_ref, bf16[768,2304]{1,0:T(8,128)(2,1)} %bitcast.25, bf16[3,2048,768]{2,1,0:T(8,128)(2,1)} %bitcast.22, ...), custom_call_target="tpu_custom_call" | custom-call | flops 3623878656 | bytes 12582912 | tf_op jit(solution)/shard_map/project_back_own/pallas_call | solution.py:1113
  365.0 60.5 %grad_qkv.1 = (f32[24,2304]{1,0:T(8,128)}, f32[8,768]{1,0:T(8,128)}) custom-call(bf16[2048,768]{1,0:T(8,128)(2,1)} %copy-done.19, bf16[3,2048,768]{2,1,0:T(8,128)(2,1)} %bitcast.23, f32[8,768]{1,0:T(8,128)} %add.61.gain_ref), custom_call_target="tpu_custom_call" | custom-call | flops 7247757312 | bytes 12582912 | tf_op jit(solution)/shard_map/grad_qkv/pallas_call | solution.py:1058
  427.6 3.3 convert_dynamic-update-slice_fusion
  (74 shorter events, 12.0 us)
Async XLA Ops:
  0.6 6.9 %copy-start.11 = (bf16[48,2304]{1,0:T(8,128)(2,1)S(1)}, bf16[48,2304]{1,0:T(8,128)(2,1)}, u32[]{:S(2)}) copy-start(bf16[48,2304]{1,0:T(8,128)(2,1)} %shard_ref.1) | copy-start | bytes 663556
  3.0 58.8 %copy-start.5 = (bf16[1024,128]{1,0:T(8,128)(2,1)}, bf16[1024,128]{1,0:T(8,128)(2,1)S(1)}, u32[]{:S(2)}) copy-start(bf16[1024,128]{1,0:T(8,128)(2,1)S(1)} %get-tuple-element.97.dk_ref.refs_7_) | copy-start | bytes 786436
  3.0 58.8 %copy-start.6 = (bf16[1024,128]{1,0:T(8,128)(2,1)}, bf16[1024,128]{1,0:T(8,128)(2,1)S(1)}, u32[]{:S(2)}) copy-start(bf16[1024,128]{1,0:T(8,128)(2,1)S(1)} %get-tuple-element.98.mk_ref.refs_6_) | copy-start | bytes 786436
  3.4 58.4 %copy-start.7 = (bf16[1024,128]{1,0:T(8,128)(2,1)}, bf16[1024,128]{1,0:T(8,128)(2,1)S(1)}, u32[]{:S(2)}) copy-start(bf16[1024,128]{1,0:T(8,128)(2,1)S(1)} %get-tuple-element.102.nq_ref.refs_5_) | copy-start | bytes 786436
  3.4 58.4 %copy-start.8 = (bf16[1024,128]{1,0:T(8,128)(2,1)}, bf16[1024,128]{1,0:T(8,128)(2,1)S(1)}, u32[]{:S(2)}) copy-start(bf16[1024,128]{1,0:T(8,128)(2,1)S(1)} %get-tuple-element.103.cq_ref.refs_4_) | copy-start | bytes 786436
  7.5 50.8 %copy-start.3 = (f32[1024,128]{1,0:T(8,128)}, f32[1024,128]{1,0:T(8,128)S(1)}, u32[]{:S(2)}) copy-start(f32[1024,128]{1,0:T(8,128)S(1)} %get-tuple-element.104.cos_ref.refs_8_) | copy-start | bytes 1572868
  7.5 50.8 %copy-start.4 = (f32[1024,128]{1,0:T(8,128)}, f32[1024,128]{1,0:T(8,128)S(1)}, u32[]{:S(2)}) copy-start(f32[1024,128]{1,0:T(8,128)S(1)} %get-tuple-element.105.sin_ref.refs_9_) | copy-start | bytes 1572868
  7.5 54.3 %copy-start.9 = (bf16[48,3072]{1,0:T(8,128)(2,1)S(1)}, bf16[48,3072]{1,0:T(8,128)(2,1)}, u32[]{:S(2)}) copy-start(bf16[48,3072]{1,0:T(8,128)(2,1)} %wu_ref.1) | copy-start | bytes 884740
  7.5 54.3 %copy-start.10 = (bf16[192,768]{1,0:T(8,128)(2,1)S(1)}, bf16[192,768]{1,0:T(8,128)(2,1)}, u32[]{:S(2)}) copy-start(bf16[192,768]{1,0:T(8,128)(2,1)} %wd_ref.1) | copy-start | bytes 884740
  7.6 54.3 %copy-start.12 = (bf16[48,768]{1,0:T(8,128)(2,1)S(1)}, bf16[48,768]{1,0:T(8,128)(2,1)}, u32[]{:S(2)}) copy-start(bf16[48,768]{1,0:T(8,128)(2,1)} %wo_ref.1) | copy-start | bytes 221188
  59.6 1.6 copy-start.19
  130.2 65.2 %copy-start.13 = (bf16[2,1024,768]{2,1,0:T(8,128)(2,1)S(1)}, bf16[2,1024,768]{2,1,0:T(8,128)(2,1)}, u32[]{:S(2)}) copy-start(bf16[2,1024,768]{2,1,0:T(8,128)(2,1)} %get-tuple-element.48.refs_1_) | copy-start | bytes 9437188
  194.7 43.2 %collective-permute-start = (bf16[1024,768]{1,0:T(8,128)(2,1)}, bf16[1024,768]{1,0:T(8,128)(2,1)}, u32[]{:S(2)}, u32[]{:S(2)}) collective-permute-start(bf16[1024,768]{1,0:T(8,128)(2,1)} %get-tuple-element.55), channel_id=1, source_target_pairs={{0,16},{16,0},{1,17},{17,1},{2,18},{18,2},{3,19},{19,3},{4,20},{20... | collective-permute-start | bytes 4718600 | tf_op jit(solution)/shard_map/ppermute | solution.py:1138
  202.3 1.4 copy-start.18
  235.0 1.4 copy-start.21
  236.4 1.4 copy-start.22
  342.3 1.4 copy-start.2
  343.7 11.0 %copy-start = (bf16[1,2,1024,768]{3,2,1,0:T(8,128)(2,1)S(1)}, bf16[1,2,1024,768]{3,2,1,0:T(8,128)(2,1)}, u32[]{:S(2)}) copy-start(bf16[1,2,1024,768]{3,2,1,0:T(8,128)(2,1)} %x_ref.1) | copy-start | bytes 9437188
  353.3 74.4 %collective-permute-start.1 = (bf16[1024,768]{1,0:T(8,128)(2,1)}, bf16[1024,768]{1,0:T(8,128)(2,1)}, u32[]{:S(2)}, u32[]{:S(2)}) collective-permute-start(bf16[1024,768]{1,0:T(8,128)(2,1)} %get-tuple-element.74), channel_id=1, source_target_pairs={{0,16},{16,0},{1,17},{17,1},{2,18},{18,2},{3,19},{19,3},{4,20},{20... | collective-permute-start | bytes 4718600 | tf_op jit(solution)/shard_map/ppermute | solution.py:1138
  365.0 61.4 %copy-start.28 = (f32[8,768]{1,0:T(8,128)S(1)}, f32[8,768]{1,0:T(8,128)}, u32[]{:S(2)}) copy-start(f32[8,768]{1,0:T(8,128)} %get-tuple-element.81) | copy-start | bytes 73732
  425.6 5.4 %copy-start.26 = (f32[24,2304]{1,0:T(8,128)S(1)}, f32[24,2304]{1,0:T(8,128)}, u32[]{:S(2)}) copy-start(f32[24,2304]{1,0:T(8,128)} %get-tuple-element.119) | copy-start | bytes 663556
  425.6 6.1 %copy-start.27 = (f32[24,768]{1,0:T(8,128)S(1)}, f32[24,768]{1,0:T(8,128)}, u32[]{:S(2)}) copy-start(f32[24,768]{1,0:T(8,128)} %get-tuple-element.120) | copy-start | bytes 221188
  425.6 6.7 %copy-start.25 = (f32[24,3072]{1,0:T(8,128)S(1)}, f32[24,3072]{1,0:T(8,128)}, u32[]{:S(2)}) copy-start(f32[24,3072]{1,0:T(8,128)} %get-tuple-element.122) | copy-start | bytes 884740
  425.6 7.4 %copy-start.24 = (f32[96,768]{1,0:T(8,128)S(1)}, f32[96,768]{1,0:T(8,128)}, u32[]{:S(2)}) copy-start(f32[96,768]{1,0:T(8,128)} %get-tuple-element.123) | copy-start | bytes 884740
  (7 other events, 7.1 us)

commit v5 on v4

--- a/solution.py
+++ b/solution.py
@@ -201,15 +201,23 @@
 
         self.copy(step).start()
 
-    def finish(self, out_ref, columns=slice(None)):
+    def finish(self, out_ref, width, first=0):
         last = len(self.order) - 1
         self.copy(last).wait_recv()
-        out_ref[:, columns] = self.keep[0].astype(f32) + self.got[last][0].astype(f32)
+        total = self.keep[0].astype(f32) + self.got[last][0].astype(f32)
+        share = out_ref.shape[0]
+        by = total.shape[0] // share
+        block = out_ref.shape[1] if by == 1 else width // by
+        for n in range(total.shape[1] // block):
+            for i in range(by):
+                at = first + (n * by + i) * block
+                out_ref[:, at : at + block] = total[i * share : (i + 1) * share, n * block : (n + 1) * block]
         for step in range(len(self.order)):
             self.copy(step).wait_send()
 
 
 ALL = (-1, 0, 1, 2, 3)
+LATE = (0, 1, 2, 3, -1)
 
 
 class GainSum:
@@ -607,7 +615,7 @@
 
 
 DOWN, UP, OUT = (-1, 1, 2, 3), (1, -1, 2, 3), (2, -1, 1, 3)
-QKV = ((1, 2, 3, -1), (2, 1, 3, -1), (2, 3, 1, -1))
+QKV = ((1, 2, 3, -1), (2, 1, 3, -1), (1, 2, 3, -1))
 
 
 def attend_back_sum_kernel(*refs, orders):
@@ -651,7 +659,7 @@
     @pl.when(step == pl.num_programs(0) - 1)
     def _():
         for one, out_ref in zip(sums, outs):
-            one.finish(out_ref)
+            one.finish(out_ref, gain_ref.shape[1])
         gain.finish(gain_out)
 
 
@@ -733,7 +741,7 @@
     dqkv_ref[0, noisy] = finish(dq[1].T, True, 0.125)
 
 
-def attend_back(qkv, mixed, grad, logs, tables, cosine, sine, pairs=None, gain=None):
+def attend_back(qkv, mixed, grad, logs, tables, cosine, sine, pairs=None, gain=None, slabs=()):
     _, copies, length, width = qkv.shape
     steps = width // LANES
     table_spec = pl.BlockSpec((length, LANES), lambda i: (0, 0), pipeline_mode=pl.Buffered(1))
@@ -750,12 +758,12 @@
         assert steps == 6
         body = functools.partial(attend_back_sum_kernel, orders=(DOWN, UP, OUT))
         params = dict(collective_id=1, has_side_effects=True)
-        for keep, send in pairs:
+        for (keep, send), slab in zip(pairs, slabs):
             slots, share, columns = keep.shape
             more_in += [keep, send]
             more_specs += [anywhere] * 2
-            more_shapes.append(jax.ShapeDtypeStruct((share, columns), f32))
-            more_out.append(fixed((share, columns)))
+            more_shapes.append(jax.ShapeDtypeStruct(slab, f32))
+            more_out.append(fixed(slab))
             more_scratch += SlabSum.scratch(slots, share, columns)
         more_in.append(gain)
         more_specs.append(fixed((8, width)))
@@ -917,6 +925,17 @@
     )(side, x_own, x_away, mixed, g_own, g_away, gain, *weights)
 
 
+def folds(share):
+    return 1 if share % 16 == 0 else 2
+
+
+def fold(slab):
+    if folds(slab.shape[0]) == 1:
+        return slab
+    middle = slab.shape[1] // 2
+    return jnp.concatenate([slab[:, :middle], slab[:, middle:]], axis=0)
+
+
 def arranged(slot, order):
     return sum((slot >> bit & 1) << (len(order) - 1 - n) for n, bit in enumerate(order))
 
@@ -939,15 +958,16 @@
     for slot in range(slabs):
         source = jnp.bitwise_xor(low_me, slot)
         into = send_ref if slot % 2 else keep_ref
-        into[arranged(slot // 2, order)] = scr[source].astype(bf16)
+        into[arranged(slot // 2, order)] = fold(scr[source]).astype(bf16)
 
 
 def weight_grad_columns(me, left, right, block, share, order, name):
     tokens, dl = left.shape
     dr = right.shape[1]
     peers = dl // share
-    shape = (peers // 2, share, dr)
-    out = pl.BlockSpec((peers // 2, share, block), lambda j, m: (0, 0, j))
+    by = folds(share)
+    shape = (peers // 2, share * by, dr // by)
+    out = pl.BlockSpec((peers // 2, share * by, block // by), lambda j, m: (0, 0, j))
     return pl.pallas_call(
         functools.partial(weight_kernel, share=share, split=False, order=order),
         name=name,
@@ -1004,77 +1024,215 @@
     )(me, left, own, away)
 
 
-def qkv_grad_kernel(hidden_ref, dqkv_ref, gain_ref, out_ref, gain_out, scr, *refs, share):
+def last_kernel(x_own, x_away, gain_ref, w_hbm, dqkv_hbm, dmid_hbm, hidden_hbm,
+                dx_ref, dw_ref, gain_out,
+                xv, w_ref, dqkv, dmid, hidden, send, land, dgain, scr,
+                load_sems, tile_sems, send_sems, recv_sems, out_sems, *refs, share):
     count = len(QKV)
-    width = scr.shape[-1]
     per = len(refs[:-3]) // count
     sums = []
     for n, order in enumerate(QKV):
-        send, keep, *got, sems = refs[n * per : (n + 1) * per]
-        sums.append(SlabSum(order, keep, send, got, sems))
-    gain = GainSum(ALL, *refs[-3:])
-    me = lax.axis_index("stream") * lax.axis_size("batch") + lax.axis_index("batch")
+        first, keep, *got, sems = refs[n * per : (n + 1) * per]
+        sums.append(SlabSum(order, keep, first, got, sems))
+    gain = GainSum(LATE, *refs[-3:])
+    side, at = lax.axis_index("stream"), lax.axis_index("batch")
+    me = side * lax.axis_size("batch") + at
     step = pl.program_id(0)
+    width = w_ref.shape[0]
+    length = land.shape[0]
+    tiles = pl.num_programs(0)
+    tile = 2 * length // 8
+    half = 4
+
+    def rows_of(t, base=0):
+        return pl.ds(pl.multiple_of((t - base) * tile, tile), tile)
+
+    loads = [
+        pltpu.make_async_copy(w_hbm, w_ref, load_sems.at[0]),
+        pltpu.make_async_copy(x_away, xv.at[pl.ds(length, length)], load_sems.at[1]),
+        pltpu.make_async_copy(hidden_hbm, hidden, load_sems.at[2]),
+        pltpu.make_async_copy(x_own.at[0, side], xv.at[pl.ds(0, length)], load_sems.at[3]),
+    ]
+
+    def load_grad(t):
+        return pltpu.make_async_copy(dqkv_hbm.at[:, rows_of(t), :], dqkv.at[:, rows_of(t), :], tile_sems.at[0, t])
+
+    def load_middle(t):
+        return pltpu.make_async_copy(dmid_hbm.at[rows_of(t), :], dmid.at[rows_of(t), :], tile_sems.at[1, t])
+
+    def away(t):
+        return pltpu.make_async_remote_copy(
+            src_ref=send.at[rows_of(t, half), :],
+            dst_ref=land.at[rows_of(t, half), :],
+            send_sem=send_sems.at[t - half],
+            recv_sem=recv_sems.at[t - half],
+            device_id=(1 - side, at),
+            device_id_type=MESH,
+        )
+
+    def result(t, row):
+        return pltpu.make_async_copy(
+            dmid.at[rows_of(t), :],
+            dx_ref.at[0, row, pl.ds(pl.multiple_of(lax.rem(t, half) * tile, tile), tile), :],
+            out_sems.at[t],
+        )
 
     @pl.when(step == 0)
     def _():
+        loads[0].start()
+        loads[1].start()
+        load_grad(4).start()
+        load_middle(4).start()
+        loads[2].start()
+        for t in (5, 6, 7, 0, 1, 2, 3):
+            load_grad(t).start()
+        loads[3].start()
+        for t in (5, 6, 7, 0, 1, 2, 3):
+            load_middle(t).start()
+        dgain[...] = jnp.zeros_like(dgain)
         greet([partner(bit) for bit in ALL])
-        gain.start(gain_ref[...])
-
-    for n, one in enumerate(sums):
-
-        @pl.when(step == n)
+        loads[0].wait()
+        loads[1].wait()
+        load_grad(4).wait()
+        load_middle(4).wait()
+
+    @pl.when(step > 0)
+    def _():
+        load_middle(lax.rem(step + half, 8)).wait()
+
+    @pl.when(step == half)
+    def _():
+        loads[3].wait()
+
+    for now, plan in {
+        1: ((0, 1), (1, 1)),
+        2: ((0, 2), (2, 1)),
+        3: ((1, 2),),
+        4: ((0, 3),),
+        6: ((2, 2), (1, 3)),
+        7: ((0, 4),),
+    }.items():
+
+        @pl.when(step == now)
         def _():
-            weight_slabs(me, hidden_ref, dqkv_ref, one.keep, one.send, scr, share=share, split=False, order=tuple(
-                {-1: 3, 1: 0, 2: 1, 3: 2}[bit] for bit in QKV[n]
-            ))
-            one.start()
-            for earlier in range(n):
-                sums[earlier].step(n - earlier)
-            if n:
-                gain.step(n)
-
-    @pl.when(step == count - 1)
-    def _():
-        for number in range(2, 5 + count - 1):
-            for n, one in enumerate(sums):
-                now = number - n
-                if count - 1 - n < now < 5:
-                    one.step(now)
-            if count - 1 < number < 5:
-                gain.step(number)
-        for n, one in enumerate(sums):
-            one.finish(out_ref, slice(n * width, (n + 1) * width))
+            for n, number in plan:
+                sums[n].step(number)
+
+    t = lax.rem(step + half, 8)
+    rows = rows_of(t)
+    x = xv[rows, :].astype(f32)
+    center = x - jnp.mean(x, axis=1, keepdims=True)
+    spread = jnp.mean(center * center, axis=1, keepdims=True)
+    inv = lax.rsqrt(spread + 1e-5)
+    norm = center * inv
+    dh = mm_t(dqkv[0, rows, :], w_ref[:, :width])
+    dh = dh + mm_t(dqkv[1, rows, :], w_ref[:, width : 2 * width])
+    dh = dh + mm_t(dqkv[2, rows, :], w_ref[:, 2 * width :])
+    dgain[...] += jnp.sum((dh * norm).reshape(-1, 8, width), axis=0)
+    e = dh * gain_ref[...]
+    dx = dmid[rows, :] + inv * (
+        e - jnp.mean(e, axis=1, keepdims=True) - norm * jnp.mean(e * norm, axis=1, keepdims=True)
+    )
+
+    @pl.when(step < half)
+    def _():
+        send[rows_of(step), :] = dx.astype(bf16)
+        away(t).start()
+
+    @pl.when(step >= half)
+    def _():
+        dmid[rows, :] = dx
+        result(t, side).start()
+
+    def part(n):
+        order = tuple({-1: 3, 1: 0, 2: 1, 3: 2}[bit] for bit in QKV[n])
+        weight_slabs(me, hidden, dqkv.at[n], sums[n].keep, sums[n].send, scr, share=share, split=False, order=order)
+        sums[n].start()
+
+    @pl.when(step == 0)
+    def _():
+        loads[2].wait()
+        for other in (5, 6, 7, 0, 1, 2, 3):
+            load_grad(other).wait()
+        part(0)
+        part(1)
+
+    @pl.when(step == 1)
+    def _():
+        part(2)
+
+    @pl.when(step == tiles - 1)
+    def _():
+        gain.start(dgain[...])
+        sums[2].step(3)
+        sums[1].step(4)
+        sums[0].finish(dw_ref, width, 0)
+        gain.step(1)
+        sums[2].step(4)
+        gain.step(2)
+        sums[1].finish(dw_ref, width, width)
+        gain.step(3)
+        sums[2].finish(dw_ref, width, 2 * width)
+        gain.step(4)
+        for other in range(half, 8):
+            away(other).wait()
+            dmid[rows_of(other), :] = land[rows_of(other, half), :].astype(f32)
+            result(other, 1 - side).start()
         gain.finish(gain_out)
-
-
-def qkv_grad(hidden, dqkv, gain, share):
-    tokens, width = hidden.shape
+        for other in range(8):
+            result(other, side).wait()
+
+
+def last(tokens, x_away, gain, w, dqkv, dmid, hidden, share):
+    tokens_all, width = hidden.shape
+    length = tokens_all // 2
     slots = width // share // 2
-    fixed = pl.BlockSpec((8, width), lambda j: (0, 0), pipeline_mode=pl.Buffered(1))
+    anywhere = pl.BlockSpec(memory_space=pl.ANY)
+
+    def fixed(shape):
+        return pl.BlockSpec(shape, lambda i: (0, 0), pipeline_mode=pl.Buffered(1))
+
     scratch = []
     for _ in range(3):
-        scratch += [pltpu.VMEM((slots, share, width), bf16), *SlabSum.scratch(slots, share, width)]
+        by = folds(share)
+        scratch += [
+            pltpu.VMEM((slots, share * by, width // by), bf16),
+            *SlabSum.scratch(slots, share * by, width // by),
+        ]
     return pl.pallas_call(
-        functools.partial(qkv_grad_kernel, share=share),
-        name="grad_qkv",
-        grid_spec=pltpu.PrefetchScalarGridSpec(
-            num_scalar_prefetch=0,
-            grid=(3,),
-            in_specs=[
-                pl.BlockSpec((tokens, width), lambda j: (0, 0), pipeline_mode=pl.Buffered(1)),
-                pl.BlockSpec((None, tokens, width), lambda j: (j, 0, 0)),
-                fixed,
-            ],
-            out_specs=[pl.BlockSpec((share, 3 * width), lambda j: (0, 0), pipeline_mode=pl.Buffered(1)), fixed],
-            scratch_shapes=[pltpu.VMEM((2 * slots, share, width), f32), *scratch, *GainSum.scratch(ALL, width)],
+        functools.partial(last_kernel, share=share),
+        name="last",
+        grid=(8,),
+        in_specs=[anywhere, anywhere, fixed((1, width)), *[anywhere] * 4],
+        out_specs=[anywhere, fixed((share, 3 * width)), fixed((8, width))],
+        out_shape=[
+            jax.ShapeDtypeStruct((1, 2, length, width), f32),
+            jax.ShapeDtypeStruct((share, 3 * width), f32),
+            jax.ShapeDtypeStruct((8, width), f32),
+        ],
+        scratch_shapes=[
+            pltpu.VMEM((2 * length, width), bf16),
+            pltpu.VMEM((width, 3 * width), bf16),
+            pltpu.VMEM((3, 2 * length, width), bf16),
+            pltpu.VMEM((2 * length, width), f32),
+            pltpu.VMEM((2 * length, width), bf16),
+            pltpu.VMEM((length, width), bf16),
+            pltpu.VMEM((length, width), bf16),
+            pltpu.VMEM((8, width), f32),
+            pltpu.VMEM((2 * slots, share, width), f32),
+            pltpu.SemaphoreType.DMA((4,)),
+            pltpu.SemaphoreType.DMA((2, 8)),
+            pltpu.SemaphoreType.DMA((4,)),
+            pltpu.SemaphoreType.DMA((4,)),
+            pltpu.SemaphoreType.DMA((8,)),
+            *scratch,
+            *GainSum.scratch(LATE, width),
+        ],
+        compiler_params=pltpu.CompilerParams(vmem_limit_bytes=62 << 20, collective_id=2, has_side_effects=True),
+        cost_estimate=pl.CostEstimate(
+            flops=24 * length * width * width, bytes_accessed=36 * length * width, transcendentals=0
         ),
-        out_shape=[jax.ShapeDtypeStruct((share, 3 * width), f32), jax.ShapeDtypeStruct((8, width), f32)],
-        compiler_params=pltpu.CompilerParams(vmem_limit_bytes=60 << 20, collective_id=2, has_side_effects=True),
-        cost_estimate=pl.CostEstimate(
-            flops=6 * tokens * width * width, bytes_accessed=8 * tokens * width, transcendentals=0
-        ),
-    )(hidden, dqkv, gain)
+    )(tokens, x_away, gain, w, dqkv, dmid, hidden)
 
 
 def project_back_kernel(side_ref, x_ref, gain_ref, w_ref, dqkv_ref, dmid_ref, dx_ref, dgain_ref):
@@ -1202,23 +1360,29 @@
     dmix = after(dmix.reshape(2, length, width), out)
     common = qkv4, mixed, dmix, logs, tables, cosine, sine
     if small:
-        dqkv, down, up, wo, dgain_two = attend_back(*common, (down, up, wo), dgain_two)
+        dqkv, down, up, wo, dgain_two = attend_back(
+            *common, (down, up, wo), dgain_two, ((ff // width * share, width), (share, ff), (share, width))
+        )
     else:
         dqkv, = attend_back(*common)
     dqkv3 = dqkv.reshape(3, 2 * length, width)
-    dx_away, dgain_away = project_back(side_array, x_away, gain_one, w_qkv_all, dqkv3, dmid, True)
-    dx, dgain_own = project_back(side_array, tokens, gain_one, w_qkv_all, dqkv3, dmid, False)
-    dgain_one = dgain_own + dgain_away
     if small:
-        wq, dgain_one = qkv_grad(hidden, dqkv3, dgain_one, share)
-    dx = place(dx, dx_away)
+        dx, wq, dgain_one = last(tokens, x_away, gain_one, w_qkv_all, dqkv3, dmid, hidden, share)
+    else:
+        dx_away, dgain_away = project_back(side_array, x_away, gain_one, w_qkv_all, dqkv3, dmid, True)
+        dx, dgain_own = project_back(side_array, tokens, gain_one, w_qkv_all, dqkv3, dmid, False)
+        dgain_one = dgain_own + dgain_away
+        dx = place(dx, dx_away)
     dgain_one, dgain_two = (jnp.sum(g, axis=0, keepdims=True) for g in (dgain_one, dgain_two))
     if not small:
 
         def scatter(pair, order):
             slots = jnp.stack(pair, axis=1)
             natural = [arranged(n, order) for n in range(16)]
-            rows = slots[jnp.array(natural)].reshape(-1, slots.shape[-1])
+            slots = slots[jnp.array(natural)]
+            by = folds(unit) if slots.shape[2] == 2 * unit else 1
+            slots = slots.reshape(32, by, slots.shape[2] // by, -1, width // by).transpose(0, 2, 3, 1, 4)
+            rows = slots.reshape(32 * slots.shape[1], -1)
             return lax.psum_scatter(rows, ("stream", "batch"), scatter_dimension=0, tiled=True).astype(f32)
 
         parts = [columns_grad(hidden, dqkv3[n], QKV[n], "grad_qkv") for n in range(3)]

time: 437 us -> 415 us (0.950)
  Pallas kernels: 398 us -> 377 us
  local copies, waits for them, and re-layouts: 23.4 us -> 27.9 us
    pallas_call x3 -> x1, Pallas kernels: 79.9 us -> 58.4 us  [last(): pl.pallas_call(functools.partial(last_kernel, share=share), name='last',...]
    unnamed x62 -> x59, local copies, waits for them, and re-layouts: 17.1 us -> 21.7 us
  transfers between devices with their start and end apart: 2 -> 1, of which waited for: 0 -> 0; matrix products, arithmetic and copies ran while one was open for 1% -> 0% of each run, Pallas kernels for 24% -> 9%
where the time goes in v5:
time: 415 us; the launch traced here: 412 us
  Pallas kernels  377 us (91%)
  local copies, waits for them, and re-layouts  27.9 us (7%)
  other arithmetic  5.09 us (1%)
    pallas_call x1, Pallas kernels, attend_back(): pl.pallas_call(body, name='attend_back', grid_spec=pltpu.PrefetchScalarGr...  102 us
    pallas_call x1, Pallas kernels, attend(): pl.pallas_call(body, name='attend', grid=(pairs,), in_specs=[pl.BlockSpec...  65.6 us
    pallas_call x1, Pallas kernels, feed(): pl.pallas_call(functools.partial(feed_kernel, half=half), name='feed', gr...  64.6 us
    pallas_call x1, Pallas kernels, last(): pl.pallas_call(functools.partial(last_kernel, share=share), name='last',...  58.4 us
    pallas_call x1, Pallas kernels, first(): pl.pallas_call(functools.partial(first_kernel, half=half), name='first',...  50.8 us
    unnamed x59, local copies, waits for them, and re-layouts  21.7 us
    pallas_call x2, Pallas kernels, weight_grad_columns(): pl.pallas_call(functools.partial(weight_kernel, share=share, split=False,...  20.4 us
    pallas_call x1, Pallas kernels, weight_grad_rows(): pl.pallas_call(functools.partial(weight_kernel, share=share, split=True,...  15 us
  transfers between devices with their start and end apart: 1, of which 0 were waited for; matrix products, arithmetic and copies ran while one was open for 0% of the time, Pallas kernels for 9%

profile of v5, /device:TPU:0, one launch (start us, length us, event | category | flops | bytes accessed | tf_op | source)
XLA Modules:
  0.0 412.2 jit_solution(7230277105577417983)
XLA Ops:
  0.7 1.3 dynamic-slice.2
  3.4 0.8 maximum_convert_fusion
  4.2 1.9 fusion
  6.6 0.9 pad_maximum_fusion
  7.6 50.8 %first.1 = (bf16[3,2048,768]{2,1,0:T(8,128)(2,1)}, bf16[2048,768]{1,0:T(8,128)(2,1)S(1)}, bf16[1024,768]{1,0:T(8,128)(2,1)S(1)}, bf16[16,48,2304]{2,1,0:T(8,128)(2,1)}, f32[8,768]{1,0:T(8,128)S(1)}) custom-call(bf16[48,2304]{1,0:T(8,128)(2,1)S(1)} %copy-done.8, f32[8,768]{1,0:T(8,128)S(1)} %dynamic_update_slice.6.gain_ref, bf16[1,2,1024,768]{3,2,1,0:T(8,128)(2,1)} %x_own.3, ...), custom_call_target="tpu_custom_call" | custom-call | flops 7247757312 | bytes 25952256 | tf_op jit(solution)/shard_map/first/pallas_call | solution.py:398
  58.4 1.6 copy-done.17
  60.0 1.1 copy-done.20
  61.8 65.6 %attend.1 = (bf16[2,1024,768]{2,1,0:T(8,128)(2,1)}, f32[2,6,2,1024]{3,2,1,0:T(2,128)S(1)}, bf16[16,48,768]{2,1,0:T(8,128)(2,1)S(1)}, bf16[16,48,3072]{2,1,0:T(8,...) custom-call(bf16[3,2,1024,768]{3,2,1,0:T(8,128)(2,1)} %bitcast.20, ...), custom_call_target="tpu_custom_call" | custom-call | flops 6442450944 | bytes 12582912 | tf_op jit(solution)/shard_map/attend/pallas_call | solution.py:586
  127.4 1.2 copy-done.14
  128.6 1.0 copy-done.16
  130.3 64.6 %feed.1 = (bf16[1,2,1024,768]{3,2,1,0:T(8,128)(2,1)}, bf16[1024,768]{1,0:T(8,128)(2,1)}, bf16[2048,3072]{1,0:T(8,128)(2,1)}, bf16[2048,3072]{1,0:T(8,128)(2,1)},...) custom-call(s32[1]{0:T(128)} %bitcast.side_ref, ...), custom_call_target="tpu_custom_call" | custom-call | flops 43486543872 | bytes 53477376 | tf_op jit(solution)/shard_map/feed/pallas_call | solution.py:894
  195.7 5.2 %grad_out.1 = (bf16[16,48,384]{2,1,0:T(8,128)(2,1)S(1)}, bf16[16,48,384]{2,1,0:T(8,128)(2,1)S(1)}) custom-call(s32[2]{0:T(128)S(1)} %pad_add_fusion.me_ref, bf16[2048,768]{1,0:T(8,128)(2,1)S(1)} %bitcast.16, bf16[2048,768]{1,0:T(8,128)(2,1)} %get-tuple-element.64.refs_0_), custom_call_target="tpu_custom_call" | custom-call | flops 2415919104 | bytes 7471104 | tf_op jit(solution)/shard_map/grad_out/pallas_call | solution.py:971
  200.9 0.8 copy-done.12
  201.7 0.8 copy-done.13
  202.6 1.4 copy-done.15
  204.0 15.0 %grad_down.1 = (bf16[2,4,2,96,768]{4,3,2,1,0:T(8,128)(2,1)S(1)}, bf16[2,4,2,96,768]{4,3,2,1,0:T(8,128)(2,1)}) custom-call(s32[2]{0:T(128)S(1)} %pad_add_fusion.me_ref, bf16[2048,3072]{1,0:T(8,128)(2,1)} %get-tuple-element.57.left_ref, bf16[1,2,1024,768]{3,2,1,0:T(8,128)(2,1)} %refs_0_.1, bf16[1024,768]{1,0:T(8,128)(2,1)S(1)} %copy-done.15), custom_call_target="tpu_custom_call" | custom-call | flops 9663676416 | bytes 20447232 | tf_op jit(solution)/shard_map/grad_down/pallas_call | solution.py:1005
  219.0 1.4 copy-done.11
  220.4 15.2 %grad_up.1 = (bf16[16,48,1536]{2,1,0:T(8,128)(2,1)S(1)}, bf16[16,48,1536]{2,1,0:T(8,128)(2,1)S(1)}) custom-call(s32[2]{0:T(128)S(1)} %pad_add_fusion.me_ref, bf16[2048,768]{1,0:T(8,128)(2,1)} %get-tuple-element.60.left_ref, bf16[2048,3072]{1,0:T(8,128)(2,1)} %get-tuple-element.61.refs_0_), custom_call_target="tpu_custom_call" | custom-call | flops 9663676416 | bytes 20447232 | tf_op jit(solution)/shard_map/grad_up/pallas_call | solution.py:971
  235.6 1.4 copy-done.18
  237.0 1.4 copy-done.19
  238.4 2.7 bitcast_dynamic-update-slice_fusion
  241.1 101.7 %attend_back.1 = (bf16[3,2,1024,768]{3,2,1,0:T(8,128)(2,1)}, f32[96,768]{1,0:T(8,128)}, f32[24,3072]{1,0:T(8,128)}, f32[24,768]{1,0:T(8,128)}, f32[8,768]{1,0:T(8,128)}) custom-call(bf16[3,2,1024,768]{3,2,1,0:T(8,128)(2,1)} %bitcast.21, bf16[2,1024,768]{2,1,0:T(8,128)(2,1)} %get-tuple-element.45.refs_1_, bf16[2,1024,768]{2,1,0:T(8,128)(2,1)} %bitcast.24, ...), custom_call_target="tpu_custom_call" | custom-call | flops 16106127360 | bytes 23592960 | tf_op jit(solution)/shard_map/attend_back/pallas_call | solution.py:773
  342.8 58.4 %last.1 = (f32[1,2,1024,768]{3,2,1,0:T(8,128)}, f32[24,2304]{1,0:T(8,128)}, f32[8,768]{1,0:T(8,128)}) custom-call(bf16[1,2,1024,768]{3,2,1,0:T(8,128)(2,1)} %x_own.3, bf16[1024,768]{1,0:T(8,128)(2,1)} %copy-done.20, f32[1,768]{1,0:T(1,128)} %get-tuple-element.89.gain_ref, bf16[768,2304]{1,0:T(8,128)(2,1)} %bitcast.23, bf16[3,2048,768]{2,1,0:T(8,128)(2,1)} %bitcast.22, ...), custom_call_target="tpu_custom_call" | custom-call | flops 14495514624 | bytes 28311552 | tf_op jit(solution)/shard_map/last/pallas_call | solution.py:1202
  403.2 6.0 %copy.25 = f32[1,2,1024,768]{3,2,1,0:T(8,128)} copy(f32[1,2,1024,768]{3,2,1,0:T(8,128)} %get-tuple-element.111) | data formatting | bytes 12582912
  (65 shorter events, 8.0 us)
Async XLA Ops:
  0.6 6.9 %copy-start.8 = (bf16[48,2304]{1,0:T(8,128)(2,1)S(1)}, bf16[48,2304]{1,0:T(8,128)(2,1)}, u32[]{:S(2)}) copy-start(bf16[48,2304]{1,0:T(8,128)(2,1)} %shard_ref.1) | copy-start | bytes 663556
  3.0 58.8 %copy-start.2 = (bf16[1024,128]{1,0:T(8,128)(2,1)}, bf16[1024,128]{1,0:T(8,128)(2,1)S(1)}, u32[]{:S(2)}) copy-start(bf16[1024,128]{1,0:T(8,128)(2,1)S(1)} %get-tuple-element.91.dk_ref.refs_7_) | copy-start | bytes 786436
  3.0 58.8 %copy-start.3 = (bf16[1024,128]{1,0:T(8,128)(2,1)}, bf16[1024,128]{1,0:T(8,128)(2,1)S(1)}, u32[]{:S(2)}) copy-start(bf16[1024,128]{1,0:T(8,128)(2,1)S(1)} %get-tuple-element.92.mk_ref.refs_6_) | copy-start | bytes 786436
  3.4 58.4 %copy-start.4 = (bf16[1024,128]{1,0:T(8,128)(2,1)}, bf16[1024,128]{1,0:T(8,128)(2,1)S(1)}, u32[]{:S(2)}) copy-start(bf16[1024,128]{1,0:T(8,128)(2,1)S(1)} %get-tuple-element.96.nq_ref.refs_5_) | copy-start | bytes 786436
  3.4 58.4 %copy-start.5 = (bf16[1024,128]{1,0:T(8,128)(2,1)}, bf16[1024,128]{1,0:T(8,128)(2,1)S(1)}, u32[]{:S(2)}) copy-start(bf16[1024,128]{1,0:T(8,128)(2,1)S(1)} %get-tuple-element.97.cq_ref.refs_4_) | copy-start | bytes 786436
  7.5 50.8 %copy-start = (f32[1024,128]{1,0:T(8,128)}, f32[1024,128]{1,0:T(8,128)S(1)}, u32[]{:S(2)}) copy-start(f32[1024,128]{1,0:T(8,128)S(1)} %get-tuple-element.98.cos_ref.refs_8_) | copy-start | bytes 1572868
  7.5 50.8 %copy-start.1 = (f32[1024,128]{1,0:T(8,128)}, f32[1024,128]{1,0:T(8,128)S(1)}, u32[]{:S(2)}) copy-start(f32[1024,128]{1,0:T(8,128)S(1)} %get-tuple-element.99.sin_ref.refs_9_) | copy-start | bytes 1572868
  7.5 54.2 %copy-start.6 = (bf16[48,3072]{1,0:T(8,128)(2,1)S(1)}, bf16[48,3072]{1,0:T(8,128)(2,1)}, u32[]{:S(2)}) copy-start(bf16[48,3072]{1,0:T(8,128)(2,1)} %wu_ref.1) | copy-start | bytes 884740
  7.5 54.2 %copy-start.7 = (bf16[192,768]{1,0:T(8,128)(2,1)S(1)}, bf16[192,768]{1,0:T(8,128)(2,1)}, u32[]{:S(2)}) copy-start(bf16[192,768]{1,0:T(8,128)(2,1)} %wd_ref.1) | copy-start | bytes 884740
  7.6 54.2 %copy-start.9 = (bf16[48,768]{1,0:T(8,128)(2,1)S(1)}, bf16[48,768]{1,0:T(8,128)(2,1)}, u32[]{:S(2)}) copy-start(bf16[48,768]{1,0:T(8,128)(2,1)} %wo_ref.1) | copy-start | bytes 221188
  58.4 1.6 copy-start.17
  60.0 1.1 copy-start.20
  127.4 1.2 copy-start.14
  130.3 65.4 %copy-start.10 = (bf16[2,1024,768]{2,1,0:T(8,128)(2,1)S(1)}, bf16[2,1024,768]{2,1,0:T(8,128)(2,1)}, u32[]{:S(2)}) copy-start(bf16[2,1024,768]{2,1,0:T(8,128)(2,1)} %get-tuple-element.45.refs_1_) | copy-start | bytes 9437188
  194.9 43.5 %collective-permute-start = (bf16[1024,768]{1,0:T(8,128)(2,1)}, bf16[1024,768]{1,0:T(8,128)(2,1)}, u32[]{:S(2)}, u32[]{:S(2)}) collective-permute-start(bf16[1024,768]{1,0:T(8,128)(2,1)} %get-tuple-element.52), channel_id=1, source_target_pairs={{0,16},{16,0},{1,17},{17,1},{2,18},{18,2},{3,19},{19,3},{4,20},{20... | collective-permute-start | bytes 4718600 | tf_op jit(solution)/shard_map/ppermute | solution.py:1296
  202.6 1.4 copy-start.15
  219.0 1.4 copy-start.11
  235.6 1.4 copy-start.18
  237.0 1.4 copy-start.19
  342.8 59.2 %copy-start.26 = (f32[8,768]{1,0:T(8,128)S(1)}, f32[8,768]{1,0:T(8,128)}, u32[]{:S(2)}) copy-start(f32[8,768]{1,0:T(8,128)} %get-tuple-element.75) | copy-start | bytes 73732
  403.2 6.0 %copy-start.24 = (f32[24,2304]{1,0:T(8,128)S(1)}, f32[24,2304]{1,0:T(8,128)}, u32[]{:S(2)}) copy-start(f32[24,2304]{1,0:T(8,128)} %get-tuple-element.113) | copy-start | bytes 663556
  403.2 6.7 %copy-start.25 = (f32[24,768]{1,0:T(8,128)S(1)}, f32[24,768]{1,0:T(8,128)}, u32[]{:S(2)}) copy-start(f32[24,768]{1,0:T(8,128)} %get-tuple-element.114) | copy-start | bytes 221188
  403.2 7.3 %copy-start.23 = (f32[24,3072]{1,0:T(8,128)S(1)}, f32[24,3072]{1,0:T(8,128)}, u32[]{:S(2)}) copy-start(f32[24,3072]{1,0:T(8,128)} %get-tuple-element.116) | copy-start | bytes 884740
  403.2 8.0 %copy-start.22 = (f32[96,768]{1,0:T(8,128)S(1)}, f32[96,768]{1,0:T(8,128)}, u32[]{:S(2)}) copy-start(f32[96,768]{1,0:T(8,128)} %get-tuple-element.117) | copy-start | bytes 884740
  (4 other events, 3.3 us)

commit v6 on v5

--- a/solution.py
+++ b/solution.py
@@ -319,34 +319,39 @@
             ],
         ),
         out_shape=[jax.ShapeDtypeStruct((3, tokens, width), bf16), jax.ShapeDtypeStruct((tokens, width), bf16)],
-        compiler_params=pltpu.CompilerParams(vmem_limit_bytes=48 << 20),
+        compiler_params=pltpu.CompilerParams(vmem_limit_bytes=62 << 20),
         cost_estimate=pl.CostEstimate(
             flops=6 * tokens * width * width, bytes_accessed=tokens * width * 10 + 6 * width * width, transcendentals=0
         ),
     )(side, own, away, gain, w, cosine, sine)
 
 
-def first_kernel(shard_ref, gain_ref, tokens_ref, own_ref, cos_ref, sin_ref, qkv_ref, hidden_ref, away_out, w_out, gains_out,
-                 w_all, away, rows, swap_sems, out_sems, send_sems, recv_sems, local_sems, *gain_scratch, half):
+def first_kernel(shard_ref, wo_ref, wu_ref, gain_ref, tokens_ref, own_ref, cos_ref, sin_ref,
+                 qkv_ref, hidden_ref, away_out, w_out, wo_all, wu_all, gains_out,
+                 w_all, away, rows, swap_sems, out_sems, *refs, half):
     side, at = lax.axis_index("stream"), lax.axis_index("batch")
     step = pl.program_id(0)
     width = own_ref.shape[-1]
     tile = own_ref.shape[-2]
-    swap = pltpu.make_async_remote_copy(
-        src_ref=tokens_ref.at[0, 1 - side],
-        dst_ref=away,
-        send_sem=swap_sems.at[0],
-        recv_sem=swap_sems.at[1],
-        device_id=(1 - side, at),
-        device_id_type=MESH,
-    )
+    def swap(n):
+        part = pl.ds(n * tile, tile)
+        return pltpu.make_async_remote_copy(
+            src_ref=tokens_ref.at[0, 1 - side, part],
+            dst_ref=away.at[part],
+            send_sem=swap_sems.at[0, n],
+            recv_sem=swap_sems.at[1, n],
+            device_id=(1 - side, at),
+            device_id_type=MESH,
+        )
 
     def chunk(n):
         cols = slice(n * width, (n + 1) * width)
         return shard_ref.at[:, cols], lambda shard: w_all.at[shard, :, cols]
 
-    weights = LineGather([chunk(n) for n in range(3)], send_sems, recv_sems, local_sems)
-    gain = GainSum((0, 1, 2, 3), *gain_scratch)
+    weights = LineGather([chunk(n) for n in range(3)], *refs[:3])
+    part = wu_ref.at[:, : wu_all.shape[2]]
+    others = LineGather([(wo_ref, lambda shard: wo_all.at[shard]), (part, lambda shard: wu_all.at[shard])], *refs[3:6])
+    gain = GainSum((0, 1, 2, 3), *refs[6:])
     keeps = [
         pltpu.make_async_copy(w_all, w_out, out_sems.at[0]),
         pltpu.make_async_copy(away, away_out, out_sems.at[1]),
@@ -355,7 +360,8 @@
     @pl.when(step == 0)
     def _():
         greet(line_partners())
-        swap.start()
+        for n in range(half):
+            swap(n).start()
         gain.start(gain_ref[...])
         for phase in range(5):
             for n in range(3):
@@ -364,12 +370,20 @@
                 gain.step(phase)
         gain.finish(gains_out)
         weights.finish()
+        for n in range(2):
+            others.phase(n, 0)
         keeps[0].start()
 
-    @pl.when(step == half)
-    def _():
-        swap.wait()
-        keeps[1].start()
+    for now in range(1, 4):
+
+        @pl.when(step == now)
+        def _():
+            for n in range(2):
+                others.phase(n, now)
+            if now >= half:
+                swap(now - half).wait()
+            if now == 2 * half - 1:
+                keeps[1].start()
 
     @pl.when(step < half)
     def _():
@@ -384,14 +398,18 @@
 
     @pl.when(step == pl.num_programs(0) - 1)
     def _():
+        for n in range(2):
+            others.phase(n, 4)
+        others.finish()
         for keep in keeps:
             keep.wait()
 
 
-def first(shard, gain, tokens, cosine, sine, tile=512):
+def first(shard, wo, wu, cut, gain, tokens, cosine, sine, tile=512):
     _, _, length, width = tokens.shape
     rows = shard.shape[0]
     half = length // tile
+    assert half == 2
     anywhere = pl.BlockSpec(memory_space=pl.ANY)
     table = pl.BlockSpec((tile, LANES), lambda i: (lax.rem(i, half), 0))
     small = pl.BlockSpec((8, width), lambda i: (0, 0))
@@ -400,6 +418,8 @@
         name="first",
         grid=(2 * half,),
         in_specs=[
+            anywhere,
+            anywhere,
             anywhere,
             small,
             anywhere,
@@ -412,6 +432,8 @@
             pl.BlockSpec((tile, width), lambda i: (i, 0)),
             anywhere,
             anywhere,
+            anywhere,
+            anywhere,
             small,
         ],
         out_shape=[
@@ -419,22 +441,25 @@
             jax.ShapeDtypeStruct((2 * length, width), bf16),
             jax.ShapeDtypeStruct((length, width), bf16),
             jax.ShapeDtypeStruct((16, rows, 3 * width), bf16),
+            jax.ShapeDtypeStruct((16, rows, width), bf16),
+            jax.ShapeDtypeStruct((16, rows, cut), bf16),
             jax.ShapeDtypeStruct((8, width), f32),
         ],
         scratch_shapes=[
             pltpu.VMEM((16, rows, 3 * width), bf16),
             pltpu.VMEM((length, width), bf16),
             pltpu.VMEM((tile, width), bf16),
-            pltpu.SemaphoreType.DMA((2,)),
+            pltpu.SemaphoreType.DMA((2, half)),
             pltpu.SemaphoreType.DMA((2,)),
             *LineGather.scratch(3),
+            *LineGather.scratch(2),
             *GainSum.scratch((0, 1, 2, 3), width),
         ],
-        compiler_params=pltpu.CompilerParams(vmem_limit_bytes=48 << 20, collective_id=0, has_side_effects=True),
+        compiler_params=pltpu.CompilerParams(vmem_limit_bytes=62 << 20, collective_id=0, has_side_effects=True),
         cost_estimate=pl.CostEstimate(
             flops=12 * length * width * width, bytes_accessed=length * width * 24 + 12 * width * width, transcendentals=0
         ),
-    )(shard, gain, tokens, tokens, cosine, sine)
+    )(shard, wo, wu, gain, tokens, tokens, cosine, sine)
 
 
 def mask_tables(length, row_length):
@@ -453,22 +478,23 @@
     return lax.broadcasted_iota(jnp.int32, shape, 1) < HD
 
 
-def attend_gather_kernel(qkv_ref, cq_ref, nq_ref, mk_ref, dk_ref, wo_ref, wu_ref, wd_ref, grad_ref,
-                         out_ref, log_ref, wo_all, wu_all, wd_all, away_ref,
+def attend_gather_kernel(qkv_ref, cq_ref, nq_ref, mk_ref, dk_ref, wu_ref, wd_ref, grad_ref,
+                         out_ref, log_ref, wu_all, wd_all, away_ref,
                          qa, ka, kd, va, s_scr, swap_sems, send_sems, recv_sems, local_sems):
     side, at = lax.axis_index("stream"), lax.axis_index("batch")
     step = pl.program_id(0)
-    wide, tall = wu_ref.shape[1] // 2, wd_ref.shape[0] // 2
+    wide, tall = wu_all.shape[2] // 2, wd_ref.shape[0] // 2
+    cut = wu_ref.shape[1] - 2 * wide
 
     def columns(n):
         cols = slice(n * wide, (n + 1) * wide)
-        return wu_ref.at[:, cols], lambda shard: wu_all.at[shard, :, cols]
+        return wu_ref.at[:, cut + n * wide : cut + (n + 1) * wide], lambda shard: wu_all.at[shard, :, cols]
 
     def rows(n):
         part = slice(n * tall, (n + 1) * tall)
         return wd_ref.at[part, :], lambda shard: wd_all.at[shard, part, :]
 
-    chunks = [(wo_ref, lambda shard: wo_all.at[shard]), columns(0), columns(1), rows(0), rows(1)]
+    chunks = [columns(0), columns(1), rows(0), rows(1)]
     weights = LineGather(chunks, send_sems, recv_sems, local_sems)
     swap = pltpu.make_async_remote_copy(
         src_ref=grad_ref.at[0, 1 - side],
@@ -480,14 +506,14 @@
     )
     slots = 2 * SLOT_STEPS
     plan = [[] for _ in range(slots + 1)]
-    items = [(chunk, phase) for phase in range(1, 5) for chunk in range(5)]
+    items = [(chunk, phase) for phase in range(1, 5) for chunk in range(4)]
     for n, item in enumerate(items):
         plan[min(1 + n * SLOT_RATE // 16, slots)].append(item)
 
     @pl.when(step == 0)
     def _():
         greet(line_partners())
-        for chunk in range(5):
+        for chunk in range(4):
             weights.phase(chunk, 0)
         swap.start()
 
@@ -513,7 +539,7 @@
 
 
 SLOT_STEPS = 6
-SLOT_RATE = 11
+SLOT_RATE = 12
 
 
 def attend_kernel(qkv_ref, cq_ref, nq_ref, mk_ref, dk_ref, out_ref, log_ref,
@@ -568,7 +594,7 @@
             out_ref[where_to, rows, :] = jnp.concatenate(parts, axis=0).T.astype(bf16)
 
 
-def attend(qkv, tables, shards=None, grad=None):
+def attend(qkv, tables, shards=None, cut=0, grad=None):
     _, copies, length, width = qkv.shape
     pairs = width // LANES
     table_spec = pl.BlockSpec((length, LANES), lambda i: (0, 0), pipeline_mode=pl.Buffered(1))
@@ -579,9 +605,10 @@
         body = attend_gather_kernel
         params = dict(collective_id=3, has_side_effects=True)
         more_in = [*shards, grad]
-        more_shapes = [jax.ShapeDtypeStruct((16, *shard.shape), bf16) for shard in shards]
+        up, down = (shard.shape for shard in shards)
+        more_shapes = [jax.ShapeDtypeStruct(s, bf16) for s in ((16, up[0], up[1] - cut), (16, *down))]
         more_shapes.append(jax.ShapeDtypeStruct((length, width), bf16))
-        more_scratch = [pltpu.SemaphoreType.DMA((2,)), *LineGather.scratch(5)]
+        more_scratch = [pltpu.SemaphoreType.DMA((2,)), *LineGather.scratch(4)]
     anywhere = pl.BlockSpec(memory_space=pl.ANY)
     return pl.pallas_call(
         body,
@@ -592,7 +619,7 @@
         out_specs=[
             pl.BlockSpec((copies, length, LANES), lambda i: (0, 0, i)),
             pl.BlockSpec((copies, 1, 2, length), lambda i: (0, i, 0, 0)),
-            *[anywhere] * len(more_in),
+            *[anywhere] * len(more_shapes),
         ],
         scratch_shapes=[
             pltpu.VMEM((3, 2, length, LANES), bf16),
@@ -607,7 +634,7 @@
             jax.ShapeDtypeStruct((copies, pairs, 2, length), f32),
             *more_shapes,
         ],
-        compiler_params=pltpu.CompilerParams(vmem_limit_bytes=48 << 20, **params),
+        compiler_params=pltpu.CompilerParams(vmem_limit_bytes=62 << 20, **params),
         cost_estimate=pl.CostEstimate(
             flops=8 * length * length * width, bytes_accessed=16 * length * width, transcendentals=length * length * 12
         ),
@@ -689,29 +716,27 @@
                 kd[head] = jnp.where(pick, qkv_ref[1, at], dk_ref[...])
     cosine, sine = cos_ref[...], sin_ref[...]
 
-    def piece(copy, tile, query, keys, kv_copy, t, mask_first):
+    def piece(copy, tile, query, keys, kv_copy, krows):
         rows = slice(tile * TILE, (tile + 1) * TILE)
-        krows = slice(t * TILE, (t + 1) * TILE)
         kv_at = clean if kv_copy == 0 else noisy
         at = clean if copy == 0 else noisy
-        probs, raws = [], []
+        probs, raws, dqs = [], [], []
         for head in range(2):
             s = mm_t(keys[head, krows, :], qa[query, head, rows, :])
             p = jnp.exp(s - log_ref[at, 0, head : head + 1, rows])
-            if mask_first:
+            if kv_copy == 0 and copy == 1 and tile == 0:
                 first = lax.broadcasted_iota(jnp.int32, s.shape, 1) < BLOCK
                 p = jnp.where(first, 0.0, p)
             dp = mm_t(qkv_ref[2, kv_at, krows, :], doz[copy, head, rows, :])
             raw = (p * (dp - dsum[copy, head : head + 1, rows])).astype(bf16)
-            p = p.astype(bf16)
-            dq[copy, head * HD : (head + 1) * HD, rows] += mm(kt[kv_copy, head * HD : (head + 1) * HD, krows], raw)
-            probs.append(p)
+            dqs.append(mm(kt[kv_copy, head * HD : (head + 1) * HD, krows], raw))
+            probs.append(p.astype(bf16))
             raws.append(raw)
         p2 = jnp.concatenate(probs, axis=1)
         r2 = jnp.concatenate(raws, axis=1)
         do2 = jnp.concatenate([doz[copy, 0, rows, :], doz[copy, 1, rows, :]], axis=0)
         q2 = jnp.concatenate([qz[copy, 0, rows, :], qz[copy, 1, rows, :]], axis=0)
-        return mm(p2, do2), mm(r2, q2)
+        return jnp.concatenate(dqs, axis=0), mm(r2, q2), mm(p2, do2)
 
     def finish(field, rotate, scale):
         if rotate:
@@ -719,23 +744,29 @@
             field = field * c - half_partner(field) * s
         return (field * scale if scale != 1.0 else field).astype(bf16)
 
-    dq[...] = jnp.zeros_like(dq)
-    for t in range(tiles):
-        krows = slice(t * TILE, (t + 1) * TILE)
-        dv_t, dk_t = piece(1, t, 2, kd, 1, t, False)
-        dqkv_ref[2, noisy, krows, :] = dv_t.astype(bf16)
-        dkc[krows, :] = dk_t
+    for tile in range(tiles):
+        rows = slice(tile * TILE, (tile + 1) * TILE)
+        dq_t, dk_t, dv_t = piece(1, tile, 2, kd, 1, rows)
+        dq[1, :, rows] = dq_t
+        dkc[rows, :] = dk_t
+        dqkv_ref[2, noisy, rows, :] = dv_t.astype(bf16)
     dqkv_ref[1, noisy] = finish(dkc[...], True, 1.0)
-    for t in range(tiles):
-        krows = slice(t * TILE, (t + 1) * TILE)
-        dv_acc = dk_acc = None
-        for tile in range(t, tiles):
-            for copy in range(2):
-                dv_t, dk_t = piece(copy, tile, copy, ka, 0, t, copy == 1 and tile == 0)
-                dv_acc = dv_t if dv_acc is None else dv_acc + dv_t
-                dk_acc = dk_t if dk_acc is None else dk_acc + dk_t
-        dqkv_ref[2, clean, krows, :] = dv_acc.astype(bf16)
-        dkc[krows, :] = dk_acc
+    for tile in reversed(range(tiles)):
+        rows = slice(tile * TILE, (tile + 1) * TILE)
+        seen = slice(0, (tile + 1) * TILE)
+        for copy in range(2):
+            dq_t, dk_t, dv_t = piece(copy, tile, copy, ka, 0, seen)
+            if copy == 0:
+                dq[0, :, rows] = dq_t
+            else:
+                dq[1, :, rows] += dq_t
+            if copy == 0 and tile == tiles - 1:
+                dkc[...] = dk_t
+                dvc[...] = dv_t
+            else:
+                dkc[seen, :] += dk_t
+                dvc[seen, :] += dv_t
+    dqkv_ref[2, clean] = dvc[...].astype(bf16)
     dqkv_ref[1, clean] = finish(dkc[...], True, 1.0)
     dqkv_ref[0, clean] = finish(dq[0].T, True, 0.125)
     dqkv_ref[0, noisy] = finish(dq[1].T, True, 0.125)
@@ -795,7 +826,7 @@
             ],
         ),
         out_shape=[jax.ShapeDtypeStruct((3, copies, length, width), bf16), *more_shapes],
-        compiler_params=pltpu.CompilerParams(vmem_limit_bytes=60 << 20, **params),
+        compiler_params=pltpu.CompilerParams(vmem_limit_bytes=62 << 20, **params),
         cost_estimate=pl.CostEstimate(
             flops=20 * length * length * width, bytes_accessed=30 * length * width, transcendentals=length * length * 12
         ),
@@ -805,7 +836,7 @@
 ROOT = math.sqrt(2.0 / math.pi)
 
 
-def feed_kernel(side_ref, x_own, x_away, mixed_ref, g_own, g_away, gain_ref, wo_all, wu_all, wd_all,
+def feed_kernel(side_ref, x_own, x_away, mixed_ref, g_own, g_away, gain_ref, wo_all, wu_all, wu_more, wd_all,
                 out_own, out_away, act_ref, du_ref, h2_ref, dmid_ref, dbr_ref, dmix_ref, dgain_ref,
                 wo_ref, wu_ref, wd_ref, sems, *, half):
     groups, rows, width = wo_ref.shape
@@ -814,10 +845,21 @@
     @pl.when(pl.program_id(0) == 0)
     def _():
         copies = [pltpu.make_async_copy(wo_all, wo_ref, sems.at[0])]
-        for n in range(fold):
-            cols = wu_all.at[:, :, n * width : (n + 1) * width]
-            copies.append(pltpu.make_async_copy(cols, wu_ref.at[n], sems.at[1 + n]))
-        copies.append(pltpu.make_async_copy(wd_all, wd_ref, sems.at[1 + fold]))
+        begin = 0
+        for array in (wu_all, wu_more):
+            end = begin + array.shape[2]
+            for n in range(fold):
+                low, high = max(begin, n * width), min(end, (n + 1) * width)
+                if low < high:
+                    copies.append(
+                        pltpu.make_async_copy(
+                            array.at[:, :, low - begin : high - begin],
+                            wu_ref.at[n, :, :, low - n * width : high - n * width],
+                            sems.at[len(copies)],
+                        )
+                    )
+            begin = end
+        copies.append(pltpu.make_async_copy(wd_all, wd_ref, sems.at[len(copies)]))
         for copy in copies:
             copy.start()
         for copy in copies:
@@ -881,7 +923,8 @@
 
 def feed(side, x_own, x_away, mixed, g_own, g_away, gain, weights, tile=512):
     tokens, width = mixed.shape
-    groups, rows, ff = weights[1].shape
+    groups, rows, _ = weights[0].shape
+    ff = weights[1].shape[2] + weights[2].shape[2]
     fold = ff // width
     half = tokens // 2 // tile
     row = pl.BlockSpec((tile, width), lambda i, s: (i, 0))
@@ -897,13 +940,13 @@
         grid_spec=pltpu.PrefetchScalarGridSpec(
             num_scalar_prefetch=1,
             grid=(2 * half,),
-            in_specs=[own, away, row, own, away, keep((1, width)), *[pl.BlockSpec(memory_space=pl.ANY)] * 3],
+            in_specs=[own, away, row, own, away, keep((1, width)), *[pl.BlockSpec(memory_space=pl.ANY)] * 4],
             out_specs=[own, away, wide, wide, row, row, row, row, pl.BlockSpec((8, width), lambda i, s: (0, 0))],
             scratch_shapes=[
                 pltpu.VMEM((groups, rows, width), bf16),
                 pltpu.VMEM((fold, groups, rows, width), bf16),
                 pltpu.VMEM((groups, fold * rows, width), bf16),
-                pltpu.SemaphoreType.DMA((2 + fold,)),
+                pltpu.SemaphoreType.DMA((3 + fold,)),
             ],
         ),
         out_shape=[
@@ -917,7 +960,7 @@
             jax.ShapeDtypeStruct((tokens, width), bf16),
             jax.ShapeDtypeStruct((8, width), f32),
         ],
-        compiler_params=pltpu.CompilerParams(vmem_limit_bytes=60 << 20),
+        compiler_params=pltpu.CompilerParams(vmem_limit_bytes=62 << 20),
         cost_estimate=pl.CostEstimate(
             flops=tokens * width * (4 * width + 8 * ff), bytes_accessed=tokens * (width * 18 + ff * 4),
             transcendentals=tokens * ff
@@ -982,7 +1025,7 @@
             scratch_shapes=[pltpu.VMEM((peers, share, block), f32)],
         ),
         out_shape=[jax.ShapeDtypeStruct(shape, bf16)] * 2,
-        compiler_params=pltpu.CompilerParams(vmem_limit_bytes=48 << 20),
+        compiler_params=pltpu.CompilerParams(vmem_limit_bytes=62 << 20),
         cost_estimate=pl.CostEstimate(
             flops=2 * tokens * dl * dr, bytes_accessed=2 * tokens * (dl + dr) + 2 * dl * dr, transcendentals=0
         ),
@@ -1017,7 +1060,7 @@
             scratch_shapes=[pltpu.VMEM((slabs, share, dr), f32)],
         ),
         out_shape=[jax.ShapeDtypeStruct(shape, bf16)] * 2,
-        compiler_params=pltpu.CompilerParams(vmem_limit_bytes=48 << 20),
+        compiler_params=pltpu.CompilerParams(vmem_limit_bytes=62 << 20),
         cost_estimate=pl.CostEstimate(
             flops=2 * tokens * dl * dr, bytes_accessed=2 * tokens * (dl + dr) + 2 * dl * dr, transcendentals=0
         ),
@@ -1284,7 +1327,7 @@
             out_specs=[out_spec, pl.BlockSpec((8, width), lambda i, s: (0, 0))],
         ),
         out_shape=[out_shape, jax.ShapeDtypeStruct((8, width), f32)],
-        compiler_params=pltpu.CompilerParams(vmem_limit_bytes=48 << 20),
+        compiler_params=pltpu.CompilerParams(vmem_limit_bytes=62 << 20),
         cost_estimate=pl.CostEstimate(
             flops=6 * length * width * width, bytes_accessed=length * width * 16, transcendentals=0
         ),
@@ -1312,6 +1355,7 @@
     index = side * peers + at
     me = jnp.stack([index if small else 0 * index, side]).astype(jnp.int32)
     share = width // (2 * peers)
+    cut = ff // 3 // LANES * LANES
 
     cosine, sine = rotary_tables(length)
     tables = mask_tables(length, jnp.take(lengths, side))
@@ -1319,11 +1363,14 @@
         rows = width // peers
         gains = jnp.zeros((8, width), f32)
         gains = lax.dynamic_update_slice(gains, jnp.stack([ln1_gain, ln2_gain]).astype(f32), (0, at * rows))
-        qkv, hidden, x_away, w_qkv_all, gains = first(w_qkv, gains, tokens, cosine, sine)
+        qkv, hidden, x_away, w_qkv_all, wo_all, wu_all, gains = first(
+            w_qkv, w_out, w_up, cut, gains, tokens, cosine, sine
+        )
         qkv4 = qkv.reshape(3, 2, length, width)
         w_qkv_all = w_qkv_all.reshape(width, 3 * width)
         gain_one, gain_two = gains[0:1], gains[1:2]
-        mixed, logs, *weights, g_away = attend(qkv4, tables, (w_out, w_up, w_down), cotangent)
+        mixed, logs, wu_more, wd_all, g_away = attend(qkv4, tables, (w_up, w_down), cut, cotangent)
+        weights = [wo_all, wu_all, wu_more, wd_all]
     else:
 
         def whole(x):
@@ -1334,6 +1381,7 @@
         w_qkv_all = whole(w_qkv)
         gain_one, gain_two = (whole(gain)[None].astype(f32) for gain in (ln1_gain, ln2_gain))
         weights = [whole(w).reshape(16, -1, w.shape[1]) for w in (w_out, w_up, w_down)]
+        weights[1:2] = [weights[1][:, :, :cut], weights[1][:, :, cut:]]
         qkv, hidden = project(side_array, tokens, x_away, gain_one, w_qkv_all, cosine, sine)
         qkv4 = qkv.reshape(3, 2, length, width)
         mixed, logs = attend(qkv4, tables)

time: 415 us -> 397 us (0.957)
  local copies, waits for them, and re-layouts: 27.9 us -> 14.2 us
  Pallas kernels: 377 us -> 364 us
    unnamed x59 -> x17, local copies, waits for them, and re-layouts: 21.7 us -> 8.74 us
    pallas_call x1, Pallas kernels: 65.6 us -> 53.9 us  [attend(): pl.pallas_call(body, name='attend', grid=(pairs,), in_specs=[pl.BlockSpec...]
    pallas_call x1, Pallas kernels: 102 us -> 93.5 us  [attend_back(): pl.pallas_call(body, name='attend_back', grid_spec=pltpu.PrefetchScalarGr...]
  transfers between devices with their start and end apart: 1 -> 1, of which waited for: 0 -> 0; matrix products, arithmetic and copies ran while one was open for 0% -> 0% of each run, Pallas kernels for 9% -> 10%
where the time goes in v6:
time: 397 us; the launch traced here: 390 us
  Pallas kernels  364 us (92%)
  local copies, waits for them, and re-layouts  14.2 us (4%)
  other arithmetic  8.18 us (2%)
    pallas_call x1, Pallas kernels, attend_back(): pl.pallas_call(body, name='attend_back', grid_spec=pltpu.PrefetchScalarGr...  93.5 us
    pallas_call x1, Pallas kernels, feed(): pl.pallas_call(functools.partial(feed_kernel, half=half), name='feed', gr...  64.2 us
    pallas_call x1, Pallas kernels, last(): pl.pallas_call(functools.partial(last_kernel, share=share), name='last',...  60.7 us
    pallas_call x1, Pallas kernels, attend(): pl.pallas_call(body, name='attend', grid=(pairs,), in_specs=[pl.BlockSpec...  53.9 us
    pallas_call x1, Pallas kernels, first(): pl.pallas_call(functools.partial(first_kernel, half=half), name='first',...  53.5 us
    pallas_call x2, Pallas kernels, weight_grad_columns(): pl.pallas_call(functools.partial(weight_kernel, share=share, split=False,...  23 us
    pallas_call x1, Pallas kernels, weight_grad_rows(): pl.pallas_call(functools.partial(weight_kernel, share=share, split=True,...  15.7 us
    unnamed x17, local copies, waits for them, and re-layouts  8.74 us
  transfers between devices with their start and end apart: 1, of which 0 were waited for; matrix products, arithmetic and copies ran while one was open for 0% of the time, Pallas kernels for 10%

profile of v6, /device:TPU:0, one launch (start us, length us, event | category | flops | bytes accessed | tf_op | source)
XLA Modules:
  0.0 390.1 jit_solution(3225025782699754260)
XLA Ops:
  0.7 1.2 dynamic-slice.2
  2.6 1.1 select_convert_fusion
  3.7 1.1 compare_convert_fusion
  4.9 0.7 maximum_convert_fusion
  5.5 1.9 fusion
  7.9 1.9 pad_maximum_fusion
  9.7 53.5 %first.1 = (bf16[3,2048,768]{2,1,0:T(8,128)(2,1)}, bf16[2048,768]{1,0:T(8,128)(2,1)}, bf16[1024,768]{1,0:T(8,128)(2,1)}, bf16[16,48,2304]{2,1,0:T(8,128)(2,1)}, ...) custom-call(bf16[48,2304]{1,0:T(8,128)(2,1)} %shard_ref.1, bf16[48,768]{1,0:T(8,128)(2,1)} %wo_ref.1, ...), custom_call_target="tpu_custom_call" | custom-call | flops 7247757312 | bytes 25952256 | tf_op jit(solution)/shard_map/first/pallas_call | solution.py:416
  63.3 1.4 fusion.4
  64.7 53.9 %attend.1 = (bf16[2,1024,768]{2,1,0:T(8,128)(2,1)}, f32[2,6,2,1024]{3,2,1,0:T(2,128)}, bf16[16,48,2048]{2,1,0:T(8,128)(2,1)}, bf16[16,192,768]{2,1,0:T(8,128)(2,1)}, bf16[1024,768]{1,0:T(8,128)(2,1)}) custom-call(bf16[3,2,1024,768]{3,2,1,0:T(8,128)(2,1)} %bitcast.17, bf16[1024,128]{1,0:T(8,128)(2,1)} %get-tuple-element.99.cq_ref.refs_4_, ...), custom_call_target="tpu_custom_call" | custom-call | flops 6442450944 | bytes 12582912 | tf_op jit(solution)/shard_map/attend/pallas_call | solution.py:613
  118.5 64.2 %feed.1 = (bf16[1,2,1024,768]{3,2,1,0:T(8,128)(2,1)}, bf16[1024,768]{1,0:T(8,128)(2,1)}, bf16[2048,3072]{1,0:T(8,128)(2,1)}, bf16[2048,3072]{1,0:T(8,128)(2,1)},...) custom-call(s32[1]{0:T(128)} %bitcast.side_ref, ...), custom_call_target="tpu_custom_call" | custom-call | flops 43486543872 | bytes 53477376 | tf_op jit(solution)/shard_map/feed/pallas_call | solution.py:937
  182.8 1.6 collective-permute-start
  184.4 0.7 pad_add_fusion.me_ref
  185.0 7.2 %grad_out.1 = (bf16[16,48,384]{2,1,0:T(8,128)(2,1)}, bf16[16,48,384]{2,1,0:T(8,128)(2,1)}) custom-call(s32[2]{0:T(128)} %pad_add_fusion.me_ref, bf16[2048,768]{1,0:T(8,128)(2,1)} %bitcast.22, bf16[2048,768]{1,0:T(8,128)(2,1)} %get-tuple-element.66.refs_0_), custom_call_target="tpu_custom_call" | custom-call | flops 2415919104 | bytes 7471104 | tf_op jit(solution)/shard_map/grad_out/pallas_call | solution.py:1014
  192.2 15.7 %grad_down.1 = (bf16[2,4,2,96,768]{4,3,2,1,0:T(8,128)(2,1)}, bf16[2,4,2,96,768]{4,3,2,1,0:T(8,128)(2,1)}) custom-call(s32[2]{0:T(128)} %pad_add_fusion.me_ref, bf16[2048,3072]{1,0:T(8,128)(2,1)} %get-tuple-element.59.left_ref, bf16[1,2,1024,768]{3,2,1,0:T(8,128)(2,1)} %refs_0_.1, bf16[1024,768]{1,0:T(8,128)(2,1)} %get-tuple-element.47.g_away.refs_1_), custom_call_target="tpu_custom_call" | custom-call | flops 9663676416 | bytes 20447232 | tf_op jit(solution)/shard_map/grad_down/pallas_call | solution.py:1048
  207.9 15.8 %grad_up.1 = (bf16[16,48,1536]{2,1,0:T(8,128)(2,1)}, bf16[16,48,1536]{2,1,0:T(8,128)(2,1)}) custom-call(s32[2]{0:T(128)} %pad_add_fusion.me_ref, bf16[2048,768]{1,0:T(8,128)(2,1)} %get-tuple-element.62.left_ref, bf16[2048,3072]{1,0:T(8,128)(2,1)} %get-tuple-element.63.refs_0_), custom_call_target="tpu_custom_call" | custom-call | flops 9663676416 | bytes 20447232 | tf_op jit(solution)/shard_map/grad_up/pallas_call | solution.py:1014
  223.8 1.2 bitcast_dynamic-update-slice_fusion
  225.0 93.5 %attend_back.1 = (bf16[3,2,1024,768]{3,2,1,0:T(8,128)(2,1)}, f32[96,768]{1,0:T(8,128)}, f32[24,3072]{1,0:T(8,128)}, f32[24,768]{1,0:T(8,128)}, f32[8,768]{1,0:T(8,128)}) custom-call(bf16[3,2,1024,768]{3,2,1,0:T(8,128)(2,1)} %bitcast.18, bf16[2,1024,768]{2,1,0:T(8,128)(2,1)} %get-tuple-element.46.refs_1_, bf16[2,1024,768]{2,1,0:T(8,128)(2,1)} %bitcast.23, ...), custom_call_target="tpu_custom_call" | custom-call | flops 16106127360 | bytes 23592960 | tf_op jit(solution)/shard_map/attend_back/pallas_call | solution.py:804
  318.5 60.7 %last.1 = (f32[1,2,1024,768]{3,2,1,0:T(8,128)}, f32[24,2304]{1,0:T(8,128)}, f32[8,768]{1,0:T(8,128)}) custom-call(bf16[1,2,1024,768]{3,2,1,0:T(8,128)(2,1)} %x_own.3, bf16[1024,768]{1,0:T(8,128)(2,1)} %get-tuple-element.44.x_away, f32[1,768]{1,0:T(1,128)} %get-tuple-element.91.gain_ref, bf16[768,2304]{1,0:T(8,128)(2,1)} %bitcast.20, ...), custom_call_target="tpu_custom_call" | custom-call | flops 14495514624 | bytes 28311552 | tf_op jit(solution)/shard_map/last/pallas_call | solution.py:1245
  379.2 0.8 reduce_sum.18
  381.2 6.0 %copy.25 = f32[1,2,1024,768]{3,2,1,0:T(8,128)} copy(f32[1,2,1024,768]{3,2,1,0:T(8,128)} %get-tuple-element.113) | data formatting | bytes 12582912
  387.1 0.7 copy.26
  387.8 0.6 copy.27
  388.5 0.7 copy.28
  389.2 0.7 copy.29
  (23 shorter events, 1.6 us)
Async XLA Ops:
  7.8 1.9 copy-start.5
  182.8 41.0 %collective-permute-start = (bf16[1024,768]{1,0:T(8,128)(2,1)}, bf16[1024,768]{1,0:T(8,128)(2,1)S(1)}, u32[]{:S(2)}, u32[]{:S(2)}) collective-permute-start(bf16[1024,768]{1,0:T(8,128)(2,1)} %get-tuple-element.54), channel_id=1, source_target_pairs={{0,16},{16,0},{1,17},{17,1},{2,18},{18,2},{3,19},{19,3},{4,20},{20... | collective-permute-start | bytes 4718600 | tf_op jit(solution)/shard_map/ppermute | solution.py:1339
  318.5 61.4 %copy-start.4 = (f32[8,768]{1,0:T(8,128)S(1)}, f32[8,768]{1,0:T(8,128)}, u32[]{:S(2)}) copy-start(f32[8,768]{1,0:T(8,128)} %get-tuple-element.77) | copy-start | bytes 73732
  381.1 6.0 %copy-start.2 = (f32[24,2304]{1,0:T(8,128)S(1)}, f32[24,2304]{1,0:T(8,128)}, u32[]{:S(2)}) copy-start(f32[24,2304]{1,0:T(8,128)} %get-tuple-element.115) | copy-start | bytes 663556
  381.1 6.7 %copy-start.3 = (f32[24,768]{1,0:T(8,128)S(1)}, f32[24,768]{1,0:T(8,128)}, u32[]{:S(2)}) copy-start(f32[24,768]{1,0:T(8,128)} %get-tuple-element.116) | copy-start | bytes 221188
  381.1 7.3 %copy-start.1 = (f32[24,3072]{1,0:T(8,128)S(1)}, f32[24,3072]{1,0:T(8,128)}, u32[]{:S(2)}) copy-start(f32[24,3072]{1,0:T(8,128)} %get-tuple-element.118) | copy-start | bytes 884740
  381.1 8.0 %copy-start = (f32[96,768]{1,0:T(8,128)S(1)}, f32[96,768]{1,0:T(8,128)}, u32[]{:S(2)}) copy-start(f32[96,768]{1,0:T(8,128)} %get-tuple-element.119) | copy-start | bytes 884740

commit v7 on v6

--- a/solution.py
+++ b/solution.py
@@ -67,9 +67,10 @@
 
 
 class LineGather:
-    SENDS = 29
-
-    def __init__(self, chunks, send_sems, recv_sems, local_sems):
+    SENDS = 37
+
+    def __init__(self, chunks, send_sems, recv_sems, local_sems, across_first=()):
+        self.across_first = across_first
         self.chunks, self.send_sems, self.recv_sems, self.local_sems = chunks, send_sems, recv_sems, local_sems
         self.side, self.at = lax.axis_index("stream"), lax.axis_index("batch")
         self.z = lax.div(self.at, 4)
@@ -97,26 +98,35 @@
         source, place = self.chunks[chunk]
         return pltpu.make_async_copy(source, place(self.at), self.local_sems.at[chunk])
 
-    def sends(self, phase):
+    def sends(self, chunk, phase):
         at, z = self.at, self.z
         across, core = jnp.bitwise_xor(at, 2), jnp.bitwise_xor(at, 1)
         up, down = (at + 4, z < 3), (at - 4, z > 0)
         other = jnp.bitwise_xor
+        early = chunk in self.across_first
         if phase == 0:
             yield None, at, [(*up, 0), (*down, 1), (across, None, 2), (core, None, 3)]
         if 1 <= phase <= 3:
             n = 4 + 6 * (phase - 1)
-            yield z >= phase, at - 4 * phase, [(*up, n), (across, None, n + 1), (core, None, n + 2)]
-            yield z + phase <= 3, at + 4 * phase, [(*down, n + 3), (across, None, n + 4), (core, None, n + 5)]
+            below, above = [(*up, n), (core, None, n + 2)], [(*down, n + 3), (core, None, n + 5)]
+            if not early:
+                below.append((across, None, n + 1))
+                above.append((across, None, n + 4))
+            yield z >= phase, at - 4 * phase, below
+            yield z + phase <= 3, at + 4 * phase, above
         if phase == 1:
-            yield None, across, [(core, None, 22)]
+            yield None, across, [(*up, 22), (*down, 23), (core, None, 24)] if early else [(core, None, 24)]
         if 2 <= phase <= 4:
-            d, n = phase - 1, 23 + 2 * (phase - 2)
-            yield z >= d, other(at - 4 * d, 2), [(core, None, n)]
-            yield z + d <= 3, other(at + 4 * d, 2), [(core, None, n + 1)]
-
-    def each(self, phase, act):
-        for when, shard, sends in self.sends(phase):
+            d, n = phase - 1, 25 + 4 * (phase - 2)
+            below, above = [(core, None, n + 1)], [(core, None, n + 3)]
+            if early:
+                below.append((*up, n))
+                above.append((*down, n + 2))
+            yield z >= d, other(at - 4 * d, 2), below
+            yield z + d <= 3, other(at + 4 * d, 2), above
+
+    def each(self, chunk, phase, act):
+        for when, shard, sends in self.sends(chunk, phase):
 
             def run():
                 act(shard, None, None)
@@ -141,7 +151,7 @@
             else:
                 self.copy(chunk, shard, target, number, own=phase == 0).start()
 
-        self.each(phase, act)
+        self.each(chunk, phase, act)
 
     def finish(self):
         for chunk in range(len(self.chunks)):
@@ -155,7 +165,7 @@
                     if target is not None:
                         self.copy(chunk, shard, target, number, own=phase == 0).wait_send()
 
-                self.each(phase, act)
+                self.each(chunk, phase, act)
 
 
 class SlabSum:
@@ -495,7 +505,7 @@
         return wd_ref.at[part, :], lambda shard: wd_all.at[shard, part, :]
 
     chunks = [columns(0), columns(1), rows(0), rows(1)]
-    weights = LineGather(chunks, send_sems, recv_sems, local_sems)
+    weights = LineGather(chunks, send_sems, recv_sems, local_sems, EARLY)
     swap = pltpu.make_async_remote_copy(
         src_ref=grad_ref.at[0, 1 - side],
         dst_ref=away_ref,
@@ -506,7 +516,7 @@
     )
     slots = 2 * SLOT_STEPS
     plan = [[] for _ in range(slots + 1)]
-    items = [(chunk, phase) for phase in range(1, 5) for chunk in range(4)]
+    items = SLOT_ORDER
     for n, item in enumerate(items):
         plan[min(1 + n * SLOT_RATE // 16, slots)].append(item)
 
@@ -538,8 +548,10 @@
         swap.wait()
 
 
+EARLY = (0,)
 SLOT_STEPS = 6
-SLOT_RATE = 12
+SLOT_RATE = 14
+SLOT_ORDER = [(chunk, phase) for phase in range(1, 5) for chunk in range(4)]
 
 
 def attend_kernel(qkv_ref, cq_ref, nq_ref, mk_ref, dk_ref, out_ref, log_ref,
@@ -732,11 +744,12 @@
             dqs.append(mm(kt[kv_copy, head * HD : (head + 1) * HD, krows], raw))
             probs.append(p.astype(bf16))
             raws.append(raw)
-        p2 = jnp.concatenate(probs, axis=1)
-        r2 = jnp.concatenate(raws, axis=1)
-        do2 = jnp.concatenate([doz[copy, 0, rows, :], doz[copy, 1, rows, :]], axis=0)
-        q2 = jnp.concatenate([qz[copy, 0, rows, :], qz[copy, 1, rows, :]], axis=0)
-        return jnp.concatenate(dqs, axis=0), mm(r2, q2), mm(p2, do2)
+        grads = [doz[copy, head, rows, :] for head in range(2)]
+        queries = [qz[copy, head, rows, :] for head in range(2)]
+        return jnp.concatenate(dqs, axis=0), (raws, queries), (probs, grads)
+
+    def product(pair):
+        return mm(jnp.concatenate(pair[0], axis=1), jnp.concatenate(pair[1], axis=0))
 
     def finish(field, rotate, scale):
         if rotate:
@@ -748,24 +761,24 @@
         rows = slice(tile * TILE, (tile + 1) * TILE)
         dq_t, dk_t, dv_t = piece(1, tile, 2, kd, 1, rows)
         dq[1, :, rows] = dq_t
-        dkc[rows, :] = dk_t
-        dqkv_ref[2, noisy, rows, :] = dv_t.astype(bf16)
+        dkc[rows, :] = product(dk_t)
+        dqkv_ref[2, noisy, rows, :] = product(dv_t).astype(bf16)
     dqkv_ref[1, noisy] = finish(dkc[...], True, 1.0)
     for tile in reversed(range(tiles)):
         rows = slice(tile * TILE, (tile + 1) * TILE)
         seen = slice(0, (tile + 1) * TILE)
-        for copy in range(2):
-            dq_t, dk_t, dv_t = piece(copy, tile, copy, ka, 0, seen)
-            if copy == 0:
-                dq[0, :, rows] = dq_t
-            else:
-                dq[1, :, rows] += dq_t
-            if copy == 0 and tile == tiles - 1:
-                dkc[...] = dk_t
-                dvc[...] = dv_t
-            else:
-                dkc[seen, :] += dk_t
-                dvc[seen, :] += dv_t
+        dq_t, dk_c, dv_c = piece(0, tile, 0, ka, 0, seen)
+        dq[0, :, rows] = dq_t
+        dq_t, dk_n, dv_n = piece(1, tile, 1, ka, 0, seen)
+        dq[1, :, rows] += dq_t
+        dk_t = product((dk_c[0] + dk_n[0], dk_c[1] + dk_n[1]))
+        dv_t = product((dv_c[0] + dv_n[0], dv_c[1] + dv_n[1]))
+        if tile == tiles - 1:
+            dkc[...] = dk_t
+            dvc[...] = dv_t
+        else:
+            dkc[seen, :] += dk_t
+            dvc[seen, :] += dv_t
     dqkv_ref[2, clean] = dvc[...].astype(bf16)
     dqkv_ref[1, clean] = finish(dkc[...], True, 1.0)
     dqkv_ref[0, clean] = finish(dq[0].T, True, 0.125)

time: 397 us -> 390 us (0.982)
  Pallas kernels: 364 us -> 358 us
    pallas_call x1, Pallas kernels: 93.5 us -> 86.2 us  [attend_back(): pl.pallas_call(body, name='attend_back', grid_spec=pltpu.PrefetchScalarGr...]
where the time goes in v7:
time: 390 us; the launch traced here: 383 us
  Pallas kernels  358 us (92%)
  local copies, waits for them, and re-layouts  14.2 us (4%)
  other arithmetic  8.18 us (2%)
    pallas_call x1, Pallas kernels, attend_back(): pl.pallas_call(body, name='attend_back', grid_spec=pltpu.PrefetchScalarGr...  86.2 us
    pallas_call x1, Pallas kernels, feed(): pl.pallas_call(functools.partial(feed_kernel, half=half), name='feed', gr...  64.3 us
    pallas_call x1, Pallas kernels, last(): pl.pallas_call(functools.partial(last_kernel, share=share), name='last',...  59.7 us
    pallas_call x1, Pallas kernels, attend(): pl.pallas_call(body, name='attend', grid=(pairs,), in_specs=[pl.BlockSpec...  55 us
    pallas_call x1, Pallas kernels, first(): pl.pallas_call(functools.partial(first_kernel, half=half), name='first',...  53.9 us
    pallas_call x2, Pallas kernels, weight_grad_columns(): pl.pallas_call(functools.partial(weight_kernel, share=share, split=False,...  23 us
    pallas_call x1, Pallas kernels, weight_grad_rows(): pl.pallas_call(functools.partial(weight_kernel, share=share, split=True,...  15.7 us
    unnamed x17, local copies, waits for them, and re-layouts  8.74 us
  transfers between devices with their start and end apart: 1, of which 0 were waited for; matrix products, arithmetic and copies ran while one was open for 0% of the time, Pallas kernels for 10%

profile of v7, /device:TPU:0, one launch (start us, length us, event | category | flops | bytes accessed | tf_op | source)
XLA Modules:
  0.0 383.3 jit_solution(16813734998964955485)
XLA Ops:
  0.7 1.2 dynamic-slice.2
  2.6 1.1 select_convert_fusion
  3.7 1.1 compare_convert_fusion
  4.9 0.7 maximum_convert_fusion
  5.5 1.9 fusion
  7.9 1.9 pad_maximum_fusion
  9.7 53.9 %first.1 = (bf16[3,2048,768]{2,1,0:T(8,128)(2,1)}, bf16[2048,768]{1,0:T(8,128)(2,1)}, bf16[1024,768]{1,0:T(8,128)(2,1)}, bf16[16,48,2304]{2,1,0:T(8,128)(2,1)}, ...) custom-call(bf16[48,2304]{1,0:T(8,128)(2,1)} %shard_ref.1, bf16[48,768]{1,0:T(8,128)(2,1)} %wo_ref.1, ...), custom_call_target="tpu_custom_call" | custom-call | flops 7247757312 | bytes 25952256 | tf_op jit(solution)/shard_map/first/pallas_call | solution.py:426
  63.6 1.4 fusion.4
  65.0 55.0 %attend.1 = (bf16[2,1024,768]{2,1,0:T(8,128)(2,1)}, f32[2,6,2,1024]{3,2,1,0:T(2,128)}, bf16[16,48,2048]{2,1,0:T(8,128)(2,1)}, bf16[16,192,768]{2,1,0:T(8,128)(2,1)}, bf16[1024,768]{1,0:T(8,128)(2,1)}) custom-call(bf16[3,2,1024,768]{3,2,1,0:T(8,128)(2,1)} %bitcast.17, bf16[1024,128]{1,0:T(8,128)(2,1)} %get-tuple-element.99.cq_ref.refs_4_, ...), custom_call_target="tpu_custom_call" | custom-call | flops 6442450944 | bytes 12582912 | tf_op jit(solution)/shard_map/attend/pallas_call | solution.py:625
  120.0 64.3 %feed.1 = (bf16[1,2,1024,768]{3,2,1,0:T(8,128)(2,1)}, bf16[1024,768]{1,0:T(8,128)(2,1)}, bf16[2048,3072]{1,0:T(8,128)(2,1)}, bf16[2048,3072]{1,0:T(8,128)(2,1)},...) custom-call(s32[1]{0:T(128)} %bitcast.side_ref, ...), custom_call_target="tpu_custom_call" | custom-call | flops 43486543872 | bytes 53477376 | tf_op jit(solution)/shard_map/feed/pallas_call | solution.py:950
  184.3 1.6 collective-permute-start
  185.9 0.7 pad_add_fusion.me_ref
  186.5 7.2 %grad_out.1 = (bf16[16,48,384]{2,1,0:T(8,128)(2,1)}, bf16[16,48,384]{2,1,0:T(8,128)(2,1)}) custom-call(s32[2]{0:T(128)} %pad_add_fusion.me_ref, bf16[2048,768]{1,0:T(8,128)(2,1)} %bitcast.22, bf16[2048,768]{1,0:T(8,128)(2,1)} %get-tuple-element.66.refs_0_), custom_call_target="tpu_custom_call" | custom-call | flops 2415919104 | bytes 7471104 | tf_op jit(solution)/shard_map/grad_out/pallas_call | solution.py:1027
  193.7 15.7 %grad_down.1 = (bf16[2,4,2,96,768]{4,3,2,1,0:T(8,128)(2,1)}, bf16[2,4,2,96,768]{4,3,2,1,0:T(8,128)(2,1)}) custom-call(s32[2]{0:T(128)} %pad_add_fusion.me_ref, bf16[2048,3072]{1,0:T(8,128)(2,1)} %get-tuple-element.59.left_ref, bf16[1,2,1024,768]{3,2,1,0:T(8,128)(2,1)} %refs_0_.1, bf16[1024,768]{1,0:T(8,128)(2,1)} %get-tuple-element.47.g_away.refs_1_), custom_call_target="tpu_custom_call" | custom-call | flops 9663676416 | bytes 20447232 | tf_op jit(solution)/shard_map/grad_down/pallas_call | solution.py:1061
  209.4 15.8 %grad_up.1 = (bf16[16,48,1536]{2,1,0:T(8,128)(2,1)}, bf16[16,48,1536]{2,1,0:T(8,128)(2,1)}) custom-call(s32[2]{0:T(128)} %pad_add_fusion.me_ref, bf16[2048,768]{1,0:T(8,128)(2,1)} %get-tuple-element.62.left_ref, bf16[2048,3072]{1,0:T(8,128)(2,1)} %get-tuple-element.63.refs_0_), custom_call_target="tpu_custom_call" | custom-call | flops 9663676416 | bytes 20447232 | tf_op jit(solution)/shard_map/grad_up/pallas_call | solution.py:1027
  225.3 1.2 bitcast_dynamic-update-slice_fusion
  226.5 86.2 %attend_back.1 = (bf16[3,2,1024,768]{3,2,1,0:T(8,128)(2,1)}, f32[96,768]{1,0:T(8,128)}, f32[24,3072]{1,0:T(8,128)}, f32[24,768]{1,0:T(8,128)}, f32[8,768]{1,0:T(8,128)}) custom-call(bf16[3,2,1024,768]{3,2,1,0:T(8,128)(2,1)} %bitcast.18, bf16[2,1024,768]{2,1,0:T(8,128)(2,1)} %get-tuple-element.46.refs_1_, bf16[2,1024,768]{2,1,0:T(8,128)(2,1)} %bitcast.23, ...), custom_call_target="tpu_custom_call" | custom-call | flops 16106127360 | bytes 23592960 | tf_op jit(solution)/shard_map/attend_back/pallas_call | solution.py:817
  312.7 59.7 %last.1 = (f32[1,2,1024,768]{3,2,1,0:T(8,128)}, f32[24,2304]{1,0:T(8,128)}, f32[8,768]{1,0:T(8,128)}) custom-call(bf16[1,2,1024,768]{3,2,1,0:T(8,128)(2,1)} %x_own.3, bf16[1024,768]{1,0:T(8,128)(2,1)} %get-tuple-element.44.x_away, f32[1,768]{1,0:T(1,128)} %get-tuple-element.91.gain_ref, bf16[768,2304]{1,0:T(8,128)(2,1)} %bitcast.20, ...), custom_call_target="tpu_custom_call" | custom-call | flops 14495514624 | bytes 28311552 | tf_op jit(solution)/shard_map/last/pallas_call | solution.py:1258
  372.4 0.8 reduce_sum.18
  374.4 6.0 %copy.25 = f32[1,2,1024,768]{3,2,1,0:T(8,128)} copy(f32[1,2,1024,768]{3,2,1,0:T(8,128)} %get-tuple-element.113) | data formatting | bytes 12582912
  380.4 0.7 copy.26
  381.1 0.6 copy.27
  381.7 0.7 copy.28
  382.4 0.7 copy.29
  (23 shorter events, 1.6 us)
Async XLA Ops:
  7.8 1.9 copy-start.5
  184.3 41.0 %collective-permute-start = (bf16[1024,768]{1,0:T(8,128)(2,1)}, bf16[1024,768]{1,0:T(8,128)(2,1)S(1)}, u32[]{:S(2)}, u32[]{:S(2)}) collective-permute-start(bf16[1024,768]{1,0:T(8,128)(2,1)} %get-tuple-element.54), channel_id=1, source_target_pairs={{0,16},{16,0},{1,17},{17,1},{2,18},{18,2},{3,19},{19,3},{4,20},{20... | collective-permute-start | bytes 4718600 | tf_op jit(solution)/shard_map/ppermute | solution.py:1352
  312.7 60.5 %copy-start.4 = (f32[8,768]{1,0:T(8,128)S(1)}, f32[8,768]{1,0:T(8,128)}, u32[]{:S(2)}) copy-start(f32[8,768]{1,0:T(8,128)} %get-tuple-element.77) | copy-start | bytes 73732
  374.4 6.0 %copy-start.2 = (f32[24,2304]{1,0:T(8,128)S(1)}, f32[24,2304]{1,0:T(8,128)}, u32[]{:S(2)}) copy-start(f32[24,2304]{1,0:T(8,128)} %get-tuple-element.115) | copy-start | bytes 663556
  374.4 6.7 %copy-start.3 = (f32[24,768]{1,0:T(8,128)S(1)}, f32[24,768]{1,0:T(8,128)}, u32[]{:S(2)}) copy-start(f32[24,768]{1,0:T(8,128)} %get-tuple-element.116) | copy-start | bytes 221188
  374.4 7.3 %copy-start.1 = (f32[24,3072]{1,0:T(8,128)S(1)}, f32[24,3072]{1,0:T(8,128)}, u32[]{:S(2)}) copy-start(f32[24,3072]{1,0:T(8,128)} %get-tuple-element.118) | copy-start | bytes 884740
  374.4 8.0 %copy-start = (f32[96,768]{1,0:T(8,128)S(1)}, f32[96,768]{1,0:T(8,128)}, u32[]{:S(2)}) copy-start(f32[96,768]{1,0:T(8,128)} %get-tuple-element.119) | copy-start | bytes 884740

commit v8 on v7

--- a/solution.py
+++ b/solution.py
@@ -358,7 +358,7 @@
         cols = slice(n * width, (n + 1) * width)
         return shard_ref.at[:, cols], lambda shard: w_all.at[shard, :, cols]
 
-    weights = LineGather([chunk(n) for n in range(3)], *refs[:3])
+    weights = LineGather([chunk(n) for n in range(3)], *refs[:3], across_first=(0,))
     part = wu_ref.at[:, : wu_all.shape[2]]
     others = LineGather([(wo_ref, lambda shard: wo_all.at[shard]), (part, lambda shard: wu_all.at[shard])], *refs[3:6])
     gain = GainSum((0, 1, 2, 3), *refs[6:])
@@ -902,8 +902,9 @@
         sq = u * u
         t = jnp.tanh(u * (ROOT + (ROOT * 0.044715) * sq))
         part = 0.5 + 0.5 * t
-        act = (u * part).astype(bf16)
-        slope = part + (u * (part * (1.0 - t))) * (ROOT + (3 * ROOT * 0.044715) * sq)
+        wide = u * part
+        act = wide.astype(bf16)
+        slope = part + (wide * (1.0 - t)) * (ROOT + (3 * ROOT * 0.044715) * sq)
         du = (da * slope).astype(bf16)
         act_ref[:, cols] = act
         du_ref[:, cols] = du

time: 390 us -> 393 us (level)
  no operation moved by 1% of the time
where the time goes in v8:
time: 393 us; the launch traced here: 386 us
  Pallas kernels  360 us (92%)
  local copies, waits for them, and re-layouts  14.2 us (4%)
  other arithmetic  8.18 us (2%)
    pallas_call x1, Pallas kernels, attend_back(): pl.pallas_call(body, name='attend_back', grid_spec=pltpu.PrefetchScalarGr...  86.8 us
    pallas_call x1, Pallas kernels, feed(): pl.pallas_call(functools.partial(feed_kernel, half=half), name='feed', gr...  65.5 us
    pallas_call x1, Pallas kernels, last(): pl.pallas_call(functools.partial(last_kernel, share=share), name='last',...  59.9 us
    pallas_call x1, Pallas kernels, first(): pl.pallas_call(functools.partial(first_kernel, half=half), name='first',...  55.4 us
    pallas_call x1, Pallas kernels, attend(): pl.pallas_call(body, name='attend', grid=(pairs,), in_specs=[pl.BlockSpec...  53.8 us
    pallas_call x2, Pallas kernels, weight_grad_columns(): pl.pallas_call(functools.partial(weight_kernel, share=share, split=False,...  23 us
    pallas_call x1, Pallas kernels, weight_grad_rows(): pl.pallas_call(functools.partial(weight_kernel, share=share, split=True,...  15.7 us
    unnamed x17, local copies, waits for them, and re-layouts  8.74 us
  transfers between devices with their start and end apart: 1, of which 0 were waited for; matrix products, arithmetic and copies ran while one was open for 0% of the time, Pallas kernels for 10%

profile of v8, /device:TPU:0, one launch (start us, length us, event | category | flops | bytes accessed | tf_op | source)
XLA Modules:
  0.0 385.8 jit_solution(17555352407594105107)
XLA Ops:
  0.7 1.2 dynamic-slice.2
  2.6 1.1 select_convert_fusion
  3.7 1.1 compare_convert_fusion
  4.9 0.7 maximum_convert_fusion
  5.5 1.9 fusion
  7.9 1.9 pad_maximum_fusion
  9.7 55.4 %first.1 = (bf16[3,2048,768]{2,1,0:T(8,128)(2,1)}, bf16[2048,768]{1,0:T(8,128)(2,1)}, bf16[1024,768]{1,0:T(8,128)(2,1)}, bf16[16,48,2304]{2,1,0:T(8,128)(2,1)}, ...) custom-call(bf16[48,2304]{1,0:T(8,128)(2,1)} %shard_ref.1, bf16[48,768]{1,0:T(8,128)(2,1)} %wo_ref.1, ...), custom_call_target="tpu_custom_call" | custom-call | flops 7247757312 | bytes 25952256 | tf_op jit(solution)/shard_map/first/pallas_call | solution.py:426
  65.1 1.4 fusion.4
  66.5 53.8 %attend.1 = (bf16[2,1024,768]{2,1,0:T(8,128)(2,1)}, f32[2,6,2,1024]{3,2,1,0:T(2,128)}, bf16[16,48,2048]{2,1,0:T(8,128)(2,1)}, bf16[16,192,768]{2,1,0:T(8,128)(2,1)}, bf16[1024,768]{1,0:T(8,128)(2,1)}) custom-call(bf16[3,2,1024,768]{3,2,1,0:T(8,128)(2,1)} %bitcast.17, bf16[1024,128]{1,0:T(8,128)(2,1)} %get-tuple-element.99.cq_ref.refs_4_, ...), custom_call_target="tpu_custom_call" | custom-call | flops 6442450944 | bytes 12582912 | tf_op jit(solution)/shard_map/attend/pallas_call | solution.py:625
  120.4 65.5 %feed.1 = (bf16[1,2,1024,768]{3,2,1,0:T(8,128)(2,1)}, bf16[1024,768]{1,0:T(8,128)(2,1)}, bf16[2048,3072]{1,0:T(8,128)(2,1)}, bf16[2048,3072]{1,0:T(8,128)(2,1)},...) custom-call(s32[1]{0:T(128)} %bitcast.side_ref, ...), custom_call_target="tpu_custom_call" | custom-call | flops 43486543872 | bytes 53477376 | tf_op jit(solution)/shard_map/feed/pallas_call | solution.py:951
  185.9 1.6 collective-permute-start
  187.5 0.7 pad_add_fusion.me_ref
  188.1 7.2 %grad_out.1 = (bf16[16,48,384]{2,1,0:T(8,128)(2,1)}, bf16[16,48,384]{2,1,0:T(8,128)(2,1)}) custom-call(s32[2]{0:T(128)} %pad_add_fusion.me_ref, bf16[2048,768]{1,0:T(8,128)(2,1)} %bitcast.22, bf16[2048,768]{1,0:T(8,128)(2,1)} %get-tuple-element.66.refs_0_), custom_call_target="tpu_custom_call" | custom-call | flops 2415919104 | bytes 7471104 | tf_op jit(solution)/shard_map/grad_out/pallas_call | solution.py:1028
  195.3 15.7 %grad_down.1 = (bf16[2,4,2,96,768]{4,3,2,1,0:T(8,128)(2,1)}, bf16[2,4,2,96,768]{4,3,2,1,0:T(8,128)(2,1)}) custom-call(s32[2]{0:T(128)} %pad_add_fusion.me_ref, bf16[2048,3072]{1,0:T(8,128)(2,1)} %get-tuple-element.59.left_ref, bf16[1,2,1024,768]{3,2,1,0:T(8,128)(2,1)} %refs_0_.1, bf16[1024,768]{1,0:T(8,128)(2,1)} %get-tuple-element.47.g_away.refs_1_), custom_call_target="tpu_custom_call" | custom-call | flops 9663676416 | bytes 20447232 | tf_op jit(solution)/shard_map/grad_down/pallas_call | solution.py:1062
  211.0 15.8 %grad_up.1 = (bf16[16,48,1536]{2,1,0:T(8,128)(2,1)}, bf16[16,48,1536]{2,1,0:T(8,128)(2,1)}) custom-call(s32[2]{0:T(128)} %pad_add_fusion.me_ref, bf16[2048,768]{1,0:T(8,128)(2,1)} %get-tuple-element.62.left_ref, bf16[2048,3072]{1,0:T(8,128)(2,1)} %get-tuple-element.63.refs_0_), custom_call_target="tpu_custom_call" | custom-call | flops 9663676416 | bytes 20447232 | tf_op jit(solution)/shard_map/grad_up/pallas_call | solution.py:1028
  226.9 1.2 bitcast_dynamic-update-slice_fusion
  228.1 86.8 %attend_back.1 = (bf16[3,2,1024,768]{3,2,1,0:T(8,128)(2,1)}, f32[96,768]{1,0:T(8,128)}, f32[24,3072]{1,0:T(8,128)}, f32[24,768]{1,0:T(8,128)}, f32[8,768]{1,0:T(8,128)}) custom-call(bf16[3,2,1024,768]{3,2,1,0:T(8,128)(2,1)} %bitcast.18, bf16[2,1024,768]{2,1,0:T(8,128)(2,1)} %get-tuple-element.46.refs_1_, bf16[2,1024,768]{2,1,0:T(8,128)(2,1)} %bitcast.23, ...), custom_call_target="tpu_custom_call" | custom-call | flops 16106127360 | bytes 23592960 | tf_op jit(solution)/shard_map/attend_back/pallas_call | solution.py:817
  314.9 59.9 %last.1 = (f32[1,2,1024,768]{3,2,1,0:T(8,128)}, f32[24,2304]{1,0:T(8,128)}, f32[8,768]{1,0:T(8,128)}) custom-call(bf16[1,2,1024,768]{3,2,1,0:T(8,128)(2,1)} %x_own.3, bf16[1024,768]{1,0:T(8,128)(2,1)} %get-tuple-element.44.x_away, f32[1,768]{1,0:T(1,128)} %get-tuple-element.91.gain_ref, bf16[768,2304]{1,0:T(8,128)(2,1)} %bitcast.20, ...), custom_call_target="tpu_custom_call" | custom-call | flops 14495514624 | bytes 28311552 | tf_op jit(solution)/shard_map/last/pallas_call | solution.py:1259
  374.9 0.8 reduce_sum.18
  376.8 6.0 %copy.25 = f32[1,2,1024,768]{3,2,1,0:T(8,128)} copy(f32[1,2,1024,768]{3,2,1,0:T(8,128)} %get-tuple-element.113) | data formatting | bytes 12582912
  382.8 0.7 copy.26
  383.5 0.6 copy.27
  384.1 0.7 copy.28
  384.8 0.7 copy.29
  (23 shorter events, 1.6 us)
Async XLA Ops:
  7.8 1.9 copy-start.5
  185.9 41.0 %collective-permute-start = (bf16[1024,768]{1,0:T(8,128)(2,1)}, bf16[1024,768]{1,0:T(8,128)(2,1)S(1)}, u32[]{:S(2)}, u32[]{:S(2)}) collective-permute-start(bf16[1024,768]{1,0:T(8,128)(2,1)} %get-tuple-element.54), channel_id=1, source_target_pairs={{0,16},{16,0},{1,17},{17,1},{2,18},{18,2},{3,19},{19,3},{4,20},{20... | collective-permute-start | bytes 4718600 | tf_op jit(solution)/shard_map/ppermute | solution.py:1353
  314.9 60.7 %copy-start.4 = (f32[8,768]{1,0:T(8,128)S(1)}, f32[8,768]{1,0:T(8,128)}, u32[]{:S(2)}) copy-start(f32[8,768]{1,0:T(8,128)} %get-tuple-element.77) | copy-start | bytes 73732
  376.8 6.0 %copy-start.2 = (f32[24,2304]{1,0:T(8,128)S(1)}, f32[24,2304]{1,0:T(8,128)}, u32[]{:S(2)}) copy-start(f32[24,2304]{1,0:T(8,128)} %get-tuple-element.115) | copy-start | bytes 663556
  376.8 6.7 %copy-start.3 = (f32[24,768]{1,0:T(8,128)S(1)}, f32[24,768]{1,0:T(8,128)}, u32[]{:S(2)}) copy-start(f32[24,768]{1,0:T(8,128)} %get-tuple-element.116) | copy-start | bytes 221188
  376.8 7.3 %copy-start.1 = (f32[24,3072]{1,0:T(8,128)S(1)}, f32[24,3072]{1,0:T(8,128)}, u32[]{:S(2)}) copy-start(f32[24,3072]{1,0:T(8,128)} %get-tuple-element.118) | copy-start | bytes 884740
  376.8 8.0 %copy-start = (f32[96,768]{1,0:T(8,128)S(1)}, f32[96,768]{1,0:T(8,128)}, u32[]{:S(2)}) copy-start(f32[96,768]{1,0:T(8,128)} %get-tuple-element.119) | copy-start | bytes 884740

commit v9 on v7

--- a/solution.py
+++ b/solution.py
@@ -1368,7 +1368,7 @@
     index = side * peers + at
     me = jnp.stack([index if small else 0 * index, side]).astype(jnp.int32)
     share = width // (2 * peers)
-    cut = ff // 3 // LANES * LANES
+    cut = ff // 4 // LANES * LANES
 
     cosine, sine = rotary_tables(length)
     tables = mask_tables(length, jnp.take(lengths, side))

time: 390 us -> 391 us (level)
  no operation moved by 1% of the time
where the time goes in v9:
time: 391 us; the launch traced here: 384 us
  Pallas kernels  359 us (92%)
  local copies, waits for them, and re-layouts  14.2 us (4%)
  other arithmetic  8.1 us (2%)
    pallas_call x1, Pallas kernels, attend_back(): pl.pallas_call(body, name='attend_back', grid_spec=pltpu.PrefetchScalarGr...  86.5 us
    pallas_call x1, Pallas kernels, feed(): pl.pallas_call(functools.partial(feed_kernel, half=half), name='feed', gr...  64.2 us
    pallas_call x1, Pallas kernels, last(): pl.pallas_call(functools.partial(last_kernel, share=share), name='last',...  59.6 us
    pallas_call x1, Pallas kernels, attend(): pl.pallas_call(body, name='attend', grid=(pairs,), in_specs=[pl.BlockSpec...  56.6 us
    pallas_call x1, Pallas kernels, first(): pl.pallas_call(functools.partial(first_kernel, half=half), name='first',...  53.3 us
    pallas_call x2, Pallas kernels, weight_grad_columns(): pl.pallas_call(functools.partial(weight_kernel, share=share, split=False,...  22.9 us
    pallas_call x1, Pallas kernels, weight_grad_rows(): pl.pallas_call(functools.partial(weight_kernel, share=share, split=True,...  15.7 us
    unnamed x17, local copies, waits for them, and re-layouts  8.74 us
  transfers between devices with their start and end apart: 1, of which 0 were waited for; matrix products, arithmetic and copies ran while one was open for 0% of the time, Pallas kernels for 10%

profile of v9, /device:TPU:0, one launch (start us, length us, event | category | flops | bytes accessed | tf_op | source)
XLA Modules:
  0.0 384.3 jit_solution(9756954185005883259)
XLA Ops:
  0.7 1.2 dynamic-slice.2
  2.6 1.1 select_convert_fusion
  3.7 1.1 compare_convert_fusion
  4.9 0.7 maximum_convert_fusion
  5.5 1.9 fusion
  7.9 1.9 pad_maximum_fusion
  9.7 53.3 %first.1 = (bf16[3,2048,768]{2,1,0:T(8,128)(2,1)}, bf16[2048,768]{1,0:T(8,128)(2,1)}, bf16[1024,768]{1,0:T(8,128)(2,1)}, bf16[16,48,2304]{2,1,0:T(8,128)(2,1)}, ...) custom-call(bf16[48,2304]{1,0:T(8,128)(2,1)} %shard_ref.1, bf16[48,768]{1,0:T(8,128)(2,1)} %wo_ref.1, ...), custom_call_target="tpu_custom_call" | custom-call | flops 7247757312 | bytes 25952256 | tf_op jit(solution)/shard_map/first/pallas_call | solution.py:426
  63.0 1.4 fusion.4
  64.5 56.6 %attend.1 = (bf16[2,1024,768]{2,1,0:T(8,128)(2,1)}, f32[2,6,2,1024]{3,2,1,0:T(2,128)}, bf16[16,48,2304]{2,1,0:T(8,128)(2,1)}, bf16[16,192,768]{2,1,0:T(8,128)(2,1)}, bf16[1024,768]{1,0:T(8,128)(2,1)}) custom-call(bf16[3,2,1024,768]{3,2,1,0:T(8,128)(2,1)} %bitcast.17, bf16[1024,128]{1,0:T(8,128)(2,1)} %get-tuple-element.99.cq_ref.refs_4_, ...), custom_call_target="tpu_custom_call" | custom-call | flops 6442450944 | bytes 12582912 | tf_op jit(solution)/shard_map/attend/pallas_call | solution.py:625
  121.1 64.2 %feed.1 = (bf16[1,2,1024,768]{3,2,1,0:T(8,128)(2,1)}, bf16[1024,768]{1,0:T(8,128)(2,1)}, bf16[2048,3072]{1,0:T(8,128)(2,1)}, bf16[2048,3072]{1,0:T(8,128)(2,1)},...) custom-call(s32[1]{0:T(128)} %bitcast.side_ref, ...), custom_call_target="tpu_custom_call" | custom-call | flops 43486543872 | bytes 53477376 | tf_op jit(solution)/shard_map/feed/pallas_call | solution.py:950
  185.3 1.6 collective-permute-start
  187.5 7.2 %grad_out.1 = (bf16[16,48,384]{2,1,0:T(8,128)(2,1)}, bf16[16,48,384]{2,1,0:T(8,128)(2,1)}) custom-call(s32[2]{0:T(128)} %pad_add_fusion.me_ref, bf16[2048,768]{1,0:T(8,128)(2,1)} %bitcast.22, bf16[2048,768]{1,0:T(8,128)(2,1)} %get-tuple-element.66.refs_0_), custom_call_target="tpu_custom_call" | custom-call | flops 2415919104 | bytes 7471104 | tf_op jit(solution)/shard_map/grad_out/pallas_call | solution.py:1027
  194.7 15.7 %grad_down.1 = (bf16[2,4,2,96,768]{4,3,2,1,0:T(8,128)(2,1)}, bf16[2,4,2,96,768]{4,3,2,1,0:T(8,128)(2,1)}) custom-call(s32[2]{0:T(128)} %pad_add_fusion.me_ref, bf16[2048,3072]{1,0:T(8,128)(2,1)} %get-tuple-element.59.left_ref, bf16[1,2,1024,768]{3,2,1,0:T(8,128)(2,1)} %refs_0_.1, bf16[1024,768]{1,0:T(8,128)(2,1)} %get-tuple-element.47.g_away.refs_1_), custom_call_target="tpu_custom_call" | custom-call | flops 9663676416 | bytes 20447232 | tf_op jit(solution)/shard_map/grad_down/pallas_call | solution.py:1061
  210.4 15.7 %grad_up.1 = (bf16[16,48,1536]{2,1,0:T(8,128)(2,1)}, bf16[16,48,1536]{2,1,0:T(8,128)(2,1)}) custom-call(s32[2]{0:T(128)} %pad_add_fusion.me_ref, bf16[2048,768]{1,0:T(8,128)(2,1)} %get-tuple-element.62.left_ref, bf16[2048,3072]{1,0:T(8,128)(2,1)} %get-tuple-element.63.refs_0_), custom_call_target="tpu_custom_call" | custom-call | flops 9663676416 | bytes 20447232 | tf_op jit(solution)/shard_map/grad_up/pallas_call | solution.py:1027
  226.1 1.2 bitcast_dynamic-update-slice_fusion
  227.3 86.5 %attend_back.1 = (bf16[3,2,1024,768]{3,2,1,0:T(8,128)(2,1)}, f32[96,768]{1,0:T(8,128)}, f32[24,3072]{1,0:T(8,128)}, f32[24,768]{1,0:T(8,128)}, f32[8,768]{1,0:T(8,128)}) custom-call(bf16[3,2,1024,768]{3,2,1,0:T(8,128)(2,1)} %bitcast.18, bf16[2,1024,768]{2,1,0:T(8,128)(2,1)} %get-tuple-element.46.refs_1_, bf16[2,1024,768]{2,1,0:T(8,128)(2,1)} %bitcast.23, ...), custom_call_target="tpu_custom_call" | custom-call | flops 16106127360 | bytes 23592960 | tf_op jit(solution)/shard_map/attend_back/pallas_call | solution.py:817
  313.8 59.6 %last.1 = (f32[1,2,1024,768]{3,2,1,0:T(8,128)}, f32[24,2304]{1,0:T(8,128)}, f32[8,768]{1,0:T(8,128)}) custom-call(bf16[1,2,1024,768]{3,2,1,0:T(8,128)(2,1)} %x_own.3, bf16[1024,768]{1,0:T(8,128)(2,1)} %get-tuple-element.44.x_away, f32[1,768]{1,0:T(1,128)} %get-tuple-element.91.gain_ref, bf16[768,2304]{1,0:T(8,128)(2,1)} %bitcast.20, ...), custom_call_target="tpu_custom_call" | custom-call | flops 14495514624 | bytes 28311552 | tf_op jit(solution)/shard_map/last/pallas_call | solution.py:1258
  373.4 0.8 reduce_sum.18
  374.2 0.6 dynamic_slice.6
  375.4 6.0 %copy.25 = f32[1,2,1024,768]{3,2,1,0:T(8,128)} copy(f32[1,2,1024,768]{3,2,1,0:T(8,128)} %get-tuple-element.113) | data formatting | bytes 12582912
  381.3 0.7 copy.26
  382.0 0.6 copy.27
  382.7 0.7 copy.28
  383.4 0.7 copy.29
  (23 shorter events, 1.6 us)
Async XLA Ops:
  7.8 1.9 copy-start.5
  185.3 40.8 %collective-permute-start = (bf16[1024,768]{1,0:T(8,128)(2,1)}, bf16[1024,768]{1,0:T(8,128)(2,1)S(1)}, u32[]{:S(2)}, u32[]{:S(2)}) collective-permute-start(bf16[1024,768]{1,0:T(8,128)(2,1)} %get-tuple-element.54), channel_id=1, source_target_pairs={{0,16},{16,0},{1,17},{17,1},{2,18},{18,2},{3,19},{19,3},{4,20},{20... | collective-permute-start | bytes 4718600 | tf_op jit(solution)/shard_map/ppermute | solution.py:1352
  313.8 60.4 %copy-start.4 = (f32[8,768]{1,0:T(8,128)S(1)}, f32[8,768]{1,0:T(8,128)}, u32[]{:S(2)}) copy-start(f32[8,768]{1,0:T(8,128)} %get-tuple-element.77) | copy-start | bytes 73732
  375.4 6.0 %copy-start.2 = (f32[24,2304]{1,0:T(8,128)S(1)}, f32[24,2304]{1,0:T(8,128)}, u32[]{:S(2)}) copy-start(f32[24,2304]{1,0:T(8,128)} %get-tuple-element.115) | copy-start | bytes 663556
  375.4 6.7 %copy-start.3 = (f32[24,768]{1,0:T(8,128)S(1)}, f32[24,768]{1,0:T(8,128)}, u32[]{:S(2)}) copy-start(f32[24,768]{1,0:T(8,128)} %get-tuple-element.116) | copy-start | bytes 221188
  375.4 7.3 %copy-start.1 = (f32[24,3072]{1,0:T(8,128)S(1)}, f32[24,3072]{1,0:T(8,128)}, u32[]{:S(2)}) copy-start(f32[24,3072]{1,0:T(8,128)} %get-tuple-element.118) | copy-start | bytes 884740
  375.4 8.0 %copy-start = (f32[96,768]{1,0:T(8,128)S(1)}, f32[96,768]{1,0:T(8,128)}, u32[]{:S(2)}) copy-start(f32[96,768]{1,0:T(8,128)} %get-tuple-element.119) | copy-start | bytes 884740
